TPU v7x, 32 devices: a whole 2x2x4 slice. The times are simulated.
32 devices in a mesh: cuts: 8 (over z, core), tile: 4 (over y, x).
Axes of the slice: x: 2, y: 2, z: 4, core: 2. Of those that a mesh axis runs over, the one named last changes fastest.
Arguments:
- object_slices: float32 [8, 2, 768, 512], P('cuts', None, None, 'tile'), may hold values from -1.25 to 1.25, as said below
- probe_modes: float32 [4, 2, 128, 128], replicated, may hold values from -3 to 3
- prop_phase: float32 [128, 128], replicated, may hold values from -3.140625 to 3.140625
- measured: float32 [16, 128, 128], P('tile'), may hold values from 0 to 4
- row_offsets: int32 [16], P('tile'), may hold values from 0 to 640
- col_offsets: int32 [16], P('tile'), may hold values from 0 to 127
- counts: int32 [4], P('tile'), may hold values from 1 to 4, 12 in all
Outputs:
- object_grad: float32 [8, 2, 768, 512], P('cuts', None, None, 'tile')
Inputs may be any that keep to these rules, and one draw needn't show every extreme that they name: `counts`: every group of 4 slots holds at least one window, and some group is full in every draw. `object_slices`: each pixel's transmission has a magnitude between 0.8 and 1.25.
All inputs are finite; a program needn't handle non-finite values.
Results may differ from a plain program's by a relative error of at most 0.03.
Values may be sent and summed in bfloat16 or wider, within the bound.
No kernel may reach another device: no remote copies, remote signals or barrier semaphores. Data moves between devices by JAX's collectives and lax.ppermute only.
A program may use at most 64 MiB of HBM per device.

v0:
```python
import math

import jax
import jax.numpy as jnp
from jax import lax
from jax.sharding import PartitionSpec as P

HIGHEST = lax.Precision.HIGHEST


def passed_along(block, axis, distance):
    devices = range(lax.axis_size(axis))
    route = [(i - distance, i) for i in devices if i - distance in devices]
    return lax.ppermute(block, axis, route)


def dft_tables(win_size):
    numbers = jnp.arange(win_size, dtype=jnp.int32)
    angles = (numbers[:, None] * numbers[None, :] % win_size).astype(jnp.float32) * (
        2.0 * math.pi / win_size
    )
    factor = 1.0 / math.sqrt(win_size)
    return (jnp.cos(angles) * factor, jnp.sin(angles) * factor)


def left_mul(mat_real, mat_imag, real_part, imag_part):
    real_real = jnp.einsum("jk,...kl->...jl", mat_real, real_part, precision=HIGHEST)
    imag_imag = jnp.einsum("jk,...kl->...jl", mat_imag, imag_part, precision=HIGHEST)
    real_imag = jnp.einsum("jk,...kl->...jl", mat_real, imag_part, precision=HIGHEST)
    imag_real = jnp.einsum("jk,...kl->...jl", mat_imag, real_part, precision=HIGHEST)
    return (real_real - imag_imag, real_imag + imag_real)


def right_mul(real_part, imag_part, mat_real, mat_imag):
    real_real = jnp.einsum("...jk,kl->...jl", real_part, mat_real, precision=HIGHEST)
    imag_imag = jnp.einsum("...jk,kl->...jl", imag_part, mat_imag, precision=HIGHEST)
    real_imag = jnp.einsum("...jk,kl->...jl", real_part, mat_imag, precision=HIGHEST)
    imag_real = jnp.einsum("...jk,kl->...jl", imag_part, mat_real, precision=HIGHEST)
    return (real_real - imag_imag, real_imag + imag_real)


def transform(real_part, imag_part, cosine, sine_table, forward):
    signed = -sine_table if forward else sine_table
    real_part, imag_part = left_mul(cosine, signed, real_part, imag_part)
    return right_mul(real_part, imag_part, cosine, signed)


def complex_mul(a_real, a_imag, b_real, b_imag):
    return (a_real * b_real - a_imag * b_imag, a_real * b_imag + a_imag * b_real)


def propagate(real_part, imag_part, phase_cos, phase_sin, cosine, sine_table):
    freq_real, freq_imag = transform(real_part, imag_part, cosine, sine_table, True)
    freq_real, freq_imag = complex_mul(phase_cos, phase_sin, freq_real, freq_imag)
    return transform(freq_real, freq_imag, cosine, sine_table, False)


def section_forward(incoming, patch_now, phase_cos, phase_sin, cosine, sine_table):
    wave_real = incoming[:, 0].astype(jnp.float32)
    wave_imag = incoming[:, 1].astype(jnp.float32)
    prod_real, prod_imag = complex_mul(wave_real, wave_imag, patch_now[0], patch_now[1])
    out_real, out_imag = propagate(prod_real, prod_imag, phase_cos, phase_sin, cosine, sine_table)
    return jnp.stack([out_real, out_imag], axis=1).astype(jnp.bfloat16)


def loss_back(incoming, patch_now, target, weight, cosine, sine_table):
    wave_real = incoming[:, 0].astype(jnp.float32)
    wave_imag = incoming[:, 1].astype(jnp.float32)
    prod_real, prod_imag = complex_mul(wave_real, wave_imag, patch_now[0], patch_now[1])
    det_real, det_imag = transform(prod_real, prod_imag, cosine, sine_table, True)
    intensity = jnp.sum(det_real * det_real + det_imag * det_imag, axis=0)
    factor = weight * (intensity - target) * 0.25
    return transform(factor * det_real, factor * det_imag, cosine, sine_table, False)


def adjoint_back(returned, phase_cos, phase_sin, cosine, sine_table):
    real_part = returned[:, 0].astype(jnp.float32)
    imag_part = returned[:, 1].astype(jnp.float32)
    return propagate(real_part, imag_part, phase_cos, -phase_sin, cosine, sine_table)


def patch_grad(incoming, back_pair):
    wave_real = incoming[:, 0].astype(jnp.float32)
    wave_imag = incoming[:, 1].astype(jnp.float32)
    back_real, back_imag = back_pair
    grad_real = jnp.sum(wave_real * back_real + wave_imag * back_imag, axis=0)
    grad_imag = jnp.sum(wave_real * back_imag - wave_imag * back_real, axis=0)
    return jnp.stack([grad_real, grad_imag], axis=0)


def wave_grad(patch_now, back_pair):
    back_real, back_imag = back_pair
    ret_real = patch_now[0] * back_real + patch_now[1] * back_imag
    ret_imag = patch_now[0] * back_imag - patch_now[1] * back_real
    return jnp.stack([ret_real, ret_imag], axis=1).astype(jnp.bfloat16)


def local(object_slices, probe_modes, prop_phase, measured, row_offsets, col_offsets, counts):
    win_size = probe_modes.shape[-1]
    slot_count = row_offsets.shape[0]
    sections = lax.axis_size("cuts")
    section_id = lax.axis_index("cuts")
    cosine, sine_table = dft_tables(win_size)
    phase_cos = jnp.cos(prop_phase)
    phase_sin = jnp.sin(prop_phase)
    own_strip = object_slices[0]
    strip_rows = own_strip.shape[1]
    anchor = jnp.zeros((), jnp.int32)
    valid_flags = (jnp.arange(slot_count, dtype=jnp.int32) < counts[0]).astype(jnp.float32)
    offset_pairs = jnp.stack([row_offsets, col_offsets], axis=1)
    left_pairs = passed_along(offset_pairs, "tile", 1)
    block_shape = (2, win_size, win_size)
    beside = passed_along(own_strip, "tile", -1)
    widened = jnp.concatenate([own_strip, beside], axis=2)
    patches = jnp.stack(
        [
            lax.dynamic_slice(
                widened, (anchor, row_offsets[member], col_offsets[member]), block_shape
            )
            for member in range(slot_count)
        ]
    )
    probe_wave = probe_modes.astype(jnp.bfloat16)
    wave_shape = probe_modes.shape

    def forward_step(counter, carried):
        received, stored = carried
        slot_id = counter - section_id
        active = (slot_id >= 0) & (slot_id < slot_count)
        position = jnp.clip(slot_id, 0, slot_count - 1)
        incoming = jnp.where(section_id == 0, probe_wave, received)
        stored = lax.cond(
            active,
            lambda: lax.dynamic_update_index_in_dim(stored, incoming, position, 0),
            lambda: stored,
        )
        patch_now = lax.dynamic_index_in_dim(patches, position, 0, keepdims=False)
        outgoing = lax.cond(
            active & (section_id < sections - 1),
            lambda: section_forward(incoming, patch_now, phase_cos, phase_sin, cosine, sine_table),
            lambda: jnp.zeros(wave_shape, jnp.bfloat16),
        )
        received = passed_along(outgoing, "cuts", 1)
        return (received, stored)

    start_wave = jnp.zeros(wave_shape, jnp.bfloat16)
    start_store = jnp.zeros((slot_count,) + wave_shape, jnp.bfloat16)
    _, stored = lax.fori_loop(0, sections + slot_count - 1, forward_step, (start_wave, start_store))

    def backward_step(counter, carried):
        received, grad_store = carried
        slot_id = counter - (sections - 1 - section_id)
        active = (slot_id >= 0) & (slot_id < slot_count)
        position = jnp.clip(slot_id, 0, slot_count - 1)
        incoming = lax.dynamic_index_in_dim(stored, position, 0, keepdims=False)
        patch_now = lax.dynamic_index_in_dim(patches, position, 0, keepdims=False)
        target = lax.dynamic_index_in_dim(measured, position, 0, keepdims=False)
        weight = lax.dynamic_index_in_dim(valid_flags, position, 0, keepdims=False)

        def compute_slot():
            back_pair = lax.cond(
                section_id == sections - 1,
                lambda: loss_back(incoming, patch_now, target, weight, cosine, sine_table),
                lambda: adjoint_back(received, phase_cos, phase_sin, cosine, sine_table),
            )
            return (patch_grad(incoming, back_pair), wave_grad(patch_now, back_pair))

        def skip_slot():
            return (jnp.zeros(block_shape, jnp.float32), jnp.zeros(wave_shape, jnp.bfloat16))

        grad_now, outgoing = lax.cond(active, compute_slot, skip_slot)
        grad_store = lax.cond(
            active,
            lambda: lax.dynamic_update_index_in_dim(grad_store, grad_now, position, 0),
            lambda: grad_store,
        )
        received = passed_along(outgoing, "cuts", -1)
        return (received, grad_store)

    start_grads = jnp.zeros((slot_count,) + block_shape, jnp.float32)
    _, grad_store = lax.fori_loop(
        0, sections + slot_count - 1, backward_step, (start_wave, start_grads)
    )
    own_part = jnp.zeros((2, strip_rows, win_size), jnp.float32)
    right_parts = []
    for member in range(slot_count):
        widened = jnp.zeros((2, win_size, 2 * win_size), jnp.float32)
        widened = lax.dynamic_update_slice(
            widened, grad_store[member], (anchor, anchor, col_offsets[member])
        )
        current = lax.dynamic_slice(own_part, (anchor, row_offsets[member], anchor), block_shape)
        own_part = lax.dynamic_update_slice(
            own_part, current + widened[:, :, :win_size], (anchor, row_offsets[member], anchor)
        )
        right_parts.append(widened[:, :, win_size:])
    arriving = passed_along(jnp.stack(right_parts), "tile", 1)
    for member in range(slot_count):
        current = lax.dynamic_slice(own_part, (anchor, left_pairs[member, 0], anchor), block_shape)
        own_part = lax.dynamic_update_slice(
            own_part, current + arriving[member], (anchor, left_pairs[member, 0], anchor)
        )
    return own_part[None]


def solution(mesh):
    placed = (
        P("cuts", None, None, "tile"),
        P(),
        P(),
        P("tile", None, None),
        P("tile"),
        P("tile"),
        P("tile"),
    )
    return jax.shard_map(
        local, mesh=mesh, in_specs=placed, out_specs=P("cuts", None, None, "tile"), check_vma=False
    )
```

profile of v0, /device:TPU:0, one launch (start us, length us, event | category | flops | bytes accessed | tf_op | source)
XLA Modules:
  0.0 394.6 jit_solution(13673412457112158984)
XLA Ops:
  23.8 138.6 %while.42 = (s32[]{:T(128)}, bf16[4,2,128,128]{3,2,0,1:T(8,128)(2,1)S(1)}, bf16[4,4,2,128,128]{4,3,2,1,0:T(8,128)(2,1)S(1)}, s32[]{:T(128)}, pred[]{:T(512)}, /*...) while((s32[]{:T(128)}, ...), condition=%wide.region_5.6_spmd.clone.clone, body=%wide.region_0.5_spmd.clone.clone.sunk | while | flops 1613955072 | bytes 17564076 | solution.py:148
  24.0 9.5 %conditional.18 = (bf16[4,2,128,128]{3,2,0,1:T(8,128)(2,1)S(1)}) conditional(s32[]{:T(128)} %convert_element_type.236, () %tuple.220, (f32[128,128]{1,0:T(8,128)S(1)}, bf16[4,2,128,128]{3,2,1,0:T(8,128)(2,1)S(1)}, f32[4,2,128,128]{2,3,1,0:T(8,128)S(1)}, s32[]{:T(128)}, f32[128,128]{1,0:T(8,128)S(1)}, /*index=5*/f32[128,128]{1,0:T(8,128)S(1)}, ...), branch_computations={%region_1.1_spmd, %region_2.2_spmd.clone} | conditional | flops 1613594624 | bytes 15073308 | solution.py:138
  36.0 9.5 %conditional.18 = (bf16[4,2,128,128]{3,2,0,1:T(8,128)(2,1)S(1)}) conditional(s32[]{:T(128)} %convert_element_type.236, () %tuple.220, (f32[128,128]{1,0:T(8,128)S(1)}, bf16[4,2,128,128]{3,2,1,0:T(8,128)(2,1)S(1)}, f32[4,2,128,128]{2,3,1,0:T(8,128)S(1)}, s32[]{:T(128)}, f32[128,128]{1,0:T(8,128)S(1)}, /*index=5*/f32[128,128]{1,0:T(8,128)S(1)}, ...), branch_computations={%region_1.1_spmd, %region_2.2_spmd.clone} | conditional | flops 1613594624 | bytes 15073308 | solution.py:138
  49.0 9.5 %conditional.18 = (bf16[4,2,128,128]{3,2,0,1:T(8,128)(2,1)S(1)}) conditional(s32[]{:T(128)} %convert_element_type.236, () %tuple.220, (f32[128,128]{1,0:T(8,128)S(1)}, bf16[4,2,128,128]{3,2,1,0:T(8,128)(2,1)S(1)}, f32[4,2,128,128]{2,3,1,0:T(8,128)S(1)}, s32[]{:T(128)}, f32[128,128]{1,0:T(8,128)S(1)}, /*index=5*/f32[128,128]{1,0:T(8,128)S(1)}, ...), branch_computations={%region_1.1_spmd, %region_2.2_spmd.clone} | conditional | flops 1613594624 | bytes 15073308 | solution.py:138
  63.8 9.5 %conditional.18 = (bf16[4,2,128,128]{3,2,0,1:T(8,128)(2,1)S(1)}) conditional(s32[]{:T(128)} %convert_element_type.236, () %tuple.220, (f32[128,128]{1,0:T(8,128)S(1)}, bf16[4,2,128,128]{3,2,1,0:T(8,128)(2,1)S(1)}, f32[4,2,128,128]{2,3,1,0:T(8,128)S(1)}, s32[]{:T(128)}, f32[128,128]{1,0:T(8,128)S(1)}, /*index=5*/f32[128,128]{1,0:T(8,128)S(1)}, ...), branch_computations={%region_1.1_spmd, %region_2.2_spmd.clone} | conditional | flops 1613594624 | bytes 15073308 | solution.py:138
  81.2 16.0 %collective-permute-start = (bf16[4,2,128,128]{3,2,0,1:T(8,128)(2,1)S(1)}, bf16[4,2,128,128]{3,2,0,1:T(8,128)(2,1)S(1)}, u32[]{:S(2)}, u32[]{:S(2)}) collective-permute-start(bf16[4,2,128,128]{3,2,0,1:T(8,128)(2,1)S(1)} %get-tuple-element.1642), channel_id=1, source_target_pairs={{0,4},{4,8},{8,12},{12,16},{16,20},{20,24},{24,28},{1,5},{5,9},{9,... | collective-permute-start | bytes 786440 | tf_op jit(solution)/shard_map/while/body/eval_jaxpr/ppermute | solution.py:14
  98.5 6.6 %collective-permute-start = (bf16[4,2,128,128]{3,2,0,1:T(8,128)(2,1)S(1)}, bf16[4,2,128,128]{3,2,0,1:T(8,128)(2,1)S(1)}, u32[]{:S(2)}, u32[]{:S(2)}) collective-permute-start(bf16[4,2,128,128]{3,2,0,1:T(8,128)(2,1)S(1)} %get-tuple-element.1642), channel_id=1, source_target_pairs={{0,4},{4,8},{8,12},{12,16},{16,20},{20,24},{24,28},{1,5},{5,9},{9,... | collective-permute-start | bytes 786440 | tf_op jit(solution)/shard_map/while/body/eval_jaxpr/ppermute | solution.py:14
  106.3 16.0 %collective-permute-start = (bf16[4,2,128,128]{3,2,0,1:T(8,128)(2,1)S(1)}, bf16[4,2,128,128]{3,2,0,1:T(8,128)(2,1)S(1)}, u32[]{:S(2)}, u32[]{:S(2)}) collective-permute-start(bf16[4,2,128,128]{3,2,0,1:T(8,128)(2,1)S(1)} %get-tuple-element.1642), channel_id=1, source_target_pairs={{0,4},{4,8},{8,12},{12,16},{16,20},{20,24},{24,28},{1,5},{5,9},{9,... | collective-permute-start | bytes 786440 | tf_op jit(solution)/shard_map/while/body/eval_jaxpr/ppermute | solution.py:14
  131.5 7.1 %collective-permute-start = (bf16[4,2,128,128]{3,2,0,1:T(8,128)(2,1)S(1)}, bf16[4,2,128,128]{3,2,0,1:T(8,128)(2,1)S(1)}, u32[]{:S(2)}, u32[]{:S(2)}) collective-permute-start(bf16[4,2,128,128]{3,2,0,1:T(8,128)(2,1)S(1)} %get-tuple-element.1642), channel_id=1, source_target_pairs={{0,4},{4,8},{8,12},{12,16},{16,20},{20,24},{24,28},{1,5},{5,9},{9,... | collective-permute-start | bytes 786440 | tf_op jit(solution)/shard_map/while/body/eval_jaxpr/ppermute | solution.py:14
  147.8 13.5 %collective-permute-start = (bf16[4,2,128,128]{3,2,0,1:T(8,128)(2,1)S(1)}, bf16[4,2,128,128]{3,2,0,1:T(8,128)(2,1)S(1)}, u32[]{:S(2)}, u32[]{:S(2)}) collective-permute-start(bf16[4,2,128,128]{3,2,0,1:T(8,128)(2,1)S(1)} %get-tuple-element.1642), channel_id=1, source_target_pairs={{0,4},{4,8},{8,12},{12,16},{16,20},{20,24},{24,28},{1,5},{5,9},{9,... | collective-permute-start | bytes 786440 | tf_op jit(solution)/shard_map/while/body/eval_jaxpr/ppermute | solution.py:14
  162.6 196.0 %while.43 = (s32[]{:T(128)}, bf16[4,2,128,128]{3,2,0,1:T(8,128)(2,1)S(1)}, f32[4,2,128,128]{3,2,1,0:T(8,128)S(1)}, s32[]{:T(128)}, bf16[4,4,2,128,128]{4,3,1,2,0...) while((s32[]{:T(128)}, ...), condition=%wide.region_16.17_spmd.clone.clone, body=%wide.region_6.16_spmd.clone.clone.sunk | while | flops 1614643200 | bytes 18875232 | solution.py:181
  173.3 7.6 %collective-permute-done.1 = bf16[4,2,128,128]{3,2,0,1:T(8,128)(2,1)S(1)} collective-permute-done((bf16[4,2,128,128]{3,2,0,1:T(8,128)(2,1)S(1)}, bf16[4,2,128,128]{3,2,0,1:T(8,128)(2,1)S(1)}, u32[]{:S(2)}, u32[]{:S(2)}) %collective-permute-start.1) | collective-permute-done | bytes 262176 | tf_op jit(solution)/shard_map/while/body/eval_jaxpr/ppermute | solution.py:14
  191.6 13.9 %collective-permute-done.1 = bf16[4,2,128,128]{3,2,0,1:T(8,128)(2,1)S(1)} collective-permute-done((bf16[4,2,128,128]{3,2,0,1:T(8,128)(2,1)S(1)}, bf16[4,2,128,128]{3,2,0,1:T(8,128)(2,1)S(1)}, u32[]{:S(2)}, u32[]{:S(2)}) %collective-permute-start.1) | collective-permute-done | bytes 262176 | tf_op jit(solution)/shard_map/while/body/eval_jaxpr/ppermute | solution.py:14
  216.2 7.0 %collective-permute-done.1 = bf16[4,2,128,128]{3,2,0,1:T(8,128)(2,1)S(1)} collective-permute-done((bf16[4,2,128,128]{3,2,0,1:T(8,128)(2,1)S(1)}, bf16[4,2,128,128]{3,2,0,1:T(8,128)(2,1)S(1)}, u32[]{:S(2)}, u32[]{:S(2)}) %collective-permute-start.1) | collective-permute-done | bytes 262176 | tf_op jit(solution)/shard_map/while/body/eval_jaxpr/ppermute | solution.py:14
  225.3 65.5 %collective-permute-done.1 = bf16[4,2,128,128]{3,2,0,1:T(8,128)(2,1)S(1)} collective-permute-done((bf16[4,2,128,128]{3,2,0,1:T(8,128)(2,1)S(1)}, bf16[4,2,128,128]{3,2,0,1:T(8,128)(2,1)S(1)}, u32[]{:S(2)}, u32[]{:S(2)}) %collective-permute-start.1) | collective-permute-done | bytes 262176 | tf_op jit(solution)/shard_map/while/body/eval_jaxpr/ppermute | solution.py:14
  291.6 9.6 %conditional.20 = (f32[2,128,128]{2,1,0:T(8,128)S(1)}, bf16[4,2,128,128]{3,2,0,1:T(8,128)(2,1)S(1)}) conditional(s32[]{:T(128)} %convert_element_type.240, () %tuple.224, (bf16[4,4,2,128,128]{4,3,1,2,0:T(8,128)(2,1)S(1)}, s32[]{:T(128)}, s32[]{:T(128)}, f32[4,2,128,128]{2,3,1,0:T(8,128)S(1)}, f32[128,128]{1,0:T(8,128)S(1)}, ...), branch_computations={%region_7.7_spmd, %region_8.13_spmd.clone} | conditional | flops 1614413824 | bytes 17432990 | solution.py:171
  292.1 8.6 %conditional.13 = (f32[4,128,128]{2,1,0:T(8,128)S(1)}, f32[4,128,128]{2,1,0:T(8,128)S(1)}) conditional(s32[]{:T(128)} %convert_element_type.221, (f32[128,128]{1,0:T(8,128)S(1)}, bf16[4,2,128,128]{3,2,0,1:T(8,128)(2,1)S(1)}, f32[128,128]{1,0:T(8,128)S(1)}, f32[128,128]{1,0:T(8,128)S(1)}, f32[128,128]{1,0:T(8,128)S(1)}, ...), branch_computations={%region_9.8_spmd, %region_10.10_spmd} | conditional | flops 1613070336 | bytes 13631524 | solution.py:161
  309.6 9.6 %conditional.20 = (f32[2,128,128]{2,1,0:T(8,128)S(1)}, bf16[4,2,128,128]{3,2,0,1:T(8,128)(2,1)S(1)}) conditional(s32[]{:T(128)} %convert_element_type.240, () %tuple.224, (bf16[4,4,2,128,128]{4,3,1,2,0:T(8,128)(2,1)S(1)}, s32[]{:T(128)}, s32[]{:T(128)}, f32[4,2,128,128]{2,3,1,0:T(8,128)S(1)}, f32[128,128]{1,0:T(8,128)S(1)}, ...), branch_computations={%region_7.7_spmd, %region_8.13_spmd.clone} | conditional | flops 1614413824 | bytes 17432990 | solution.py:171
  310.1 8.6 %conditional.13 = (f32[4,128,128]{2,1,0:T(8,128)S(1)}, f32[4,128,128]{2,1,0:T(8,128)S(1)}) conditional(s32[]{:T(128)} %convert_element_type.221, (f32[128,128]{1,0:T(8,128)S(1)}, bf16[4,2,128,128]{3,2,0,1:T(8,128)(2,1)S(1)}, f32[128,128]{1,0:T(8,128)S(1)}, f32[128,128]{1,0:T(8,128)S(1)}, f32[128,128]{1,0:T(8,128)S(1)}, ...), branch_computations={%region_9.8_spmd, %region_10.10_spmd} | conditional | flops 1613070336 | bytes 13631524 | solution.py:161
  327.6 9.6 %conditional.20 = (f32[2,128,128]{2,1,0:T(8,128)S(1)}, bf16[4,2,128,128]{3,2,0,1:T(8,128)(2,1)S(1)}) conditional(s32[]{:T(128)} %convert_element_type.240, () %tuple.224, (bf16[4,4,2,128,128]{4,3,1,2,0:T(8,128)(2,1)S(1)}, s32[]{:T(128)}, s32[]{:T(128)}, f32[4,2,128,128]{2,3,1,0:T(8,128)S(1)}, f32[128,128]{1,0:T(8,128)S(1)}, ...), branch_computations={%region_7.7_spmd, %region_8.13_spmd.clone} | conditional | flops 1614413824 | bytes 17432990 | solution.py:171
  328.1 8.6 %conditional.13 = (f32[4,128,128]{2,1,0:T(8,128)S(1)}, f32[4,128,128]{2,1,0:T(8,128)S(1)}) conditional(s32[]{:T(128)} %convert_element_type.221, (f32[128,128]{1,0:T(8,128)S(1)}, bf16[4,2,128,128]{3,2,0,1:T(8,128)(2,1)S(1)}, f32[128,128]{1,0:T(8,128)S(1)}, f32[128,128]{1,0:T(8,128)S(1)}, f32[128,128]{1,0:T(8,128)S(1)}, ...), branch_computations={%region_9.8_spmd, %region_10.10_spmd} | conditional | flops 1613070336 | bytes 13631524 | solution.py:161
  345.6 9.6 %conditional.20 = (f32[2,128,128]{2,1,0:T(8,128)S(1)}, bf16[4,2,128,128]{3,2,0,1:T(8,128)(2,1)S(1)}) conditional(s32[]{:T(128)} %convert_element_type.240, () %tuple.224, (bf16[4,4,2,128,128]{4,3,1,2,0:T(8,128)(2,1)S(1)}, s32[]{:T(128)}, s32[]{:T(128)}, f32[4,2,128,128]{2,3,1,0:T(8,128)S(1)}, f32[128,128]{1,0:T(8,128)S(1)}, ...), branch_computations={%region_7.7_spmd, %region_8.13_spmd.clone} | conditional | flops 1614413824 | bytes 17432990 | solution.py:171
  346.2 8.6 %conditional.13 = (f32[4,128,128]{2,1,0:T(8,128)S(1)}, f32[4,128,128]{2,1,0:T(8,128)S(1)}) conditional(s32[]{:T(128)} %convert_element_type.221, (f32[128,128]{1,0:T(8,128)S(1)}, bf16[4,2,128,128]{3,2,0,1:T(8,128)(2,1)S(1)}, f32[128,128]{1,0:T(8,128)S(1)}, f32[128,128]{1,0:T(8,128)S(1)}, f32[128,128]{1,0:T(8,128)S(1)}, ...), branch_computations={%region_9.8_spmd, %region_10.10_spmd} | conditional | flops 1613070336 | bytes 13631524 | solution.py:161
  374.0 7.2 %collective-permute-done.3 = s32[4,2]{0,1:T(2,128)S(1)} collective-permute-done((s32[4,2]{0,1:T(2,128)S(1)}, s32[4,2]{0,1:T(2,128)S(1)}, u32[]{:S(2)}, u32[]{:S(2)}) %collective-permute-start.3) | collective-permute-done | bytes 64 | tf_op jit(solution)/shard_map/ppermute | solution.py:14
  (415 shorter events, 208.7 us)
Async XLA Ops:
  0.0 22.7 %collective-permute-start.2 = (f32[2,768,128]{2,1,0:T(8,128)}, f32[2,768,128]{2,1,0:T(8,128)S(1)}, u32[]{:S(2)}, u32[]{:S(2)}) collective-permute-start(f32[2,768,128]{2,1,0:T(8,128)} %bitcast.399), channel_id=1, source_target_pairs={{1,0},{2,1},{3,2},{5,4},{6,5},{7,6},{9,8},{10,9},{11,10},{13,12},{... | collective-permute-start | bytes 2359304 | tf_op jit(solution)/shard_map/ppermute | solution.py:14
  45.5 3.4 collective-permute-start
  58.5 5.2 %collective-permute-start = (bf16[4,2,128,128]{3,2,0,1:T(8,128)(2,1)S(1)}, bf16[4,2,128,128]{3,2,0,1:T(8,128)(2,1)S(1)}, u32[]{:S(2)}, u32[]{:S(2)}) collective-permute-start(bf16[4,2,128,128]{3,2,0,1:T(8,128)(2,1)S(1)} %get-tuple-element.1642), channel_id=1, source_target_pairs={{0,4},{4,8},{8,12},{12,16},{16,20},{20,24},{24,28},{1,5},{5,9},{9,... | collective-permute-start | bytes 786440 | tf_op jit(solution)/shard_map/while/body/eval_jaxpr/ppermute | solution.py:14
  73.3 7.7 %collective-permute-start = (bf16[4,2,128,128]{3,2,0,1:T(8,128)(2,1)S(1)}, bf16[4,2,128,128]{3,2,0,1:T(8,128)(2,1)S(1)}, u32[]{:S(2)}, u32[]{:S(2)}) collective-permute-start(bf16[4,2,128,128]{3,2,0,1:T(8,128)(2,1)S(1)} %get-tuple-element.1642), channel_id=1, source_target_pairs={{0,4},{4,8},{8,12},{12,16},{16,20},{20,24},{24,28},{1,5},{5,9},{9,... | collective-permute-start | bytes 786440 | tf_op jit(solution)/shard_map/while/body/eval_jaxpr/ppermute | solution.py:14
  81.2 17.1 %collective-permute-start = (bf16[4,2,128,128]{3,2,0,1:T(8,128)(2,1)S(1)}, bf16[4,2,128,128]{3,2,0,1:T(8,128)(2,1)S(1)}, u32[]{:S(2)}, u32[]{:S(2)}) collective-permute-start(bf16[4,2,128,128]{3,2,0,1:T(8,128)(2,1)S(1)} %get-tuple-element.1642), channel_id=1, source_target_pairs={{0,4},{4,8},{8,12},{12,16},{16,20},{20,24},{24,28},{1,5},{5,9},{9,... | collective-permute-start | bytes 786440 | tf_op jit(solution)/shard_map/while/body/eval_jaxpr/ppermute | solution.py:14
  98.5 7.7 %collective-permute-start = (bf16[4,2,128,128]{3,2,0,1:T(8,128)(2,1)S(1)}, bf16[4,2,128,128]{3,2,0,1:T(8,128)(2,1)S(1)}, u32[]{:S(2)}, u32[]{:S(2)}) collective-permute-start(bf16[4,2,128,128]{3,2,0,1:T(8,128)(2,1)S(1)} %get-tuple-element.1642), channel_id=1, source_target_pairs={{0,4},{4,8},{8,12},{12,16},{16,20},{20,24},{24,28},{1,5},{5,9},{9,... | collective-permute-start | bytes 786440 | tf_op jit(solution)/shard_map/while/body/eval_jaxpr/ppermute | solution.py:14
  106.3 17.1 %collective-permute-start = (bf16[4,2,128,128]{3,2,0,1:T(8,128)(2,1)S(1)}, bf16[4,2,128,128]{3,2,0,1:T(8,128)(2,1)S(1)}, u32[]{:S(2)}, u32[]{:S(2)}) collective-permute-start(bf16[4,2,128,128]{3,2,0,1:T(8,128)(2,1)S(1)} %get-tuple-element.1642), channel_id=1, source_target_pairs={{0,4},{4,8},{8,12},{12,16},{16,20},{20,24},{24,28},{1,5},{5,9},{9,... | collective-permute-start | bytes 786440 | tf_op jit(solution)/shard_map/while/body/eval_jaxpr/ppermute | solution.py:14
  123.6 7.7 %collective-permute-start = (bf16[4,2,128,128]{3,2,0,1:T(8,128)(2,1)S(1)}, bf16[4,2,128,128]{3,2,0,1:T(8,128)(2,1)S(1)}, u32[]{:S(2)}, u32[]{:S(2)}) collective-permute-start(bf16[4,2,128,128]{3,2,0,1:T(8,128)(2,1)S(1)} %get-tuple-element.1642), channel_id=1, source_target_pairs={{0,4},{4,8},{8,12},{12,16},{16,20},{20,24},{24,28},{1,5},{5,9},{9,... | collective-permute-start | bytes 786440 | tf_op jit(solution)/shard_map/while/body/eval_jaxpr/ppermute | solution.py:14
  131.5 8.2 %collective-permute-start = (bf16[4,2,128,128]{3,2,0,1:T(8,128)(2,1)S(1)}, bf16[4,2,128,128]{3,2,0,1:T(8,128)(2,1)S(1)}, u32[]{:S(2)}, u32[]{:S(2)}) collective-permute-start(bf16[4,2,128,128]{3,2,0,1:T(8,128)(2,1)S(1)} %get-tuple-element.1642), channel_id=1, source_target_pairs={{0,4},{4,8},{8,12},{12,16},{16,20},{20,24},{24,28},{1,5},{5,9},{9,... | collective-permute-start | bytes 786440 | tf_op jit(solution)/shard_map/while/body/eval_jaxpr/ppermute | solution.py:14
  139.9 7.7 %collective-permute-start = (bf16[4,2,128,128]{3,2,0,1:T(8,128)(2,1)S(1)}, bf16[4,2,128,128]{3,2,0,1:T(8,128)(2,1)S(1)}, u32[]{:S(2)}, u32[]{:S(2)}) collective-permute-start(bf16[4,2,128,128]{3,2,0,1:T(8,128)(2,1)S(1)} %get-tuple-element.1642), channel_id=1, source_target_pairs={{0,4},{4,8},{8,12},{12,16},{16,20},{20,24},{24,28},{1,5},{5,9},{9,... | collective-permute-start | bytes 786440 | tf_op jit(solution)/shard_map/while/body/eval_jaxpr/ppermute | solution.py:14
  147.8 14.6 %collective-permute-start = (bf16[4,2,128,128]{3,2,0,1:T(8,128)(2,1)S(1)}, bf16[4,2,128,128]{3,2,0,1:T(8,128)(2,1)S(1)}, u32[]{:S(2)}, u32[]{:S(2)}) collective-permute-start(bf16[4,2,128,128]{3,2,0,1:T(8,128)(2,1)S(1)} %get-tuple-element.1642), channel_id=1, source_target_pairs={{0,4},{4,8},{8,12},{12,16},{16,20},{20,24},{24,28},{1,5},{5,9},{9,... | collective-permute-start | bytes 786440 | tf_op jit(solution)/shard_map/while/body/eval_jaxpr/ppermute | solution.py:14
  163.6 7.6 %collective-permute-start.1 = (bf16[4,2,128,128]{3,2,0,1:T(8,128)(2,1)S(1)}, bf16[4,2,128,128]{3,2,0,1:T(8,128)(2,1)S(1)}, u32[]{:S(2)}, u32[]{:S(2)}) collective-permute-start(bf16[4,2,128,128]{3,2,0,1:T(8,128)(2,1)S(1)} %get-tuple-element.1539), channel_id=1, source_target_pairs={{4,0},{8,4},{12,8},{16,12},{20,16},{24,20},{28,24},{5,1},{9,5},{13... | collective-permute-start | bytes 786440 | tf_op jit(solution)/shard_map/while/body/eval_jaxpr/ppermute | solution.py:14
  172.0 9.0 %collective-permute-start.1 = (bf16[4,2,128,128]{3,2,0,1:T(8,128)(2,1)S(1)}, bf16[4,2,128,128]{3,2,0,1:T(8,128)(2,1)S(1)}, u32[]{:S(2)}, u32[]{:S(2)}) collective-permute-start(bf16[4,2,128,128]{3,2,0,1:T(8,128)(2,1)S(1)} %get-tuple-element.1539), channel_id=1, source_target_pairs={{4,0},{8,4},{12,8},{16,12},{20,16},{24,20},{28,24},{5,1},{9,5},{13... | collective-permute-start | bytes 786440 | tf_op jit(solution)/shard_map/while/body/eval_jaxpr/ppermute | solution.py:14
  181.8 7.7 %collective-permute-start.1 = (bf16[4,2,128,128]{3,2,0,1:T(8,128)(2,1)S(1)}, bf16[4,2,128,128]{3,2,0,1:T(8,128)(2,1)S(1)}, u32[]{:S(2)}, u32[]{:S(2)}) collective-permute-start(bf16[4,2,128,128]{3,2,0,1:T(8,128)(2,1)S(1)} %get-tuple-element.1539), channel_id=1, source_target_pairs={{4,0},{8,4},{12,8},{16,12},{20,16},{24,20},{28,24},{5,1},{9,5},{13... | collective-permute-start | bytes 786440 | tf_op jit(solution)/shard_map/while/body/eval_jaxpr/ppermute | solution.py:14
  190.3 15.3 %collective-permute-start.1 = (bf16[4,2,128,128]{3,2,0,1:T(8,128)(2,1)S(1)}, bf16[4,2,128,128]{3,2,0,1:T(8,128)(2,1)S(1)}, u32[]{:S(2)}, u32[]{:S(2)}) collective-permute-start(bf16[4,2,128,128]{3,2,0,1:T(8,128)(2,1)S(1)} %get-tuple-element.1539), channel_id=1, source_target_pairs={{4,0},{8,4},{12,8},{16,12},{20,16},{24,20},{28,24},{5,1},{9,5},{13... | collective-permute-start | bytes 786440 | tf_op jit(solution)/shard_map/while/body/eval_jaxpr/ppermute | solution.py:14
  206.4 7.7 %collective-permute-start.1 = (bf16[4,2,128,128]{3,2,0,1:T(8,128)(2,1)S(1)}, bf16[4,2,128,128]{3,2,0,1:T(8,128)(2,1)S(1)}, u32[]{:S(2)}, u32[]{:S(2)}) collective-permute-start(bf16[4,2,128,128]{3,2,0,1:T(8,128)(2,1)S(1)} %get-tuple-element.1539), channel_id=1, source_target_pairs={{4,0},{8,4},{12,8},{16,12},{20,16},{24,20},{28,24},{5,1},{9,5},{13... | collective-permute-start | bytes 786440 | tf_op jit(solution)/shard_map/while/body/eval_jaxpr/ppermute | solution.py:14
  214.9 8.3 %collective-permute-start.1 = (bf16[4,2,128,128]{3,2,0,1:T(8,128)(2,1)S(1)}, bf16[4,2,128,128]{3,2,0,1:T(8,128)(2,1)S(1)}, u32[]{:S(2)}, u32[]{:S(2)}) collective-permute-start(bf16[4,2,128,128]{3,2,0,1:T(8,128)(2,1)S(1)} %get-tuple-element.1539), channel_id=1, source_target_pairs={{4,0},{8,4},{12,8},{16,12},{20,16},{24,20},{28,24},{5,1},{9,5},{13... | collective-permute-start | bytes 786440 | tf_op jit(solution)/shard_map/while/body/eval_jaxpr/ppermute | solution.py:14
  224.0 66.9 %collective-permute-start.1 = (bf16[4,2,128,128]{3,2,0,1:T(8,128)(2,1)S(1)}, bf16[4,2,128,128]{3,2,0,1:T(8,128)(2,1)S(1)}, u32[]{:S(2)}, u32[]{:S(2)}) collective-permute-start(bf16[4,2,128,128]{3,2,0,1:T(8,128)(2,1)S(1)} %get-tuple-element.1539), channel_id=1, source_target_pairs={{4,0},{8,4},{12,8},{16,12},{20,16},{24,20},{28,24},{5,1},{9,5},{13... | collective-permute-start | bytes 786440 | tf_op jit(solution)/shard_map/while/body/eval_jaxpr/ppermute | solution.py:14
  301.2 7.7 %collective-permute-start.1 = (bf16[4,2,128,128]{3,2,0,1:T(8,128)(2,1)S(1)}, bf16[4,2,128,128]{3,2,0,1:T(8,128)(2,1)S(1)}, u32[]{:S(2)}, u32[]{:S(2)}) collective-permute-start(bf16[4,2,128,128]{3,2,0,1:T(8,128)(2,1)S(1)} %get-tuple-element.1539), channel_id=1, source_target_pairs={{4,0},{8,4},{12,8},{16,12},{20,16},{24,20},{28,24},{5,1},{9,5},{13... | collective-permute-start | bytes 786440 | tf_op jit(solution)/shard_map/while/body/eval_jaxpr/ppermute | solution.py:14
  319.2 7.7 %collective-permute-start.1 = (bf16[4,2,128,128]{3,2,0,1:T(8,128)(2,1)S(1)}, bf16[4,2,128,128]{3,2,0,1:T(8,128)(2,1)S(1)}, u32[]{:S(2)}, u32[]{:S(2)}) collective-permute-start(bf16[4,2,128,128]{3,2,0,1:T(8,128)(2,1)S(1)} %get-tuple-element.1539), channel_id=1, source_target_pairs={{4,0},{8,4},{12,8},{16,12},{20,16},{24,20},{28,24},{5,1},{9,5},{13... | collective-permute-start | bytes 786440 | tf_op jit(solution)/shard_map/while/body/eval_jaxpr/ppermute | solution.py:14
  337.2 7.7 %collective-permute-start.1 = (bf16[4,2,128,128]{3,2,0,1:T(8,128)(2,1)S(1)}, bf16[4,2,128,128]{3,2,0,1:T(8,128)(2,1)S(1)}, u32[]{:S(2)}, u32[]{:S(2)}) collective-permute-start(bf16[4,2,128,128]{3,2,0,1:T(8,128)(2,1)S(1)} %get-tuple-element.1539), channel_id=1, source_target_pairs={{4,0},{8,4},{12,8},{16,12},{20,16},{24,20},{28,24},{5,1},{9,5},{13... | collective-permute-start | bytes 786440 | tf_op jit(solution)/shard_map/while/body/eval_jaxpr/ppermute | solution.py:14
  355.2 3.4 collective-permute-start.1
  364.8 25.4 %collective-permute-start.4 = (f32[4,2,128,128]{3,2,1,0:T(8,128)S(1)}, f32[4,2,128,128]{3,2,1,0:T(8,128)S(1)}, u32[]{:S(2)}, u32[]{:S(2)}) collective-permute-start(f32[4,2,128,128]{3,2,1,0:T(8,128)S(1)} %pad_maximum_fusion.4), channel_id=1, source_target_pairs={{0,1},{1,2},{2,3},{4,5},{5,6},{6,7},{8,9},{9,10},{10,11},{12,13},{... | collective-permute-start | bytes 1572872 | tf_op jit(solution)/shard_map/ppermute | solution.py:14
  369.7 11.4 %collective-permute-start.3 = (s32[4,2]{0,1:T(2,128)S(1)}, s32[4,2]{0,1:T(2,128)S(1)}, u32[]{:S(2)}, u32[]{:S(2)}) collective-permute-start(s32[4,2]{0,1:T(2,128)S(1)} %pad_add_fusion), channel_id=1, source_target_pairs={{0,1},{1,2},{2,3},{4,5},{5,6},{6,7},{8,9},{9,10},{10,11},{12,13},{... | collective-permute-start | bytes 104 | tf_op jit(solution)/shard_map/ppermute | solution.py:14
  (5 other events, 38.3 us)
where the time goes:
time: 397 us; the launch traced here: 395 us
  waiting for transfers between devices  155 us (39%)
  starting transfers between devices  111 us (28%)
  matrix products  67.5 us (17%)
  between operations  23 us (6%)
  local copies, waits for them, and re-layouts  19.6 us (5%)
  other arithmetic  14.6 us (4%)
  loops' own time  4.08 us (1%)
    ppermute x25, waiting for transfers between devices, passed_along(): return lax.ppermute(block, axis, route)  155 us
    ppermute x25, starting transfers between devices, passed_along(): return lax.ppermute(block, axis, route)  111 us
    dot_general x16, matrix products, right_mul(): jnp.einsum('...jk,kl->...jl', imag_part, mat_imag, precision=HIGHEST)  9.44 us
    dot_general x16, matrix products, right_mul(): jnp.einsum('...jk,kl->...jl', imag_part, mat_real, precision=HIGHEST)  9.44 us
    dot_general x16, matrix products, right_mul(): jnp.einsum('...jk,kl->...jl', real_part, mat_imag, precision=HIGHEST)  9.43 us
    dot_general x16, matrix products, right_mul(): jnp.einsum('...jk,kl->...jl', real_part, mat_real, precision=HIGHEST)  9.43 us
  transfers between devices with their start and end apart: 25, of which 24 were waited for; matrix products, arithmetic and copies ran while one was open for 2% of the time, Pallas kernels for 0%

commit v1 on v0

v1 whole, which is shorter than its diff:
```python
import functools
import math

import jax
import jax.numpy as jnp
import numpy as np
from jax import lax
from jax.experimental import pallas as pl
from jax.experimental.pallas import tpu as pltpu
from jax.sharding import PartitionSpec as P

F32 = jnp.float32
BF16 = jnp.bfloat16
CORES = 2
ENTRY_SCALE = 1.62475

VMEM = pl.BlockSpec(memory_space=pltpu.VMEM)
SMEM = pl.BlockSpec(memory_space=pltpu.SMEM)


def passed_along(block, axis, distance):
    devices = range(lax.axis_size(axis))
    route = [(i - distance, i) for i in devices if i - distance in devices]
    return lax.ppermute(block, axis, route)


def rotated(block, distance):
    size = lax.axis_size("cuts")
    return lax.ppermute(block, "cuts", [(i, (i + distance) % size) for i in range(size)])


def swapped(block):
    size = lax.axis_size("cuts")
    return lax.ppermute(block, "cuts", [(i, i ^ 1) for i in range(size)])


def dft_blocks(win):
    numbers = np.arange(win)
    angles = (numbers[:, None] * numbers[None, :] % win) * (2.0 * math.pi / win)
    cosine, sine = np.cos(angles) * ENTRY_SCALE, np.sin(angles) * ENTRY_SCALE
    return np.block([[cosine, sine], [-sine, cosine]]).astype(np.float32)


def rolled_rows(strip_ref, part, row_at, win, rows_mask_from):
    last = strip_ref.shape[1] // win - 1
    block = row_at // win
    upper = strip_ref[part, pl.ds(pl.multiple_of(block * win, win), win), :]
    after = jnp.minimum(block + 1, last)
    lower = strip_ref[part, pl.ds(pl.multiple_of(after * win, win), win), :]
    return jnp.where(rows_mask_from >= row_at - block * win, upper, lower)


def rows_kernel(chips, slots, win, chip_ref, rows_ref, strip_ref, *out_refs):
    row_ids = lax.broadcasted_iota(jnp.int32, (win, win), 0)
    for r in range(chips):
        slot = lax.rem(chip_ref[0] + r, chips) // (chips // slots)
        row_at = rows_ref[slot]
        for part in range(2):
            out_refs[r][part] = rolled_rows(strip_ref, part, row_at, win, row_ids).astype(BF16)


def rolled_probe_kernel(win, place_ref, probe_ref, out_ref):
    row_at, col_at = lax.rem(place_ref[0], win), place_ref[1]
    for mode in range(probe_ref.shape[0]):
        for part in range(2):
            block = pltpu.roll(probe_ref[mode, part], row_at, 0)
            out_ref[mode, part] = pltpu.roll(block, col_at, 1).astype(BF16)


def window_kernel(chips, modes, win, *refs):
    slices = CORES * chips
    (ints_ref, weight_ref, left_ref, right_ref, probe_ref, hcos_ref, hsin_ref, target_ref) = refs[:8]
    own_refs = refs[8 : 8 + chips]
    other_refs = refs[8 + chips : 8 + 2 * chips]
    out_refs = refs[8 + 2 * chips : 8 + 3 * chips]
    patch_ref, wave_ref, grad_ref = refs[8 + 3 * chips :]
    chip, core = ints_ref[0], ints_ref[1]
    unit = 1.0 / (ENTRY_SCALE * ENTRY_SCALE * win)
    for r in range(chips):
        source = lax.rem(chip - r + chips, chips)
        patch_ref[CORES * source + core] = own_refs[r][...]
        patch_ref[CORES * source + 1 - core] = other_refs[r][...]

    def from_left(matrix, pairs):
        stacked = jnp.concatenate(
            [jnp.concatenate([pair[k].astype(BF16) for pair in pairs], 1) for k in range(2)], 0
        )
        prod = jnp.dot(matrix, stacked, preferred_element_type=F32)
        return [
            (prod[:win, m * win : (m + 1) * win], prod[win:, m * win : (m + 1) * win])
            for m in range(modes)
        ]

    def from_right(pairs, matrix):
        stacked = jnp.concatenate(
            [jnp.concatenate([pair[k].astype(BF16) for k in range(2)], 1) for pair in pairs], 0
        )
        prod = jnp.dot(stacked, matrix, preferred_element_type=F32)
        return [
            (prod[m * win : (m + 1) * win, :win], prod[m * win : (m + 1) * win, win:])
            for m in range(modes)
        ]

    def transform(pairs):
        return from_right(from_left(left_ref[...], pairs), right_ref[...])

    def inverse(pairs):
        return from_right(from_left(right_ref[...], pairs), left_ref[...])

    def mul(a, b):
        return (a[0] * b[0] - a[1] * b[1], a[0] * b[1] + a[1] * b[0])

    def conj_mul(a, b):
        return (a[0] * b[0] + a[1] * b[1], a[0] * b[1] - a[1] * b[0])

    def patch_at(s):
        return (patch_ref[s, 0].astype(F32), patch_ref[s, 1].astype(F32))

    def waves_at(s):
        return [(wave_ref[s, m, 0], wave_ref[s, m, 1]) for m in range(modes)]

    def propagator():
        return (hcos_ref[...], hsin_ref[...])

    for m in range(modes):
        for part in range(2):
            wave_ref[0, m, part] = probe_ref[m, part].astype(F32)

    def forward_step(s, carry):
        patch = patch_at(s)
        freq = transform([mul(wave, patch) for wave in waves_at(s)])
        spread = propagator()
        waves = inverse([mul(spread, pair) for pair in freq])
        for m in range(modes):
            for part in range(2):
                wave_ref[s + 1, m, part] = waves[m][part]
        return carry

    lax.fori_loop(0, slices - 1, forward_step, 0)
    patch = patch_at(slices - 1)
    exits = transform([mul(wave, patch) for wave in waves_at(slices - 1)])
    power = sum(pair[0] * pair[0] + pair[1] * pair[1] for pair in exits) * (unit * unit)
    factor = (power - target_ref[...]) * (weight_ref[0] * (0.25 * unit * unit))
    back = inverse([(factor * pair[0], factor * pair[1]) for pair in exits])

    def keep_grad(s, back):
        grads = [conj_mul(wave, pair) for wave, pair in zip(waves_at(s), back)]
        for part in range(2):
            grad_ref[s, part] = sum(grad[part] for grad in grads).astype(BF16)

    keep_grad(slices - 1, back)

    def backward_step(i, back):
        s = slices - 1 - i
        patch = patch_at(s)
        freq = transform([conj_mul(patch, pair) for pair in back])
        spread = propagator()
        back = inverse([conj_mul(spread, pair) for pair in freq])
        keep_grad(s - 1, back)
        return back

    lax.fori_loop(0, slices - 1, backward_step, back)
    for r in range(chips):
        dest = lax.rem(chip + r, chips)
        out_refs[r][...] = grad_ref[CORES * dest + core]


def place_kernel(chips, slots, win, from_left, *refs):
    chip_ref, rows_ref, cols_ref = refs[:3]
    block_refs = refs[3 : 3 + chips]
    out_ref = refs[-1]
    if from_left:
        out_ref[...] = refs[3 + chips][...]
    else:
        out_ref[...] = jnp.zeros_like(out_ref)
    row_ids = lax.broadcasted_iota(jnp.int32, (win, win), 0)
    col_ids = lax.broadcasted_iota(jnp.int32, (win, win), 1)
    last = out_ref.shape[1] // win - 1
    copies = chips // slots
    for r in range(chips):
        source = lax.rem(chip_ref[0] - r + chips, chips)
        slot = source // copies
        row_at, col_at = rows_ref[slot], cols_ref[slot]
        mine = (col_ids < col_at) if from_left else (col_ids >= col_at)
        counted = lax.rem(source, copies) == 0
        block = row_at // win
        after = jnp.minimum(block + 1, last)
        upper = row_ids >= row_at - block * win
        for part in range(2):
            grad = jnp.where(mine & counted, block_refs[r][part].astype(F32), 0.0)
            at = pl.ds(pl.multiple_of(block * win, win), win)
            out_ref[part, at, :] = out_ref[part, at, :] + jnp.where(upper, grad, 0.0)
            at = pl.ds(pl.multiple_of(after * win, win), win)
            out_ref[part, at, :] = out_ref[part, at, :] + jnp.where(upper, 0.0, grad)


def local(object_slices, probe_modes, prop_phase, measured, row_offsets, col_offsets, counts):
    modes, _, win, _ = probe_modes.shape
    slots = row_offsets.shape[0]
    chips = lax.axis_size("cuts") // CORES
    copies = chips // slots
    assert chips % slots == 0
    section = lax.axis_index("cuts")
    chip, core = section // CORES, section % CORES
    strip = object_slices[0]
    block = jax.ShapeDtypeStruct((2, win, win), BF16)

    left_places = passed_along(jnp.concatenate([row_offsets, col_offsets]), "tile", 1)
    left_rows, left_cols = left_places[:slots], left_places[slots:]
    chip_one = jnp.reshape(chip, (1,)).astype(jnp.int32)

    select_rows = pl.pallas_call(
        functools.partial(rows_kernel, chips, slots, win),
        out_shape=[block] * chips,
        in_specs=[SMEM, SMEM, VMEM],
        out_specs=[VMEM] * chips,
    )
    own_rows = select_rows(chip_one, row_offsets, strip)
    slot = chip // copies
    place = jnp.stack([row_offsets[slot], col_offsets[slot]])
    probe = pl.pallas_call(
        functools.partial(rolled_probe_kernel, win),
        out_shape=jax.ShapeDtypeStruct(probe_modes.shape, BF16),
        in_specs=[SMEM, VMEM],
        out_specs=VMEM,
    )(place, probe_modes)
    matrix = dft_blocks(win)
    left_matrix = jnp.asarray(matrix, BF16)
    right_matrix = jnp.asarray(matrix.T, BF16)
    unit = 1.0 / (ENTRY_SCALE * ENTRY_SCALE * win)
    hcos = jnp.cos(prop_phase) * (unit * unit)
    hsin = jnp.sin(prop_phase) * (unit * unit)
    target = lax.dynamic_index_in_dim(measured, slot, 0, keepdims=False)
    weight = (slot < counts).astype(F32)
    ints = jnp.stack([chip, core]).astype(jnp.int32)

    beside_rows = select_rows(chip_one, left_rows, strip)
    own_blocks, other_blocks = [None] * chips, [None] * chips
    col_ids = lax.broadcasted_iota(jnp.int32, (2, win, win), 2)
    for r in list(range(1, chips)) + [0]:
        arrived = passed_along(beside_rows[r], "tile", -1)
        col_at = col_offsets[(chip + r) % chips // copies]
        merged = jnp.where(col_ids >= col_at, own_rows[r], arrived)
        own_blocks[r] = rotated(merged, CORES * r) if r else merged
        other_blocks[r] = swapped(own_blocks[r])

    grads = pl.pallas_call(
        functools.partial(window_kernel, chips, modes, win),
        out_shape=[block] * chips,
        in_specs=[SMEM, SMEM] + [VMEM] * (6 + 2 * chips),
        out_specs=[VMEM] * chips,
        scratch_shapes=[
            pltpu.VMEM((CORES * chips, 2, win, win), BF16),
            pltpu.VMEM((CORES * chips, modes, 2, win, win), F32),
            pltpu.VMEM((CORES * chips, 2, win, win), BF16),
        ],
        compiler_params=pltpu.CompilerParams(vmem_limit_bytes=48 * 2**20),
    )(ints, weight, left_matrix, right_matrix, probe, hcos, hsin, target, *own_blocks, *other_blocks)

    mine, wrapped = [], []
    for r in range(chips):
        arrived = rotated(grads[r], CORES * r) if r else grads[r]
        mine.append(arrived)
        wrapped.append(passed_along(arrived, "tile", 1))

    def placed(from_left, rows, cols, *arrays):
        return pl.pallas_call(
            functools.partial(place_kernel, chips, slots, win, from_left),
            out_shape=jax.ShapeDtypeStruct(strip.shape, F32),
            in_specs=[SMEM, SMEM, SMEM] + [VMEM] * len(arrays),
            out_specs=VMEM,
            input_output_aliases={3 + chips: 0} if from_left else {},
        )(chip_one, rows, cols, *arrays)

    own_part = placed(False, row_offsets, col_offsets, *mine)
    return placed(True, left_rows, left_cols, *wrapped, own_part)[None]


def solution(mesh):
    placed = (
        P("cuts", None, None, "tile"),
        P(),
        P(),
        P("tile", None, None),
        P("tile"),
        P("tile"),
        P("tile"),
    )
    return jax.shard_map(
        local, mesh=mesh, in_specs=placed, out_specs=P("cuts", None, None, "tile"), check_vma=False
    )
```

time: 397 us -> 77.6 us (0.20)
  waiting for transfers between devices: 155 us -> 6.14 us
  starting transfers between devices: 111 us -> 36 us
  matrix products: 67.5 us -> 0 us
  Pallas kernels: 0 us -> 23.3 us
  between operations: 23 us -> 1.09 us
  local copies, waits for them, and re-layouts: 19.6 us -> 4.81 us
  other arithmetic: 14.6 us -> 5.66 us
  loops' own time: 4.08 us -> 0 us
    ppermute x25 -> x9, waiting for transfers between devices: 155 us -> 3.65 us  [passed_along(): return lax.ppermute(block, axis, route)]
    ppermute x25 -> x9, starting transfers between devices: 111 us -> 23.7 us  [passed_along(): return lax.ppermute(block, axis, route)]
    dot_general x128 -> x0, matrix products: 67.5 us -> none  [the longest x16 9.44 us: right_mul(): jnp.einsum('...jk,kl->...jl', imag_part, mat_imag, precision=HIGHEST)]
    pallas_call x0 -> x6, Pallas kernels: none -> 23.3 us  [the longest x1 13.1 us: local(): pl.pallas_call(functools.partial(window_kernel, chips, modes, win), out_s...]
    ppermute x0 -> x10, starting transfers between devices: none -> 12.3 us  [the longest x6 11.7 us: rotated(): lax.ppermute(block, 'cuts', [(i, (i + distance) % size) for i in range(si...]
    dynamic_update_slice x20 -> x0, local copies, waits for them, and re-layouts: 9.95 us -> none  [the longest x4 3.87 us: local(): lax.dynamic_update_slice(widened, grad_store[member], (anchor, anchor, co...]
    convert_element_type x12 -> x0, other arithmetic: 8.23 us -> none  [the longest x11 7.15 us: local(): (jnp.arange(slot_count, dtype=jnp.int32) < counts[0]).astype(jnp.float32)]
    another operation x50 -> x0, loops' own time: 4.08 us -> none  [the longest x1 0.97 us: local(): lax.fori_loop(0, sections + slot_count - 1, backward_step, (start_wave, s...]
  transfers between devices with their start and end apart: 25 -> 19, of which waited for: 24 -> 6; matrix products, arithmetic and copies ran while one was open for 2% -> 8% of each run, Pallas kernels for 0% -> 8%
where the time goes in v1:
time: 77.6 us; the launch traced here: 77 us
  starting transfers between devices  36 us (46%)
  Pallas kernels  23.3 us (30%)
  waiting for transfers between devices  6.14 us (8%)
  other arithmetic  5.66 us (7%)
  local copies, waits for them, and re-layouts  4.81 us (6%)
  between operations  1.09 us (1%)
    ppermute x9, starting transfers between devices, passed_along(): return lax.ppermute(block, axis, route)  23.7 us
    pallas_call x1, Pallas kernels, local(): pl.pallas_call(functools.partial(window_kernel, chips, modes, win), out_s...  13.1 us
    ppermute x6, starting transfers between devices, rotated(): lax.ppermute(block, 'cuts', [(i, (i + distance) % size) for i in range(si...  11.7 us
    pallas_call x2, Pallas kernels, placed(): pl.pallas_call(functools.partial(place_kernel, chips, slots, win, from_le...  4.37 us
    ppermute x9, waiting for transfers between devices, passed_along(): return lax.ppermute(block, axis, route)  3.65 us
    unnamed x38, local copies, waits for them, and re-layouts  2.82 us
    ge x4, other arithmetic, local(): merged = jnp.where(col_ids >= col_at, own_rows[r], arrived)  2.61 us
    pallas_call x1, Pallas kernels, local(): pl.pallas_call(functools.partial(rolled_probe_kernel, win), out_shape=jax...  1.94 us
  transfers between devices with their start and end apart: 19, of which 6 were waited for; matrix products, arithmetic and copies ran while one was open for 8% of the time, Pallas kernels for 8%

profile of v1, /device:TPU:0, one launch (start us, length us, event | category | flops | bytes accessed | tf_op | source)
XLA Modules:
  0.0 77.0 jit_solution(4581296706914694994)
XLA Ops:
  0.0 0.8 %pad_add_fusion = s32[8]{0:T(128)S(1)} fusion(s32[4]{0:T(128)} %refs_2_.2, s32[4]{0:T(128)} %refs_1_.1), kind=kLoop, calls=%fused_computation.7 | loop fusion | flops 8 | bytes 64 | tf_op jit(solution)/shard_map/concatenate | solution.py:208
  0.8 4.8 %collective-permute-start = (s32[8]{0:T(128)S(1)}, s32[8]{0:T(128)S(1)}, u32[]{:S(2)}, u32[]{:S(2)}) collective-permute-start(s32[8]{0:T(128)S(1)} %pad_add_fusion), channel_id=1, source_target_pairs={{0,1},{1,2},{2,3},{4,5},{5,6},{6,7},{8,9},{9,10},{10,11},{12,13},{... | collective-permute-start | bytes 104 | tf_op jit(solution)/shard_map/ppermute | solution.py:24
  11.1 0.8 %copy-done.5 = f32[128,128]{1,0:T(8,128)S(1)} copy-done((f32[128,128]{1,0:T(8,128)S(1)}, f32[128,128]{1,0:T(8,128)}, u32[]{:S(2)}) %copy-start.5) | copy-done | bytes 65560
  12.1 1.9 %shard_map.92 = (bf16[2,128,128]{2,1,0:T(8,128)(2,1)}, bf16[2,128,128]{2,1,0:T(8,128)(2,1)}, bf16[2,128,128]{2,1,0:T(8,128)(2,1)}, bf16[2,128,128]{2,1,0:T(8,128)(2,1)}) custom-call(s32[1]{0:T(128)} %bitcast.chip_ref.refs_0_, s32[4]{0:T(128)} %refs_1_.1, f32[2,768,128]{2,1,0:T(8,128)} %bitcast.10), custom_call_target="tpu_custom_call" | custom-call | tf_op jit(solution)/shard_map/pallas_call | solution.py:218
  14.0 1.9 %pad_add_fusion.2.place_ref = s32[2]{0:T(128)} fusion(s32[1]{0:T(128)} %get-tuple-element.35, s32[1]{0:T(128)} %dynamic_slice.22), kind=kLoop, calls=%fused_computation.9 | loop fusion | flops 2 | bytes 16 | tf_op jit(solution)/shard_map/stack | solution.py:220
  15.9 1.9 %shard_map.91.refs_4_ = bf16[4,2,128,128]{3,2,1,0:T(8,128)(2,1)} custom-call(s32[2]{0:T(128)} %pad_add_fusion.2.place_ref, f32[4,2,128,128]{3,2,1,0:T(8,128)} %probe_ref.1), custom_call_target="tpu_custom_call" | custom-call | tf_op jit(solution)/shard_map/pallas_call | solution.py:221
  18.5 1.9 %shard_map.93 = (bf16[2,128,128]{2,1,0:T(8,128)(2,1)}, bf16[2,128,128]{2,1,0:T(8,128)(2,1)}, bf16[2,128,128]{2,1,0:T(8,128)(2,1)}, bf16[2,128,128]{2,1,0:T(8,128)(2,1)}) custom-call(s32[1]{0:T(128)} %bitcast.chip_ref.refs_0_, s32[4]{0:T(128)} %get-tuple-element.37.rows_ref.refs_1_, f32[2,768,128]{2,1,0:T(8,128)} %bitcast.11), custom_call_target="tpu_custom_call" | custom-call | tf_op jit(solution)/shard_map/pallas_call | solution.py:237
  20.5 1.3 %collective-permute-start.2 = (bf16[2,128,128]{2,1,0:T(8,128)(2,1)}, bf16[2,128,128]{2,1,0:T(8,128)(2,1)S(1)}, u32[]{:S(2)}, u32[]{:S(2)}) collective-permute-start(bf16[2,128,128]{2,1,0:T(8,128)(2,1)} %get-tuple-element.20), channel_id=1, source_target_pairs={{1,0},{2,1},{3,2},{5,4},{6,5},{7,6},{9,8},{10,9},{11,10},{13,12},{... | collective-permute-start | bytes 196616 | tf_op jit(solution)/shard_map/ppermute | solution.py:24
  22.4 1.3 %collective-permute-start.1 = (bf16[2,128,128]{2,1,0:T(8,128)(2,1)}, bf16[2,128,128]{2,1,0:T(8,128)(2,1)S(1)}, u32[]{:S(2)}, u32[]{:S(2)}) collective-permute-start(bf16[2,128,128]{2,1,0:T(8,128)(2,1)} %get-tuple-element.18), channel_id=1, source_target_pairs={{1,0},{2,1},{3,2},{5,4},{6,5},{7,6},{9,8},{10,9},{11,10},{13,12},{... | collective-permute-start | bytes 196616 | tf_op jit(solution)/shard_map/ppermute | solution.py:24
  23.7 1.3 %collective-permute-start.4 = (bf16[2,128,128]{2,1,0:T(8,128)(2,1)}, bf16[2,128,128]{2,1,0:T(8,128)(2,1)S(1)}, u32[]{:S(2)}, u32[]{:S(2)}) collective-permute-start(bf16[2,128,128]{2,1,0:T(8,128)(2,1)} %get-tuple-element.22), channel_id=1, source_target_pairs={{1,0},{2,1},{3,2},{5,4},{6,5},{7,6},{9,8},{10,9},{11,10},{13,12},{... | collective-permute-start | bytes 196616 | tf_op jit(solution)/shard_map/ppermute | solution.py:24
  25.0 1.3 %collective-permute-start.6 = (bf16[2,128,128]{2,1,0:T(8,128)(2,1)}, bf16[2,128,128]{2,1,0:T(8,128)(2,1)S(1)}, u32[]{:S(2)}, u32[]{:S(2)}) collective-permute-start(bf16[2,128,128]{2,1,0:T(8,128)(2,1)} %get-tuple-element.24), channel_id=1, source_target_pairs={{1,0},{2,1},{3,2},{5,4},{6,5},{7,6},{9,8},{10,9},{11,10},{13,12},{... | collective-permute-start | bytes 196616 | tf_op jit(solution)/shard_map/ppermute | solution.py:24
  26.8 1.6 %collective-permute-start.3 = (bf16[2,128,128]{2,1,0:T(8,128)(2,1)S(1)}, bf16[2,128,128]{2,1,0:T(8,128)(2,1)S(1)}, u32[]{:S(2)}, u32[]{:S(2)}) collective-permute-start(bf16[2,128,128]{2,1,0:T(8,128)(2,1)S(1)} %broadcast_select_fusion.2), channel_id=1, source_target_pairs={{0,8},{4,12},{8,16},{12,20},{16,24},{20,28},{24,0},{28,4},{1,9},{5... | collective-permute-start | bytes 196616 | tf_op jit(solution)/shard_map/ppermute | solution.py:29
  28.5 3.1 %collective-permute-done.4 = bf16[2,128,128]{2,1,0:T(8,128)(2,1)S(1)} collective-permute-done((bf16[2,128,128]{2,1,0:T(8,128)(2,1)}, bf16[2,128,128]{2,1,0:T(8,128)(2,1)S(1)}, u32[]{:S(2)}, u32[]{:S(2)}) %collective-permute-start.4) | collective-permute-done | bytes 65568 | tf_op jit(solution)/shard_map/ppermute | solution.py:24
  31.6 2.7 %collective-permute-start.5 = (bf16[2,128,128]{2,1,0:T(8,128)(2,1)S(1)}, bf16[2,128,128]{2,1,0:T(8,128)(2,1)S(1)}, u32[]{:S(2)}, u32[]{:S(2)}) collective-permute-start(bf16[2,128,128]{2,1,0:T(8,128)(2,1)S(1)} %broadcast_select_fusion.1), channel_id=1, source_target_pairs={{0,16},{4,20},{8,24},{12,28},{16,0},{20,4},{24,8},{28,12},{1,17},{... | collective-permute-start | bytes 196616 | tf_op jit(solution)/shard_map/ppermute | solution.py:29
  34.3 2.6 %collective-permute-start.7 = (bf16[2,128,128]{2,1,0:T(8,128)(2,1)S(1)}, bf16[2,128,128]{2,1,0:T(8,128)(2,1)S(1)}, u32[]{:S(2)}, u32[]{:S(2)}) collective-permute-start(bf16[2,128,128]{2,1,0:T(8,128)(2,1)S(1)} %broadcast_select_fusion), channel_id=1, source_target_pairs={{0,24},{4,28},{8,0},{12,4},{16,8},{20,12},{24,16},{28,20},{1,25},{... | collective-permute-start | bytes 196616 | tf_op jit(solution)/shard_map/ppermute | solution.py:29
  40.1 13.1 %shard_map.94 = (bf16[2,128,128]{2,1,0:T(8,128)(2,1)S(1)}, bf16[2,128,128]{2,1,0:T(8,128)(2,1)S(1)}, bf16[2,128,128]{2,1,0:T(8,128)(2,1)S(1)}, bf16[2,128,128]{2,1,0:T(8,128)(2,1)S(1)}) custom-call(s32[2]{0:T(128)S(1)} %pad_add_fusion.1.refs_0_, f32[1]{0:T(128)S(6)} %convert_element_type.3.refs_1_, bf16[256,256]{1,0:T(8,128)(2,1)S(1)} %copy-done.3, ...), custom_call_target="tpu_custom_call" | custom-call | tf_op jit(solution)/shard_map/pallas_call | solution.py:247
  53.3 1.4 %collective-permute-start.13 = (bf16[2,128,128]{2,1,0:T(8,128)(2,1)S(1)}, bf16[2,128,128]{2,1,0:T(8,128)(2,1)S(1)}, u32[]{:S(2)}, u32[]{:S(2)}) collective-permute-start(bf16[2,128,128]{2,1,0:T(8,128)(2,1)S(1)} %get-tuple-element.26), channel_id=1, source_target_pairs={{0,8},{4,12},{8,16},{12,20},{16,24},{20,28},{24,0},{28,4},{1,9},{5... | collective-permute-start | bytes 196616 | tf_op jit(solution)/shard_map/ppermute | solution.py:29
  54.7 3.4 %collective-permute-start.15 = (bf16[2,128,128]{2,1,0:T(8,128)(2,1)S(1)}, bf16[2,128,128]{2,1,0:T(8,128)(2,1)S(1)}, u32[]{:S(2)}, u32[]{:S(2)}) collective-permute-start(bf16[2,128,128]{2,1,0:T(8,128)(2,1)S(1)} %get-tuple-element.27), channel_id=1, source_target_pairs={{0,16},{4,20},{8,24},{12,28},{16,0},{20,4},{24,8},{28,12},{1,17},{... | collective-permute-start | bytes 196616 | tf_op jit(solution)/shard_map/ppermute | solution.py:29
  58.0 4.8 %collective-permute-start.12 = (bf16[2,128,128]{2,1,0:T(8,128)(2,1)S(1)}, bf16[2,128,128]{2,1,0:T(8,128)(2,1)S(1)}, u32[]{:S(2)}, u32[]{:S(2)}) collective-permute-start(bf16[2,128,128]{2,1,0:T(8,128)(2,1)S(1)} %get-tuple-element.25.refs_3_), channel_id=1, source_target_pairs={{0,1},{1,2},{2,3},{4,5},{5,6},{6,7},{8,9},{9,10},{10,11},{12,13},{... | collective-permute-start | bytes 196616 | tf_op jit(solution)/shard_map/ppermute | solution.py:24
  62.9 3.9 %collective-permute-start.14 = (bf16[2,128,128]{2,1,0:T(8,128)(2,1)S(1)}, bf16[2,128,128]{2,1,0:T(8,128)(2,1)S(1)}, u32[]{:S(2)}, u32[]{:S(2)}) collective-permute-start(bf16[2,128,128]{2,1,0:T(8,128)(2,1)S(1)} %collective-permute-done.13.refs_4_), channel_id=1, source_target_pairs={{0,1},{1,2},{2,3},{4,5},{5,6},{6,7},{8,9},{9,10},{10,11},{12,13},{... | collective-permute-start | bytes 196616 | tf_op jit(solution)/shard_map/ppermute | solution.py:24
  66.9 2.4 %collective-permute-start.16 = (bf16[2,128,128]{2,1,0:T(8,128)(2,1)S(1)}, bf16[2,128,128]{2,1,0:T(8,128)(2,1)S(1)}, u32[]{:S(2)}, u32[]{:S(2)}) collective-permute-start(bf16[2,128,128]{2,1,0:T(8,128)(2,1)S(1)} %collective-permute-done.15.refs_5_), channel_id=1, source_target_pairs={{0,1},{1,2},{2,3},{4,5},{5,6},{6,7},{8,9},{9,10},{10,11},{12,13},{... | collective-permute-start | bytes 196616 | tf_op jit(solution)/shard_map/ppermute | solution.py:24
  69.2 2.6 %collective-permute-start.18 = (bf16[2,128,128]{2,1,0:T(8,128)(2,1)S(1)}, bf16[2,128,128]{2,1,0:T(8,128)(2,1)S(1)}, u32[]{:S(2)}, u32[]{:S(2)}) collective-permute-start(bf16[2,128,128]{2,1,0:T(8,128)(2,1)S(1)} %collective-permute-done.17.refs_6_), channel_id=1, source_target_pairs={{0,1},{1,2},{2,3},{4,5},{5,6},{6,7},{8,9},{9,10},{10,11},{12,13},{... | collective-permute-start | bytes 196616 | tf_op jit(solution)/shard_map/ppermute | solution.py:24
  71.9 2.0 %shard_map.95.refs_7_ = f32[2,768,128]{2,1,0:T(8,128)} custom-call(s32[1]{0:T(128)} %bitcast.chip_ref.refs_0_, s32[4]{0:T(128)} %refs_1_.1, s32[4]{0:T(128)} %refs_2_.2, bf16[2,128,128]{2,1,0:T(8,128)(2,1)} %copy-done.4, bf16[2,128,128]{2,1,0:T(8,128)(2,1)} %copy-done.10, bf16[2,128,128]{2,1,0:T(8,128)(2,1)} %copy-done.11, bf16[2,128,128]{2,1,0:T(8,128)(2,1)} %copy-done.12), custom_call_target="tpu_custom_call" | custom-call | tf_op jit(solution)/shard_map/pallas_call | solution.py:267
  74.6 2.4 %shard_map.96 = f32[2,768,128]{2,1,0:T(8,128)} custom-call(s32[1]{0:T(128)} %bitcast.chip_ref.refs_0_, s32[4]{0:T(128)} %get-tuple-element.37.rows_ref.refs_1_, s32[4]{0:T(128)} %get-tuple-element.36.refs_2_, bf16[2,128,128]{2,1,0:T(8,128)(2,1)} %copy-done.13, bf16[2,128,128]{2,1,0:T(8,128)(2,1)} %copy-done.14, ...), custom_call_target="tpu_custom_call", output_to_operand_aliasing={{}: (7, {})} | custom-call | tf_op jit(solution)/shard_map/pallas_call | solution.py:267
  (74 shorter events, 10.6 us)
Async XLA Ops:
  0.0 11.0 %copy-start = (f32[4,128,128]{2,1,0:T(8,128)S(1)}, f32[4,128,128]{2,1,0:T(8,128)}, u32[]{:S(2)}) copy-start(f32[4,128,128]{2,1,0:T(8,128)} %param.12) | copy-start | bytes 786436
  0.8 17.1 %collective-permute-start = (s32[8]{0:T(128)S(1)}, s32[8]{0:T(128)S(1)}, u32[]{:S(2)}, u32[]{:S(2)}) collective-permute-start(s32[8]{0:T(128)S(1)} %pad_add_fusion), channel_id=1, source_target_pairs={{0,1},{1,2},{2,3},{4,5},{5,6},{6,7},{8,9},{9,10},{10,11},{12,13},{... | collective-permute-start | bytes 104 | tf_op jit(solution)/shard_map/ppermute | solution.py:24
  18.5 8.3 %copy-start.9 = (bf16[2,128,128]{2,1,0:T(8,128)(2,1)S(1)}, bf16[2,128,128]{2,1,0:T(8,128)(2,1)}, u32[]{:S(2)}) copy-start(bf16[2,128,128]{2,1,0:T(8,128)(2,1)} %get-tuple-element.19) | copy-start | bytes 196612
  20.5 6.4 %collective-permute-start.2 = (bf16[2,128,128]{2,1,0:T(8,128)(2,1)}, bf16[2,128,128]{2,1,0:T(8,128)(2,1)S(1)}, u32[]{:S(2)}, u32[]{:S(2)}) collective-permute-start(bf16[2,128,128]{2,1,0:T(8,128)(2,1)} %get-tuple-element.20), channel_id=1, source_target_pairs={{1,0},{2,1},{3,2},{5,4},{6,5},{7,6},{9,8},{10,9},{11,10},{13,12},{... | collective-permute-start | bytes 196616 | tf_op jit(solution)/shard_map/ppermute | solution.py:24
  22.4 14.5 %collective-permute-start.1 = (bf16[2,128,128]{2,1,0:T(8,128)(2,1)}, bf16[2,128,128]{2,1,0:T(8,128)(2,1)S(1)}, u32[]{:S(2)}, u32[]{:S(2)}) collective-permute-start(bf16[2,128,128]{2,1,0:T(8,128)(2,1)} %get-tuple-element.18), channel_id=1, source_target_pairs={{1,0},{2,1},{3,2},{5,4},{6,5},{7,6},{9,8},{10,9},{11,10},{13,12},{... | collective-permute-start | bytes 196616 | tf_op jit(solution)/shard_map/ppermute | solution.py:24
  23.7 7.9 %collective-permute-start.4 = (bf16[2,128,128]{2,1,0:T(8,128)(2,1)}, bf16[2,128,128]{2,1,0:T(8,128)(2,1)S(1)}, u32[]{:S(2)}, u32[]{:S(2)}) collective-permute-start(bf16[2,128,128]{2,1,0:T(8,128)(2,1)} %get-tuple-element.22), channel_id=1, source_target_pairs={{1,0},{2,1},{3,2},{5,4},{6,5},{7,6},{9,8},{10,9},{11,10},{13,12},{... | collective-permute-start | bytes 196616 | tf_op jit(solution)/shard_map/ppermute | solution.py:24
  25.0 9.3 %collective-permute-start.6 = (bf16[2,128,128]{2,1,0:T(8,128)(2,1)}, bf16[2,128,128]{2,1,0:T(8,128)(2,1)S(1)}, u32[]{:S(2)}, u32[]{:S(2)}) collective-permute-start(bf16[2,128,128]{2,1,0:T(8,128)(2,1)} %get-tuple-element.24), channel_id=1, source_target_pairs={{1,0},{2,1},{3,2},{5,4},{6,5},{7,6},{9,8},{10,9},{11,10},{13,12},{... | collective-permute-start | bytes 196616 | tf_op jit(solution)/shard_map/ppermute | solution.py:24
  26.8 10.2 %collective-permute-start.3 = (bf16[2,128,128]{2,1,0:T(8,128)(2,1)S(1)}, bf16[2,128,128]{2,1,0:T(8,128)(2,1)S(1)}, u32[]{:S(2)}, u32[]{:S(2)}) collective-permute-start(bf16[2,128,128]{2,1,0:T(8,128)(2,1)S(1)} %broadcast_select_fusion.2), channel_id=1, source_target_pairs={{0,8},{4,12},{8,16},{12,20},{16,24},{20,28},{24,0},{28,4},{1,9},{5... | collective-permute-start | bytes 196616 | tf_op jit(solution)/shard_map/ppermute | solution.py:29
  31.6 8.5 %copy-start.1 = (bf16[4,2,128,128]{3,2,1,0:T(8,128)(2,1)S(1)}, bf16[4,2,128,128]{3,2,1,0:T(8,128)(2,1)}, u32[]{:S(2)}) copy-start(bf16[4,2,128,128]{3,2,1,0:T(8,128)(2,1)} %shard_map.91.refs_4_) | copy-start | bytes 786436
  31.6 6.6 %collective-permute-start.5 = (bf16[2,128,128]{2,1,0:T(8,128)(2,1)S(1)}, bf16[2,128,128]{2,1,0:T(8,128)(2,1)S(1)}, u32[]{:S(2)}, u32[]{:S(2)}) collective-permute-start(bf16[2,128,128]{2,1,0:T(8,128)(2,1)S(1)} %broadcast_select_fusion.1), channel_id=1, source_target_pairs={{0,16},{4,20},{8,24},{12,28},{16,0},{20,4},{24,8},{28,12},{1,17},{... | collective-permute-start | bytes 196616 | tf_op jit(solution)/shard_map/ppermute | solution.py:29
  34.3 4.6 %collective-permute-start.7 = (bf16[2,128,128]{2,1,0:T(8,128)(2,1)S(1)}, bf16[2,128,128]{2,1,0:T(8,128)(2,1)S(1)}, u32[]{:S(2)}, u32[]{:S(2)}) collective-permute-start(bf16[2,128,128]{2,1,0:T(8,128)(2,1)S(1)} %broadcast_select_fusion), channel_id=1, source_target_pairs={{0,24},{4,28},{8,0},{12,4},{16,8},{20,12},{24,16},{28,20},{1,25},{... | collective-permute-start | bytes 196616 | tf_op jit(solution)/shard_map/ppermute | solution.py:29
  37.0 2.0 %collective-permute-start.8 = (bf16[2,128,128]{2,1,0:T(8,128)(2,1)S(1)}, bf16[2,128,128]{2,1,0:T(8,128)(2,1)S(1)}, u32[]{:S(2)}, u32[]{:S(2)}) collective-permute-start(bf16[2,128,128]{2,1,0:T(8,128)(2,1)S(1)} %broadcast_select_fusion.3.refs_8_), channel_id=1, source_target_pairs={{0,4},{4,0},{8,12},{12,8},{16,20},{20,16},{24,28},{28,24},{1,5},{5... | collective-permute-start | bytes 196616 | tf_op jit(solution)/shard_map/ppermute | solution.py:34
  37.0 1.9 %collective-permute-start.9 = (bf16[2,128,128]{2,1,0:T(8,128)(2,1)S(1)}, bf16[2,128,128]{2,1,0:T(8,128)(2,1)S(1)}, u32[]{:S(2)}, u32[]{:S(2)}) collective-permute-start(bf16[2,128,128]{2,1,0:T(8,128)(2,1)S(1)} %collective-permute-done.3.refs_9_), channel_id=1, source_target_pairs={{0,4},{4,0},{8,12},{12,8},{16,20},{20,16},{24,28},{28,24},{1,5},{5... | collective-permute-start | bytes 196616 | tf_op jit(solution)/shard_map/ppermute | solution.py:34
  38.2 1.3 %collective-permute-start.10 = (bf16[2,128,128]{2,1,0:T(8,128)(2,1)S(1)}, bf16[2,128,128]{2,1,0:T(8,128)(2,1)S(1)}, u32[]{:S(2)}, u32[]{:S(2)}) collective-permute-start(bf16[2,128,128]{2,1,0:T(8,128)(2,1)S(1)} %collective-permute-done.5.refs_10_), channel_id=1, source_target_pairs={{0,4},{4,0},{8,12},{12,8},{16,20},{20,16},{24,28},{28,24},{1,5},{5... | collective-permute-start | bytes 196616 | tf_op jit(solution)/shard_map/ppermute | solution.py:34
  38.8 1.3 %collective-permute-start.11 = (bf16[2,128,128]{2,1,0:T(8,128)(2,1)S(1)}, bf16[2,128,128]{2,1,0:T(8,128)(2,1)S(1)}, u32[]{:S(2)}, u32[]{:S(2)}) collective-permute-start(bf16[2,128,128]{2,1,0:T(8,128)(2,1)S(1)} %collective-permute-done.7.refs_11_), channel_id=1, source_target_pairs={{0,4},{4,0},{8,12},{12,8},{16,20},{20,16},{24,28},{28,24},{1,5},{5... | collective-permute-start | bytes 196616 | tf_op jit(solution)/shard_map/ppermute | solution.py:34
  53.3 18.6 %copy-start.4 = (bf16[2,128,128]{2,1,0:T(8,128)(2,1)}, bf16[2,128,128]{2,1,0:T(8,128)(2,1)S(1)}, u32[]{:S(2)}) copy-start(bf16[2,128,128]{2,1,0:T(8,128)(2,1)S(1)} %get-tuple-element.25.refs_3_) | copy-start | bytes 196612
  53.3 9.6 %collective-permute-start.13 = (bf16[2,128,128]{2,1,0:T(8,128)(2,1)S(1)}, bf16[2,128,128]{2,1,0:T(8,128)(2,1)S(1)}, u32[]{:S(2)}, u32[]{:S(2)}) collective-permute-start(bf16[2,128,128]{2,1,0:T(8,128)(2,1)S(1)} %get-tuple-element.26), channel_id=1, source_target_pairs={{0,8},{4,12},{8,16},{12,20},{16,24},{20,28},{24,0},{28,4},{1,9},{5... | collective-permute-start | bytes 196616 | tf_op jit(solution)/shard_map/ppermute | solution.py:29
  54.7 12.2 %collective-permute-start.15 = (bf16[2,128,128]{2,1,0:T(8,128)(2,1)S(1)}, bf16[2,128,128]{2,1,0:T(8,128)(2,1)S(1)}, u32[]{:S(2)}, u32[]{:S(2)}) collective-permute-start(bf16[2,128,128]{2,1,0:T(8,128)(2,1)S(1)} %get-tuple-element.27), channel_id=1, source_target_pairs={{0,16},{4,20},{8,24},{12,28},{16,0},{20,4},{24,8},{28,12},{1,17},{... | collective-permute-start | bytes 196616 | tf_op jit(solution)/shard_map/ppermute | solution.py:29
  58.0 11.2 %collective-permute-start.17 = (bf16[2,128,128]{2,1,0:T(8,128)(2,1)S(1)}, bf16[2,128,128]{2,1,0:T(8,128)(2,1)S(1)}, u32[]{:S(2)}, u32[]{:S(2)}) collective-permute-start(bf16[2,128,128]{2,1,0:T(8,128)(2,1)S(1)} %get-tuple-element.28), channel_id=1, source_target_pairs={{0,24},{4,28},{8,0},{12,4},{16,8},{20,12},{24,16},{28,20},{1,25},{... | collective-permute-start | bytes 196616 | tf_op jit(solution)/shard_map/ppermute | solution.py:29
  58.0 15.9 %collective-permute-start.12 = (bf16[2,128,128]{2,1,0:T(8,128)(2,1)S(1)}, bf16[2,128,128]{2,1,0:T(8,128)(2,1)S(1)}, u32[]{:S(2)}, u32[]{:S(2)}) collective-permute-start(bf16[2,128,128]{2,1,0:T(8,128)(2,1)S(1)} %get-tuple-element.25.refs_3_), channel_id=1, source_target_pairs={{0,1},{1,2},{2,3},{4,5},{5,6},{6,7},{8,9},{9,10},{10,11},{12,13},{... | collective-permute-start | bytes 196616 | tf_op jit(solution)/shard_map/ppermute | solution.py:24
  62.9 9.0 %copy-start.10 = (bf16[2,128,128]{2,1,0:T(8,128)(2,1)}, bf16[2,128,128]{2,1,0:T(8,128)(2,1)S(1)}, u32[]{:S(2)}) copy-start(bf16[2,128,128]{2,1,0:T(8,128)(2,1)S(1)} %collective-permute-done.13.refs_4_) | copy-start | bytes 196612
  62.9 11.1 %collective-permute-start.14 = (bf16[2,128,128]{2,1,0:T(8,128)(2,1)S(1)}, bf16[2,128,128]{2,1,0:T(8,128)(2,1)S(1)}, u32[]{:S(2)}, u32[]{:S(2)}) collective-permute-start(bf16[2,128,128]{2,1,0:T(8,128)(2,1)S(1)} %collective-permute-done.13.refs_4_), channel_id=1, source_target_pairs={{0,1},{1,2},{2,3},{4,5},{5,6},{6,7},{8,9},{9,10},{10,11},{12,13},{... | collective-permute-start | bytes 196616 | tf_op jit(solution)/shard_map/ppermute | solution.py:24
  66.9 7.1 %collective-permute-start.16 = (bf16[2,128,128]{2,1,0:T(8,128)(2,1)S(1)}, bf16[2,128,128]{2,1,0:T(8,128)(2,1)S(1)}, u32[]{:S(2)}, u32[]{:S(2)}) collective-permute-start(bf16[2,128,128]{2,1,0:T(8,128)(2,1)S(1)} %collective-permute-done.15.refs_5_), channel_id=1, source_target_pairs={{0,1},{1,2},{2,3},{4,5},{5,6},{6,7},{8,9},{9,10},{10,11},{12,13},{... | collective-permute-start | bytes 196616 | tf_op jit(solution)/shard_map/ppermute | solution.py:24
  69.2 4.7 %collective-permute-start.18 = (bf16[2,128,128]{2,1,0:T(8,128)(2,1)S(1)}, bf16[2,128,128]{2,1,0:T(8,128)(2,1)S(1)}, u32[]{:S(2)}, u32[]{:S(2)}) collective-permute-start(bf16[2,128,128]{2,1,0:T(8,128)(2,1)S(1)} %collective-permute-done.17.refs_6_), channel_id=1, source_target_pairs={{0,1},{1,2},{2,3},{4,5},{5,6},{6,7},{8,9},{9,10},{10,11},{12,13},{... | collective-permute-start | bytes 196616 | tf_op jit(solution)/shard_map/ppermute | solution.py:24
  (14 other events, 41.6 us)

commit v2 on v1

--- a/solution.py
+++ b/solution.py
@@ -16,6 +16,8 @@
 
 VMEM = pl.BlockSpec(memory_space=pltpu.VMEM)
 SMEM = pl.BlockSpec(memory_space=pltpu.SMEM)
+SMALL = pltpu.CompilerParams(vmem_limit_bytes=8 * 2**20)
+LARGE = pltpu.CompilerParams(vmem_limit_bytes=24 * 2**20)
 
 
 def passed_along(block, axis, distance):
@@ -24,9 +26,9 @@
     return lax.ppermute(block, axis, route)
 
 
-def rotated(block, distance):
+def crossed(block, distance):
     size = lax.axis_size("cuts")
-    return lax.ppermute(block, "cuts", [(i, (i + distance) % size) for i in range(size)])
+    return lax.ppermute(block, "cuts", [(i, i ^ (CORES * distance)) for i in range(size)])
 
 
 def swapped(block):
@@ -41,22 +43,23 @@
     return np.block([[cosine, sine], [-sine, cosine]]).astype(np.float32)
 
 
-def rolled_rows(strip_ref, part, row_at, win, rows_mask_from):
-    last = strip_ref.shape[1] // win - 1
-    block = row_at // win
-    upper = strip_ref[part, pl.ds(pl.multiple_of(block * win, win), win), :]
-    after = jnp.minimum(block + 1, last)
-    lower = strip_ref[part, pl.ds(pl.multiple_of(after * win, win), win), :]
-    return jnp.where(rows_mask_from >= row_at - block * win, upper, lower)
-
-
-def rows_kernel(chips, slots, win, chip_ref, rows_ref, strip_ref, *out_refs):
+def merge_kernel(chips, slots, win, ints_ref, rows_ref, cols_ref, own_ref, beside_ref, *out_refs):
     row_ids = lax.broadcasted_iota(jnp.int32, (win, win), 0)
-    for r in range(chips):
-        slot = lax.rem(chip_ref[0] + r, chips) // (chips // slots)
-        row_at = rows_ref[slot]
+    col_ids = lax.broadcasted_iota(jnp.int32, (win, win), 1)
+    last = own_ref.shape[1] // win - 1
+    for p in range(chips):
+        slot = (ints_ref[0] ^ p) // (chips // slots)
+        row_at, col_at = rows_ref[slot], cols_ref[slot]
+        block = row_at // win
+        after = jnp.minimum(block + 1, last)
+        upper = row_ids >= row_at - block * win
+        mine = col_ids >= col_at
         for part in range(2):
-            out_refs[r][part] = rolled_rows(strip_ref, part, row_at, win, row_ids).astype(BF16)
+            at = pl.ds(pl.multiple_of(block * win, win), win)
+            first = jnp.where(mine, own_ref[part, at, :].astype(F32), beside_ref[part, at, :].astype(F32))
+            at = pl.ds(pl.multiple_of(after * win, win), win)
+            second = jnp.where(mine, own_ref[part, at, :].astype(F32), beside_ref[part, at, :].astype(F32))
+            out_refs[p][part] = jnp.where(upper, first, second).astype(BF16)
 
 
 def rolled_probe_kernel(win, place_ref, probe_ref, out_ref):
@@ -76,10 +79,10 @@
     patch_ref, wave_ref, grad_ref = refs[8 + 3 * chips :]
     chip, core = ints_ref[0], ints_ref[1]
     unit = 1.0 / (ENTRY_SCALE * ENTRY_SCALE * win)
-    for r in range(chips):
-        source = lax.rem(chip - r + chips, chips)
-        patch_ref[CORES * source + core] = own_refs[r][...]
-        patch_ref[CORES * source + 1 - core] = other_refs[r][...]
+    for p in range(chips):
+        source = chip ^ p
+        patch_ref[CORES * source + core] = own_refs[p][...]
+        patch_ref[CORES * source + 1 - core] = other_refs[p][...]
 
     def from_left(matrix, pairs):
         stacked = jnp.concatenate(
@@ -160,38 +163,38 @@
         return back
 
     lax.fori_loop(0, slices - 1, backward_step, back)
-    for r in range(chips):
-        dest = lax.rem(chip + r, chips)
-        out_refs[r][...] = grad_ref[CORES * dest + core]
-
-
-def place_kernel(chips, slots, win, from_left, *refs):
+    for p in range(chips):
+        out_refs[p][...] = grad_ref[CORES * (chip ^ p) + core]
+
+
+def place_kernel(chips, slots, win, groups, from_left, *refs):
     chip_ref, rows_ref, cols_ref = refs[:3]
-    block_refs = refs[3 : 3 + chips]
+    block_refs = refs[3 : 3 + len(groups)]
     out_ref = refs[-1]
     if from_left:
-        out_ref[...] = refs[3 + chips][...]
+        out_ref[...] = refs[3 + len(groups)][...]
     else:
         out_ref[...] = jnp.zeros_like(out_ref)
     row_ids = lax.broadcasted_iota(jnp.int32, (win, win), 0)
     col_ids = lax.broadcasted_iota(jnp.int32, (win, win), 1)
     last = out_ref.shape[1] // win - 1
     copies = chips // slots
-    for r in range(chips):
-        source = lax.rem(chip_ref[0] - r + chips, chips)
-        slot = source // copies
-        row_at, col_at = rows_ref[slot], cols_ref[slot]
-        mine = (col_ids < col_at) if from_left else (col_ids >= col_at)
-        counted = lax.rem(source, copies) == 0
-        block = row_at // win
-        after = jnp.minimum(block + 1, last)
-        upper = row_ids >= row_at - block * win
-        for part in range(2):
-            grad = jnp.where(mine & counted, block_refs[r][part].astype(F32), 0.0)
-            at = pl.ds(pl.multiple_of(block * win, win), win)
-            out_ref[part, at, :] = out_ref[part, at, :] + jnp.where(upper, grad, 0.0)
-            at = pl.ds(pl.multiple_of(after * win, win), win)
-            out_ref[part, at, :] = out_ref[part, at, :] + jnp.where(upper, 0.0, grad)
+    for block_ref, group in zip(block_refs, groups):
+        for place, p in enumerate(group):
+            source = chip_ref[0] ^ p
+            slot = source // copies
+            row_at, col_at = rows_ref[slot], cols_ref[slot]
+            mine = (col_ids < col_at) if from_left else (col_ids >= col_at)
+            counted = lax.rem(source, copies) == 0
+            block = row_at // win
+            after = jnp.minimum(block + 1, last)
+            upper = row_ids >= row_at - block * win
+            for part in range(2):
+                grad = jnp.where(mine & counted, block_ref[2 * place + part].astype(F32), 0.0)
+                at = pl.ds(pl.multiple_of(block * win, win), win)
+                out_ref[part, at, :] = out_ref[part, at, :] + jnp.where(upper, grad, 0.0)
+                at = pl.ds(pl.multiple_of(after * win, win), win)
+                out_ref[part, at, :] = out_ref[part, at, :] + jnp.where(upper, 0.0, grad)
 
 
 def local(object_slices, probe_modes, prop_phase, measured, row_offsets, col_offsets, counts):
@@ -199,23 +202,16 @@
     slots = row_offsets.shape[0]
     chips = lax.axis_size("cuts") // CORES
     copies = chips // slots
-    assert chips % slots == 0
+    assert chips % slots == 0 and chips & (chips - 1) == 0
     section = lax.axis_index("cuts")
     chip, core = section // CORES, section % CORES
     strip = object_slices[0]
     block = jax.ShapeDtypeStruct((2, win, win), BF16)
-
-    left_places = passed_along(jnp.concatenate([row_offsets, col_offsets]), "tile", 1)
-    left_rows, left_cols = left_places[:slots], left_places[slots:]
-    chip_one = jnp.reshape(chip, (1,)).astype(jnp.int32)
-
-    select_rows = pl.pallas_call(
-        functools.partial(rows_kernel, chips, slots, win),
-        out_shape=[block] * chips,
-        in_specs=[SMEM, SMEM, VMEM],
-        out_specs=[VMEM] * chips,
-    )
-    own_rows = select_rows(chip_one, row_offsets, strip)
+    order = sorted(range(1, chips), reverse=True)
+
+    own_strip = strip.astype(BF16)
+    beside = passed_along(own_strip, "tile", -1)
+    ints = jnp.stack([chip, core]).astype(jnp.int32)
     slot = chip // copies
     place = jnp.stack([row_offsets[slot], col_offsets[slot]])
     probe = pl.pallas_call(
@@ -223,6 +219,7 @@
         out_shape=jax.ShapeDtypeStruct(probe_modes.shape, BF16),
         in_specs=[SMEM, VMEM],
         out_specs=VMEM,
+        compiler_params=SMALL,
     )(place, probe_modes)
     matrix = dft_blocks(win)
     left_matrix = jnp.asarray(matrix, BF16)
@@ -232,17 +229,25 @@
     hsin = jnp.sin(prop_phase) * (unit * unit)
     target = lax.dynamic_index_in_dim(measured, slot, 0, keepdims=False)
     weight = (slot < counts).astype(F32)
-    ints = jnp.stack([chip, core]).astype(jnp.int32)
-
-    beside_rows = select_rows(chip_one, left_rows, strip)
-    own_blocks, other_blocks = [None] * chips, [None] * chips
-    col_ids = lax.broadcasted_iota(jnp.int32, (2, win, win), 2)
-    for r in list(range(1, chips)) + [0]:
-        arrived = passed_along(beside_rows[r], "tile", -1)
-        col_at = col_offsets[(chip + r) % chips // copies]
-        merged = jnp.where(col_ids >= col_at, own_rows[r], arrived)
-        own_blocks[r] = rotated(merged, CORES * r) if r else merged
-        other_blocks[r] = swapped(own_blocks[r])
+
+    places = jnp.concatenate([row_offsets, col_offsets])
+    probe, hcos, hsin, target, weight, places = lax.optimization_barrier(
+        (probe, hcos, hsin, target, weight, places)
+    )
+    left_places = passed_along(places, "tile", 1)
+    beside, left_places = lax.optimization_barrier((beside, left_places))
+    left_rows, left_cols = left_places[:slots], left_places[slots:]
+    merged = pl.pallas_call(
+        functools.partial(merge_kernel, chips, slots, win),
+        out_shape=[block] * chips,
+        in_specs=[SMEM, SMEM, SMEM, VMEM, VMEM],
+        out_specs=[VMEM] * chips,
+        compiler_params=SMALL,
+    )(ints, row_offsets, col_offsets, own_strip, beside)
+    own_blocks = [merged[0]] + [None] * (chips - 1)
+    for p in order:
+        own_blocks[p] = crossed(merged[p], p)
+    other_blocks = [swapped(own_block) for own_block in own_blocks]
 
     grads = pl.pallas_call(
         functools.partial(window_kernel, chips, modes, win),
@@ -254,26 +259,30 @@
             pltpu.VMEM((CORES * chips, modes, 2, win, win), F32),
             pltpu.VMEM((CORES * chips, 2, win, win), BF16),
         ],
-        compiler_params=pltpu.CompilerParams(vmem_limit_bytes=48 * 2**20),
+        compiler_params=LARGE,
     )(ints, weight, left_matrix, right_matrix, probe, hcos, hsin, target, *own_blocks, *other_blocks)
 
-    mine, wrapped = [], []
-    for r in range(chips):
-        arrived = rotated(grads[r], CORES * r) if r else grads[r]
-        mine.append(arrived)
-        wrapped.append(passed_along(arrived, "tile", 1))
-
-    def placed(from_left, rows, cols, *arrays):
+    mine = [grads[0]] + [None] * (chips - 1)
+    for p in order:
+        mine[p] = crossed(grads[p], p)
+    early, late = order[: (chips + 1) // 2], order[(chips + 1) // 2 :]
+    groups = [[0], early, late]
+    wrapped = [
+        passed_along(jnp.concatenate([mine[p] for p in group], 0), "tile", 1) for group in groups
+    ]
+
+    def placed(groups, from_left, rows, cols, *arrays):
         return pl.pallas_call(
-            functools.partial(place_kernel, chips, slots, win, from_left),
+            functools.partial(place_kernel, chips, slots, win, groups, from_left),
             out_shape=jax.ShapeDtypeStruct(strip.shape, F32),
             in_specs=[SMEM, SMEM, SMEM] + [VMEM] * len(arrays),
             out_specs=VMEM,
-            input_output_aliases={3 + chips: 0} if from_left else {},
-        )(chip_one, rows, cols, *arrays)
-
-    own_part = placed(False, row_offsets, col_offsets, *mine)
-    return placed(True, left_rows, left_cols, *wrapped, own_part)[None]
+            input_output_aliases={3 + len(groups): 0} if from_left else {},
+            compiler_params=SMALL,
+        )(ints, rows, cols, *arrays)
+
+    own_part = placed([[p] for p in range(chips)], False, row_offsets, col_offsets, *mine)
+    return placed(groups, True, left_rows, left_cols, *wrapped, own_part)[None]
 
 
 def solution(mesh):

time: 77.6 us -> 62.5 us (0.81)
  starting transfers between devices: 36 us -> 28.4 us
  Pallas kernels: 23.3 us -> 18.3 us
  waiting for transfers between devices: 6.14 us -> 9.56 us
  local copies, waits for them, and re-layouts: 4.81 us -> 2.08 us
  other arithmetic: 5.66 us -> 2.96 us
    ppermute x6, waiting for transfers between devices: 1.31 us -> 6.09 us  [crossed(): lax.ppermute(block, 'cuts', [(i, i ^ CORES * distance) for i in range(siz...]
    ppermute x9 -> x5, starting transfers between devices: 23.7 us -> 19.5 us  [passed_along(): return lax.ppermute(block, axis, route)]
    pallas_call x4 -> x3, Pallas kernels: 8.21 us -> 4.54 us  [the longest x2 3.83 us: placed(): pl.pallas_call(functools.partial(place_kernel, chips, slots, win, groups,...]
    ppermute x6, starting transfers between devices: 11.7 us -> 8.93 us  [crossed(): lax.ppermute(block, 'cuts', [(i, i ^ CORES * distance) for i in range(siz...]
    ge x4 -> x0, other arithmetic: 2.61 us -> none  [local(): merged = jnp.where(col_ids >= col_at, own_rows[r], arrived)]
    unnamed x38 -> x14, local copies, waits for them, and re-layouts: 2.82 us -> 0.83 us
    ppermute x9 -> x5, waiting for transfers between devices: 3.65 us -> 2.23 us  [passed_along(): return lax.ppermute(block, axis, route)]
    convert_element_type x0 -> x1, other arithmetic: none -> 1.26 us  [local(): own_strip = strip.astype(BF16)]
  transfers between devices with their start and end apart: 19 -> 15, of which waited for: 6 -> 8; matrix products, arithmetic and copies ran while one was open for 8% -> 5% of each run, Pallas kernels for 8% -> 4%
where the time goes in v2:
time: 62.5 us; the launch traced here: 62.1 us
  starting transfers between devices  28.4 us (45%)
  Pallas kernels  18.3 us (29%)
  waiting for transfers between devices  9.56 us (15%)
  other arithmetic  2.96 us (5%)
  local copies, waits for them, and re-layouts  2.08 us (3%)
  between operations  0.83 us (1%)
    ppermute x5, starting transfers between devices, passed_along(): return lax.ppermute(block, axis, route)  19.5 us
    pallas_call x1, Pallas kernels, local(): pl.pallas_call(functools.partial(window_kernel, chips, modes, win), out_s...  13 us
    ppermute x6, starting transfers between devices, crossed(): lax.ppermute(block, 'cuts', [(i, i ^ CORES * distance) for i in range(siz...  8.93 us
    ppermute x6, waiting for transfers between devices, crossed(): lax.ppermute(block, 'cuts', [(i, i ^ CORES * distance) for i in range(siz...  6.09 us
    pallas_call x2, Pallas kernels, placed(): pl.pallas_call(functools.partial(place_kernel, chips, slots, win, groups,...  3.83 us
    ppermute x5, waiting for transfers between devices, passed_along(): return lax.ppermute(block, axis, route)  2.23 us
    another operation x1, other arithmetic, local(): place = jnp.stack([row_offsets[slot], col_offsets[slot]])  1.29 us
    convert_element_type x1, other arithmetic, local(): own_strip = strip.astype(BF16)  1.26 us
  transfers between devices with their start and end apart: 15, of which 8 were waited for; matrix products, arithmetic and copies ran while one was open for 5% of the time, Pallas kernels for 4%

profile of v2, /device:TPU:0, one launch (start us, length us, event | category | flops | bytes accessed | tf_op | source)
XLA Modules:
  0.0 62.1 jit_solution(103213368623175387)
XLA Ops:
  0.0 1.3 %convert_bitcast_fusion.own_ref = bf16[2,768,128]{2,1,0:T(8,128)(2,1)S(1)} fusion(f32[1,2,768,128]{3,2,1,0:T(8,128)} %param.9), kind=kLoop, calls=%fused_computation | loop fusion | flops 196608 | bytes 1179648 | tf_op jit(solution)/shard_map/convert_element_type | solution.py:212
  1.3 1.3 %collective-permute-start = (bf16[2,768,128]{2,1,0:T(8,128)(2,1)S(1)}, bf16[2,768,128]{2,1,0:T(8,128)(2,1)S(1)}, u32[]{:S(2)}, u32[]{:S(2)}) collective-permute-start(bf16[2,768,128]{2,1,0:T(8,128)(2,1)S(1)} %convert_bitcast_fusion.own_ref), channel_id=1, source_target_pairs={{1,0},{2,1},{3,2},{5,4},{6,5},{7,6},{9,8},{10,9},{11,10},{13,12},{... | collective-permute-start | bytes 1179656 | tf_op jit(solution)/shard_map/ppermute | solution.py:26
  2.6 0.6 %copy-done.4 = s32[4]{0:T(128)S(1)} copy-done((s32[4]{0:T(128)S(1)}, s32[4]{0:T(128)}, u32[]{:S(2)}) %copy-start.4) | copy-done | bytes 40
  3.2 0.6 dynamic_slice.11
  3.9 0.6 dynamic_slice.10
  4.6 1.3 %pad_add_fusion.1.place_ref = s32[2]{0:T(128)S(1)} fusion(s32[1]{0:T(128)} %dynamic_slice.11, s32[1]{0:T(128)} %dynamic_slice.10), kind=kLoop, calls=%fused_computation.6 | loop fusion | flops 2 | bytes 16 | tf_op jit(solution)/shard_map/stack | solution.py:216
  6.5 0.7 %shard_map.91.refs_4_ = bf16[4,2,128,128]{3,2,1,0:T(8,128)(2,1)S(1)} custom-call(s32[2]{0:T(128)S(1)} %pad_add_fusion.1.place_ref, f32[4,2,128,128]{3,2,1,0:T(8,128)S(1)} %copy-done.1), custom_call_target="tpu_custom_call" | custom-call | tf_op jit(solution)/shard_map/pallas_call | solution.py:217
  7.6 5.5 %collective-permute-start.1 = (s32[8]{0:T(128)S(1)}, s32[8]{0:T(128)S(1)}, u32[]{:S(2)}, u32[]{:S(2)}) collective-permute-start(s32[8]{0:T(128)S(1)} %pad_add_fusion.2), channel_id=1, source_target_pairs={{0,1},{1,2},{2,3},{4,5},{5,6},{6,7},{8,9},{9,10},{10,11},{12,13},{... | collective-permute-start | bytes 104 | tf_op jit(solution)/shard_map/ppermute | solution.py:26
  13.2 1.2 %collective-permute-done.1 = s32[8]{0:T(128)S(1)} collective-permute-done((s32[8]{0:T(128)S(1)}, s32[8]{0:T(128)S(1)}, u32[]{:S(2)}, u32[]{:S(2)}) %collective-permute-start.1) | collective-permute-done | bytes 64 | tf_op jit(solution)/shard_map/ppermute | solution.py:26
  14.4 0.8 %collective-permute-done.beside_ref = bf16[2,768,128]{2,1,0:T(8,128)(2,1)S(1)} collective-permute-done((bf16[2,768,128]{2,1,0:T(8,128)(2,1)S(1)}, bf16[2,768,128]{2,1,0:T(8,128)(2,1)S(1)}, u32[]{:S(2)}, u32[]{:S(2)}) %collective-permute-start) | collective-permute-done | bytes 393248 | tf_op jit(solution)/shard_map/ppermute | solution.py:26
  15.2 0.7 %shard_map.92 = (bf16[2,128,128]{2,1,0:T(8,128)(2,1)S(1)}, bf16[2,128,128]{2,1,0:T(8,128)(2,1)S(1)}, bf16[2,128,128]{2,1,0:T(8,128)(2,1)S(1)}, bf16[2,128,128]{2,1,0:T(8,128)(2,1)S(1)}) custom-call(s32[2]{0:T(128)S(1)} %pad_add_fusion.ints_ref.refs_0_, s32[4]{0:T(128)S(1)} %copy-done.5, s32[4]{0:T(128)S(1)} %copy-done.4, ...), custom_call_target="tpu_custom_call" | custom-call | tf_op jit(solution)/shard_map/pallas_call | solution.py:240
  15.9 1.9 %collective-permute-start.2 = (bf16[2,128,128]{2,1,0:T(8,128)(2,1)S(1)}, bf16[2,128,128]{2,1,0:T(8,128)(2,1)S(1)}, u32[]{:S(2)}, u32[]{:S(2)}) collective-permute-start(bf16[2,128,128]{2,1,0:T(8,128)(2,1)S(1)} %get-tuple-element.30), channel_id=1, source_target_pairs={{0,8},{4,12},{8,0},{12,4},{16,24},{20,28},{24,16},{28,20},{1,9},{5... | collective-permute-start | bytes 196616 | tf_op jit(solution)/shard_map/ppermute | solution.py:31
  17.8 2.6 %collective-permute-start.3 = (bf16[2,128,128]{2,1,0:T(8,128)(2,1)S(1)}, bf16[2,128,128]{2,1,0:T(8,128)(2,1)S(1)}, u32[]{:S(2)}, u32[]{:S(2)}) collective-permute-start(bf16[2,128,128]{2,1,0:T(8,128)(2,1)S(1)} %get-tuple-element.31), channel_id=1, source_target_pairs={{0,16},{4,20},{8,24},{12,28},{16,0},{20,4},{24,8},{28,12},{1,17},{... | collective-permute-start | bytes 196616 | tf_op jit(solution)/shard_map/ppermute | solution.py:31
  20.9 3.5 %collective-permute-done.3.refs_10_ = bf16[2,128,128]{2,1,0:T(8,128)(2,1)S(1)} collective-permute-done((bf16[2,128,128]{2,1,0:T(8,128)(2,1)S(1)}, bf16[2,128,128]{2,1,0:T(8,128)(2,1)S(1)}, u32[]{:S(2)}, u32[]{:S(2)}) %collective-permute-start.3) | collective-permute-done | bytes 65568 | tf_op jit(solution)/shard_map/ppermute | solution.py:31
  24.4 2.1 %collective-permute-done.4.refs_11_ = bf16[2,128,128]{2,1,0:T(8,128)(2,1)S(1)} collective-permute-done((bf16[2,128,128]{2,1,0:T(8,128)(2,1)S(1)}, bf16[2,128,128]{2,1,0:T(8,128)(2,1)S(1)}, u32[]{:S(2)}, u32[]{:S(2)}) %collective-permute-start.4) | collective-permute-done | bytes 65568 | tf_op jit(solution)/shard_map/ppermute | solution.py:31
  26.5 1.2 %collective-permute-done.8.refs_15_ = bf16[2,128,128]{2,1,0:T(8,128)(2,1)S(1)} collective-permute-done((bf16[2,128,128]{2,1,0:T(8,128)(2,1)S(1)}, bf16[2,128,128]{2,1,0:T(8,128)(2,1)S(1)}, u32[]{:S(2)}, u32[]{:S(2)}) %collective-permute-start.8) | collective-permute-done | bytes 65568 | tf_op jit(solution)/shard_map/ppermute | solution.py:36
  27.7 13.0 %shard_map.93 = (bf16[2,128,128]{2,1,0:T(8,128)(2,1)S(1)}, bf16[2,128,128]{2,1,0:T(8,128)(2,1)S(1)}, bf16[2,128,128]{2,1,0:T(8,128)(2,1)S(1)}, bf16[2,128,128]{2,1,0:T(8,128)(2,1)S(1)}) custom-call(s32[2]{0:T(128)S(1)} %pad_add_fusion.ints_ref.refs_0_, f32[1]{0:T(128)S(6)} %convert_element_type.10.refs_1_, bf16[256,256]{1,0:T(8,128)(2,1)S(1)} %copy-done.3, ...), custom_call_target="tpu_custom_call" | custom-call | tf_op jit(solution)/shard_map/pallas_call | solution.py:252
  40.8 1.1 %collective-permute-start.10 = (bf16[2,128,128]{2,1,0:T(8,128)(2,1)S(1)}, bf16[2,128,128]{2,1,0:T(8,128)(2,1)S(1)}, u32[]{:S(2)}, u32[]{:S(2)}) collective-permute-start(bf16[2,128,128]{2,1,0:T(8,128)(2,1)S(1)} %get-tuple-element.34), channel_id=1, source_target_pairs={{0,24},{4,28},{8,16},{12,20},{16,8},{20,12},{24,0},{28,4},{1,25},{... | collective-permute-start | bytes 196616 | tf_op jit(solution)/shard_map/ppermute | solution.py:31
  41.9 3.3 %collective-permute-start.13 = (bf16[2,128,128]{2,1,0:T(8,128)(2,1)S(1)}, bf16[2,128,128]{2,1,0:T(8,128)(2,1)S(1)}, u32[]{:S(2)}, u32[]{:S(2)}) collective-permute-start(bf16[2,128,128]{2,1,0:T(8,128)(2,1)S(1)} %get-tuple-element.36), channel_id=1, source_target_pairs={{0,8},{4,12},{8,0},{12,4},{16,24},{20,28},{24,16},{28,20},{1,9},{5... | collective-permute-start | bytes 196616 | tf_op jit(solution)/shard_map/ppermute | solution.py:31
  45.2 4.3 %collective-permute-start.9 = (bf16[2,128,128]{2,1,0:T(8,128)(2,1)S(1)}, bf16[2,128,128]{2,1,0:T(8,128)(2,1)S(1)}, u32[]{:S(2)}, u32[]{:S(2)}) collective-permute-start(bf16[2,128,128]{2,1,0:T(8,128)(2,1)S(1)} %get-tuple-element.33.refs_3_), channel_id=1, source_target_pairs={{0,1},{1,2},{2,3},{4,5},{5,6},{6,7},{8,9},{9,10},{10,11},{12,13},{... | collective-permute-start | bytes 196616 | tf_op jit(solution)/shard_map/ppermute | solution.py:26
  49.6 4.4 %collective-permute-start.12 = (bf16[4,128,128]{2,1,0:T(8,128)(2,1)S(1)}, bf16[4,128,128]{2,1,0:T(8,128)(2,1)S(1)}, u32[]{:S(2)}, u32[]{:S(2)}) collective-permute-start(bf16[4,128,128]{2,1,0:T(8,128)(2,1)S(1)} %pad_maximum_fusion), channel_id=1, source_target_pairs={{0,1},{1,2},{2,3},{4,5},{5,6},{6,7},{8,9},{9,10},{10,11},{12,13},{... | collective-permute-start | bytes 393224 | tf_op jit(solution)/shard_map/ppermute | solution.py:26
  54.1 4.0 %collective-permute-start.14 = (bf16[2,128,128]{2,1,0:T(8,128)(2,1)S(1)}, bf16[2,128,128]{2,1,0:T(8,128)(2,1)S(1)}, u32[]{:S(2)}, u32[]{:S(2)}) collective-permute-start(bf16[2,128,128]{2,1,0:T(8,128)(2,1)S(1)} %collective-permute-done.13.refs_4_), channel_id=1, source_target_pairs={{0,1},{1,2},{2,3},{4,5},{5,6},{6,7},{8,9},{9,10},{10,11},{12,13},{... | collective-permute-start | bytes 196616 | tf_op jit(solution)/shard_map/ppermute | solution.py:26
  58.1 1.6 %shard_map.94.refs_6_ = f32[2,768,128]{2,1,0:T(8,128)} custom-call(s32[2]{0:T(128)S(1)} %pad_add_fusion.ints_ref.refs_0_, s32[4]{0:T(128)S(1)} %copy-done.5, s32[4]{0:T(128)S(1)} %copy-done.4, bf16[2,128,128]{2,1,0:T(8,128)(2,1)S(1)} %get-tuple-element.33.refs_3_, bf16[2,128,128]{2,1,0:T(8,128)(2,1)S(1)} %collective-permute-done.13.refs_4_, ...), custom_call_target="tpu_custom_call" | custom-call | tf_op jit(solution)/shard_map/pallas_call | solution.py:275
  59.9 2.2 %shard_map.95 = f32[2,768,128]{2,1,0:T(8,128)} custom-call(s32[2]{0:T(128)S(1)} %pad_add_fusion.ints_ref.refs_0_, s32[4]{0:T(128)S(1)} %get-tuple-element.40.refs_1_, s32[4]{0:T(128)S(1)} %get-tuple-element.39.refs_2_, bf16[2,128,128]{2,1,0:T(8,128)(2,1)S(1)} %collective-permute-done.9.refs_3_, ...), custom_call_target="tpu_custom_call", output_to_operand_aliasing={{}: (6, {})} | custom-call | tf_op jit(solution)/shard_map/pallas_call | solution.py:275
  (35 shorter events, 1.5 us)
Async XLA Ops:
  0.0 4.6 %copy-start = (f32[4,128,128]{2,1,0:T(8,128)S(1)}, f32[4,128,128]{2,1,0:T(8,128)}, u32[]{:S(2)}) copy-start(f32[4,128,128]{2,1,0:T(8,128)} %param.12) | copy-start | bytes 786436
  0.0 6.5 %copy-start.1 = (f32[4,2,128,128]{3,2,1,0:T(8,128)S(1)}, f32[4,2,128,128]{3,2,1,0:T(8,128)}, u32[]{:S(2)}) copy-start(f32[4,2,128,128]{3,2,1,0:T(8,128)} %probe_ref.1) | copy-start | bytes 1572868
  1.3 14.0 %collective-permute-start = (bf16[2,768,128]{2,1,0:T(8,128)(2,1)S(1)}, bf16[2,768,128]{2,1,0:T(8,128)(2,1)S(1)}, u32[]{:S(2)}, u32[]{:S(2)}) collective-permute-start(bf16[2,768,128]{2,1,0:T(8,128)(2,1)S(1)} %convert_bitcast_fusion.own_ref), channel_id=1, source_target_pairs={{1,0},{2,1},{3,2},{5,4},{6,5},{7,6},{9,8},{10,9},{11,10},{13,12},{... | collective-permute-start | bytes 1179656 | tf_op jit(solution)/shard_map/ppermute | solution.py:26
  2.6 0.7 %copy-start.4 = (s32[4]{0:T(128)S(1)}, s32[4]{0:T(128)}, u32[]{:S(2)}) copy-start(s32[4]{0:T(128)} %refs_2_.2) | copy-start | bytes 52
  3.2 0.7 %copy-start.5 = (s32[4]{0:T(128)S(1)}, s32[4]{0:T(128)}, u32[]{:S(2)}) copy-start(s32[4]{0:T(128)} %refs_1_.1) | copy-start | bytes 52
  6.5 0.8 %copy-start.6 = (f32[128,128]{1,0:T(8,128)S(1)}, f32[128,128]{1,0:T(8,128)}, u32[]{:S(2)}) copy-start(f32[128,128]{1,0:T(8,128)} %param.11) | copy-start | bytes 196612
  7.6 6.8 %collective-permute-start.1 = (s32[8]{0:T(128)S(1)}, s32[8]{0:T(128)S(1)}, u32[]{:S(2)}, u32[]{:S(2)}) collective-permute-start(s32[8]{0:T(128)S(1)} %pad_add_fusion.2), channel_id=1, source_target_pairs={{0,1},{1,2},{2,3},{4,5},{5,6},{6,7},{8,9},{9,10},{10,11},{12,13},{... | collective-permute-start | bytes 104 | tf_op jit(solution)/shard_map/ppermute | solution.py:26
  13.2 14.5 %copy-start.2 = (bf16[256,256]{1,0:T(8,128)(2,1)S(1)}, bf16[256,256]{1,0:T(8,128)(2,1)}, u32[]{:S(2)}) copy-start(bf16[256,256]{1,0:T(8,128)(2,1)} %constant.53.clone.refs_3_) | copy-start | bytes 393220
  13.2 14.5 %copy-start.3 = (bf16[256,256]{1,0:T(8,128)(2,1)S(1)}, bf16[256,256]{1,0:T(8,128)(2,1)}, u32[]{:S(2)}) copy-start(bf16[256,256]{1,0:T(8,128)(2,1)} %constant.52.clone.refs_2_) | copy-start | bytes 393220
  15.9 5.0 %collective-permute-start.2 = (bf16[2,128,128]{2,1,0:T(8,128)(2,1)S(1)}, bf16[2,128,128]{2,1,0:T(8,128)(2,1)S(1)}, u32[]{:S(2)}, u32[]{:S(2)}) collective-permute-start(bf16[2,128,128]{2,1,0:T(8,128)(2,1)S(1)} %get-tuple-element.30), channel_id=1, source_target_pairs={{0,8},{4,12},{8,0},{12,4},{16,24},{20,28},{24,16},{28,20},{1,9},{5... | collective-permute-start | bytes 196616 | tf_op jit(solution)/shard_map/ppermute | solution.py:31
  17.8 6.6 %collective-permute-start.3 = (bf16[2,128,128]{2,1,0:T(8,128)(2,1)S(1)}, bf16[2,128,128]{2,1,0:T(8,128)(2,1)S(1)}, u32[]{:S(2)}, u32[]{:S(2)}) collective-permute-start(bf16[2,128,128]{2,1,0:T(8,128)(2,1)S(1)} %get-tuple-element.31), channel_id=1, source_target_pairs={{0,16},{4,20},{8,24},{12,28},{16,0},{20,4},{24,8},{28,12},{1,17},{... | collective-permute-start | bytes 196616 | tf_op jit(solution)/shard_map/ppermute | solution.py:31
  20.4 6.1 %collective-permute-start.4 = (bf16[2,128,128]{2,1,0:T(8,128)(2,1)S(1)}, bf16[2,128,128]{2,1,0:T(8,128)(2,1)S(1)}, u32[]{:S(2)}, u32[]{:S(2)}) collective-permute-start(bf16[2,128,128]{2,1,0:T(8,128)(2,1)S(1)} %get-tuple-element.32), channel_id=1, source_target_pairs={{0,24},{4,28},{8,16},{12,20},{16,8},{20,12},{24,0},{28,4},{1,25},{... | collective-permute-start | bytes 196616 | tf_op jit(solution)/shard_map/ppermute | solution.py:31
  20.4 6.1 %collective-permute-start.5 = (bf16[2,128,128]{2,1,0:T(8,128)(2,1)S(1)}, bf16[2,128,128]{2,1,0:T(8,128)(2,1)S(1)}, u32[]{:S(2)}, u32[]{:S(2)}) collective-permute-start(bf16[2,128,128]{2,1,0:T(8,128)(2,1)S(1)} %get-tuple-element.29.refs_8_), channel_id=1, source_target_pairs={{0,4},{4,0},{8,12},{12,8},{16,20},{20,16},{24,28},{28,24},{1,5},{5... | collective-permute-start | bytes 196616 | tf_op jit(solution)/shard_map/ppermute | solution.py:36
  20.9 5.6 %collective-permute-start.6 = (bf16[2,128,128]{2,1,0:T(8,128)(2,1)S(1)}, bf16[2,128,128]{2,1,0:T(8,128)(2,1)S(1)}, u32[]{:S(2)}, u32[]{:S(2)}) collective-permute-start(bf16[2,128,128]{2,1,0:T(8,128)(2,1)S(1)} %collective-permute-done.2.refs_9_), channel_id=1, source_target_pairs={{0,4},{4,0},{8,12},{12,8},{16,20},{20,16},{24,28},{28,24},{1,5},{5... | collective-permute-start | bytes 196616 | tf_op jit(solution)/shard_map/ppermute | solution.py:36
  24.4 2.1 %collective-permute-start.7 = (bf16[2,128,128]{2,1,0:T(8,128)(2,1)S(1)}, bf16[2,128,128]{2,1,0:T(8,128)(2,1)S(1)}, u32[]{:S(2)}, u32[]{:S(2)}) collective-permute-start(bf16[2,128,128]{2,1,0:T(8,128)(2,1)S(1)} %collective-permute-done.3.refs_10_), channel_id=1, source_target_pairs={{0,4},{4,0},{8,12},{12,8},{16,20},{20,16},{24,28},{28,24},{1,5},{5... | collective-permute-start | bytes 196616 | tf_op jit(solution)/shard_map/ppermute | solution.py:36
  26.5 1.3 %collective-permute-start.8 = (bf16[2,128,128]{2,1,0:T(8,128)(2,1)S(1)}, bf16[2,128,128]{2,1,0:T(8,128)(2,1)S(1)}, u32[]{:S(2)}, u32[]{:S(2)}) collective-permute-start(bf16[2,128,128]{2,1,0:T(8,128)(2,1)S(1)} %collective-permute-done.4.refs_11_), channel_id=1, source_target_pairs={{0,4},{4,0},{8,12},{12,8},{16,20},{20,16},{24,28},{28,24},{1,5},{5... | collective-permute-start | bytes 196616 | tf_op jit(solution)/shard_map/ppermute | solution.py:36
  40.8 8.8 %collective-permute-start.10 = (bf16[2,128,128]{2,1,0:T(8,128)(2,1)S(1)}, bf16[2,128,128]{2,1,0:T(8,128)(2,1)S(1)}, u32[]{:S(2)}, u32[]{:S(2)}) collective-permute-start(bf16[2,128,128]{2,1,0:T(8,128)(2,1)S(1)} %get-tuple-element.34), channel_id=1, source_target_pairs={{0,24},{4,28},{8,16},{12,20},{16,8},{20,12},{24,0},{28,4},{1,25},{... | collective-permute-start | bytes 196616 | tf_op jit(solution)/shard_map/ppermute | solution.py:31
  41.9 7.7 %collective-permute-start.11 = (bf16[2,128,128]{2,1,0:T(8,128)(2,1)S(1)}, bf16[2,128,128]{2,1,0:T(8,128)(2,1)S(1)}, u32[]{:S(2)}, u32[]{:S(2)}) collective-permute-start(bf16[2,128,128]{2,1,0:T(8,128)(2,1)S(1)} %get-tuple-element.35), channel_id=1, source_target_pairs={{0,16},{4,20},{8,24},{12,28},{16,0},{20,4},{24,8},{28,12},{1,17},{... | collective-permute-start | bytes 196616 | tf_op jit(solution)/shard_map/ppermute | solution.py:31
  41.9 12.1 %collective-permute-start.13 = (bf16[2,128,128]{2,1,0:T(8,128)(2,1)S(1)}, bf16[2,128,128]{2,1,0:T(8,128)(2,1)S(1)}, u32[]{:S(2)}, u32[]{:S(2)}) collective-permute-start(bf16[2,128,128]{2,1,0:T(8,128)(2,1)S(1)} %get-tuple-element.36), channel_id=1, source_target_pairs={{0,8},{4,12},{8,0},{12,4},{16,24},{20,28},{24,16},{28,20},{1,9},{5... | collective-permute-start | bytes 196616 | tf_op jit(solution)/shard_map/ppermute | solution.py:31
  45.2 14.5 %collective-permute-start.9 = (bf16[2,128,128]{2,1,0:T(8,128)(2,1)S(1)}, bf16[2,128,128]{2,1,0:T(8,128)(2,1)S(1)}, u32[]{:S(2)}, u32[]{:S(2)}) collective-permute-start(bf16[2,128,128]{2,1,0:T(8,128)(2,1)S(1)} %get-tuple-element.33.refs_3_), channel_id=1, source_target_pairs={{0,1},{1,2},{2,3},{4,5},{5,6},{6,7},{8,9},{9,10},{10,11},{12,13},{... | collective-permute-start | bytes 196616 | tf_op jit(solution)/shard_map/ppermute | solution.py:26
  49.6 10.3 %collective-permute-start.12 = (bf16[4,128,128]{2,1,0:T(8,128)(2,1)S(1)}, bf16[4,128,128]{2,1,0:T(8,128)(2,1)S(1)}, u32[]{:S(2)}, u32[]{:S(2)}) collective-permute-start(bf16[4,128,128]{2,1,0:T(8,128)(2,1)S(1)} %pad_maximum_fusion), channel_id=1, source_target_pairs={{0,1},{1,2},{2,3},{4,5},{5,6},{6,7},{8,9},{9,10},{10,11},{12,13},{... | collective-permute-start | bytes 393224 | tf_op jit(solution)/shard_map/ppermute | solution.py:26
  54.1 5.9 %collective-permute-start.14 = (bf16[2,128,128]{2,1,0:T(8,128)(2,1)S(1)}, bf16[2,128,128]{2,1,0:T(8,128)(2,1)S(1)}, u32[]{:S(2)}, u32[]{:S(2)}) collective-permute-start(bf16[2,128,128]{2,1,0:T(8,128)(2,1)S(1)} %collective-permute-done.13.refs_4_), channel_id=1, source_target_pairs={{0,1},{1,2},{2,3},{4,5},{5,6},{6,7},{8,9},{9,10},{10,11},{12,13},{... | collective-permute-start | bytes 196616 | tf_op jit(solution)/shard_map/ppermute | solution.py:26

commit v3 on v2

--- a/solution.py
+++ b/solution.py
@@ -20,10 +20,9 @@
 LARGE = pltpu.CompilerParams(vmem_limit_bytes=24 * 2**20)
 
 
-def passed_along(block, axis, distance):
-    devices = range(lax.axis_size(axis))
-    route = [(i - distance, i) for i in devices if i - distance in devices]
-    return lax.ppermute(block, axis, route)
+def passed_round(block, axis, distance):
+    size = lax.axis_size(axis)
+    return lax.ppermute(block, axis, [(i, (i + distance) % size) for i in range(size)])
 
 
 def crossed(block, distance):
@@ -47,6 +46,12 @@
     row_ids = lax.broadcasted_iota(jnp.int32, (win, win), 0)
     col_ids = lax.broadcasted_iota(jnp.int32, (win, win), 1)
     last = own_ref.shape[1] // win - 1
+    inside = ints_ref[2] == 0
+
+    def columns(part, at, mine):
+        beside = jnp.where(inside, beside_ref[part, at, :].astype(F32), 0.0)
+        return jnp.where(mine, own_ref[part, at, :].astype(F32), beside)
+
     for p in range(chips):
         slot = (ints_ref[0] ^ p) // (chips // slots)
         row_at, col_at = rows_ref[slot], cols_ref[slot]
@@ -56,9 +61,9 @@
         mine = col_ids >= col_at
         for part in range(2):
             at = pl.ds(pl.multiple_of(block * win, win), win)
-            first = jnp.where(mine, own_ref[part, at, :].astype(F32), beside_ref[part, at, :].astype(F32))
+            first = columns(part, at, mine)
             at = pl.ds(pl.multiple_of(after * win, win), win)
-            second = jnp.where(mine, own_ref[part, at, :].astype(F32), beside_ref[part, at, :].astype(F32))
+            second = columns(part, at, mine)
             out_refs[p][part] = jnp.where(upper, first, second).astype(BF16)
 
 
@@ -70,19 +75,20 @@
             out_ref[mode, part] = pltpu.roll(block, col_at, 1).astype(BF16)
 
 
-def window_kernel(chips, modes, win, *refs):
+def window_kernel(chips, modes, win, groups, *refs):
     slices = CORES * chips
     (ints_ref, weight_ref, left_ref, right_ref, probe_ref, hcos_ref, hsin_ref, target_ref) = refs[:8]
     own_refs = refs[8 : 8 + chips]
-    other_refs = refs[8 + chips : 8 + 2 * chips]
-    out_refs = refs[8 + 2 * chips : 8 + 3 * chips]
-    patch_ref, wave_ref, grad_ref = refs[8 + 3 * chips :]
+    refs = refs[8 + chips :]
+    other_refs, refs = refs[: len(groups)], refs[len(groups) :]
+    out_refs, (patch_ref, wave_ref, grad_ref) = refs[:chips], refs[chips:]
     chip, core = ints_ref[0], ints_ref[1]
     unit = 1.0 / (ENTRY_SCALE * ENTRY_SCALE * win)
     for p in range(chips):
-        source = chip ^ p
-        patch_ref[CORES * source + core] = own_refs[p][...]
-        patch_ref[CORES * source + 1 - core] = other_refs[p][...]
+        patch_ref[CORES * (chip ^ p) + core] = own_refs[p][...]
+    for other_ref, group in zip(other_refs, groups):
+        for place, p in enumerate(group):
+            patch_ref[CORES * (chip ^ p) + 1 - core] = other_ref[2 * place : 2 * place + 2]
 
     def from_left(matrix, pairs):
         stacked = jnp.concatenate(
@@ -171,8 +177,9 @@
     chip_ref, rows_ref, cols_ref = refs[:3]
     block_refs = refs[3 : 3 + len(groups)]
     out_ref = refs[-1]
+    part = pl.program_id(0)
     if from_left:
-        out_ref[...] = refs[3 + len(groups)][...]
+        out_ref[0] = refs[3 + len(groups)][part]
     else:
         out_ref[...] = jnp.zeros_like(out_ref)
     row_ids = lax.broadcasted_iota(jnp.int32, (win, win), 0)
@@ -189,12 +196,11 @@
             block = row_at // win
             after = jnp.minimum(block + 1, last)
             upper = row_ids >= row_at - block * win
-            for part in range(2):
-                grad = jnp.where(mine & counted, block_ref[2 * place + part].astype(F32), 0.0)
-                at = pl.ds(pl.multiple_of(block * win, win), win)
-                out_ref[part, at, :] = out_ref[part, at, :] + jnp.where(upper, grad, 0.0)
-                at = pl.ds(pl.multiple_of(after * win, win), win)
-                out_ref[part, at, :] = out_ref[part, at, :] + jnp.where(upper, 0.0, grad)
+            grad = jnp.where(mine & counted, block_ref[2 * place + part].astype(F32), 0.0)
+            at = pl.ds(pl.multiple_of(block * win, win), win)
+            out_ref[0, at, :] = out_ref[0, at, :] + jnp.where(upper, grad, 0.0)
+            at = pl.ds(pl.multiple_of(after * win, win), win)
+            out_ref[0, at, :] = out_ref[0, at, :] + jnp.where(upper, 0.0, grad)
 
 
 def local(object_slices, probe_modes, prop_phase, measured, row_offsets, col_offsets, counts):
@@ -208,10 +214,17 @@
     strip = object_slices[0]
     block = jax.ShapeDtypeStruct((2, win, win), BF16)
     order = sorted(range(1, chips), reverse=True)
+    near, far = list(range(chips // 2)), [p for p in order if p >= chips // 2]
+
+    def joined(blocks, group):
+        return jnp.concatenate([blocks[p] for p in group], 0) if len(group) > 1 else blocks[group[0]]
+
 
     own_strip = strip.astype(BF16)
-    beside = passed_along(own_strip, "tile", -1)
-    ints = jnp.stack([chip, core]).astype(jnp.int32)
+    beside = passed_round(own_strip, "tile", -1)
+    tile = lax.axis_index("tile")
+    rightmost = tile == lax.axis_size("tile") - 1
+    ints = jnp.stack([chip, core, rightmost]).astype(jnp.int32)
     slot = chip // copies
     place = jnp.stack([row_offsets[slot], col_offsets[slot]])
     probe = pl.pallas_call(
@@ -230,13 +243,11 @@
     target = lax.dynamic_index_in_dim(measured, slot, 0, keepdims=False)
     weight = (slot < counts).astype(F32)
 
-    places = jnp.concatenate([row_offsets, col_offsets])
-    probe, hcos, hsin, target, weight, places = lax.optimization_barrier(
-        (probe, hcos, hsin, target, weight, places)
+    note = jnp.stack([row_offsets // win, row_offsets % win, col_offsets]).astype(BF16)
+    note = jnp.pad(note, ((0, 16 - 3), (0, win - slots)))
+    beside, probe, hcos, hsin, target, weight, note = lax.optimization_barrier(
+        (beside, probe, hcos, hsin, target, weight, note)
     )
-    left_places = passed_along(places, "tile", 1)
-    beside, left_places = lax.optimization_barrier((beside, left_places))
-    left_rows, left_cols = left_places[:slots], left_places[slots:]
     merged = pl.pallas_call(
         functools.partial(merge_kernel, chips, slots, win),
         out_shape=[block] * chips,
@@ -247,12 +258,13 @@
     own_blocks = [merged[0]] + [None] * (chips - 1)
     for p in order:
         own_blocks[p] = crossed(merged[p], p)
-    other_blocks = [swapped(own_block) for own_block in own_blocks]
+    swaps = [near] + [[p] for p in far]
+    other_blocks = [swapped(joined(own_blocks, group)) for group in swaps]
 
     grads = pl.pallas_call(
-        functools.partial(window_kernel, chips, modes, win),
+        functools.partial(window_kernel, chips, modes, win, swaps),
         out_shape=[block] * chips,
-        in_specs=[SMEM, SMEM] + [VMEM] * (6 + 2 * chips),
+        in_specs=[SMEM, SMEM] + [VMEM] * (6 + chips + len(swaps)),
         out_specs=[VMEM] * chips,
         scratch_shapes=[
             pltpu.VMEM((CORES * chips, 2, win, win), BF16),
@@ -265,19 +277,21 @@
     mine = [grads[0]] + [None] * (chips - 1)
     for p in order:
         mine[p] = crossed(grads[p], p)
-    early, late = order[: (chips + 1) // 2], order[(chips + 1) // 2 :]
-    groups = [[0], early, late]
-    wrapped = [
-        passed_along(jnp.concatenate([mine[p] for p in group], 0), "tile", 1) for group in groups
-    ]
+    size = len(near) * 2 * win
+    first = jnp.concatenate([mine[p].reshape(2 * win, win) for p in near] + [note], 0)
+    first = passed_round(first, "tile", 1)
+    places = first[size : size + 3, :slots].astype(jnp.int32)
+    left_rows, left_cols = places[0] * win + places[1], jnp.where(tile > 0, places[2], 0)
+    groups = [near, far]
+    wrapped = [first[:size].reshape(-1, win, win), passed_round(joined(mine, far), "tile", 1)]
 
     def placed(groups, from_left, rows, cols, *arrays):
         return pl.pallas_call(
             functools.partial(place_kernel, chips, slots, win, groups, from_left),
             out_shape=jax.ShapeDtypeStruct(strip.shape, F32),
+            grid=(2,),
             in_specs=[SMEM, SMEM, SMEM] + [VMEM] * len(arrays),
-            out_specs=VMEM,
-            input_output_aliases={3 + len(groups): 0} if from_left else {},
+            out_specs=pl.BlockSpec((1,) + strip.shape[1:], lambda part: (part, 0, 0)),
             compiler_params=SMALL,
         )(ints, rows, cols, *arrays)
 

time: 62.5 us -> 56.9 us (0.910)
  starting transfers between devices: 28.4 us -> 16.9 us
  waiting for transfers between devices: 9.56 us -> 16.3 us
  Pallas kernels: 18.3 us -> 16.9 us
  local copies, waits for them, and re-layouts: 2.08 us -> 2.76 us
    ppermute x5 -> x3, starting transfers between devices: 19.5 us -> 8.83 us  [passed_round(): lax.ppermute(block, axis, [(i, (i + distance) % size) for i in range(size)])]
    ppermute x5 -> x3, waiting for transfers between devices: 2.23 us -> 5.66 us  [passed_round(): lax.ppermute(block, axis, [(i, (i + distance) % size) for i in range(size)])]
    ppermute x6, waiting for transfers between devices: 6.09 us -> 9.37 us  [crossed(): lax.ppermute(block, 'cuts', [(i, i ^ CORES * distance) for i in range(siz...]
    pallas_call x2, Pallas kernels: 3.83 us -> 2.35 us  [placed(): pl.pallas_call(functools.partial(place_kernel, chips, slots, win, groups,...]
    ppermute x6, starting transfers between devices: 8.93 us -> 8 us  [crossed(): lax.ppermute(block, 'cuts', [(i, i ^ CORES * distance) for i in range(siz...]
    unnamed x14, local copies, waits for them, and re-layouts: 0.83 us -> 1.49 us
    ppermute x4 -> x3, waiting for transfers between devices: 1.24 us -> 1.25 us  [swapped(): return lax.ppermute(block, 'cuts', [(i, i ^ 1) for i in range(size)])]
  transfers between devices with their start and end apart: 15 -> 12, of which waited for: 8 -> 9; matrix products, arithmetic and copies ran while one was open for 5% -> 5% of each run, Pallas kernels for 4% -> 3%
where the time goes in v3:
time: 56.9 us; the launch traced here: 56.7 us
  starting transfers between devices  16.9 us (30%)
  Pallas kernels  16.9 us (30%)
  waiting for transfers between devices  16.3 us (29%)
  other arithmetic  2.99 us (5%)
  local copies, waits for them, and re-layouts  2.76 us (5%)
  between operations  0.82 us (1%)
    pallas_call x1, Pallas kernels, local(): pl.pallas_call(functools.partial(window_kernel, chips, modes, win, swaps)...  13.1 us
    ppermute x6, waiting for transfers between devices, crossed(): lax.ppermute(block, 'cuts', [(i, i ^ CORES * distance) for i in range(siz...  9.37 us
    ppermute x3, starting transfers between devices, passed_round(): lax.ppermute(block, axis, [(i, (i + distance) % size) for i in range(size)])  8.83 us
    ppermute x6, starting transfers between devices, crossed(): lax.ppermute(block, 'cuts', [(i, i ^ CORES * distance) for i in range(siz...  8 us
    ppermute x3, waiting for transfers between devices, passed_round(): lax.ppermute(block, axis, [(i, (i + distance) % size) for i in range(size)])  5.66 us
    pallas_call x2, Pallas kernels, placed(): pl.pallas_call(functools.partial(place_kernel, chips, slots, win, groups,...  2.35 us
    unnamed x14, local copies, waits for them, and re-layouts  1.49 us
    another operation x1, other arithmetic, local(): place = jnp.stack([row_offsets[slot], col_offsets[slot]])  1.33 us
  transfers between devices with their start and end apart: 12, of which 9 were waited for; matrix products, arithmetic and copies ran while one was open for 5% of the time, Pallas kernels for 3%

profile of v3, /device:TPU:0, one launch (start us, length us, event | category | flops | bytes accessed | tf_op | source)
XLA Modules:
  0.0 56.7 jit_solution(14687227259006062908)
XLA Ops:
  0.0 1.3 %convert_bitcast_fusion.own_ref = bf16[2,768,128]{2,1,0:T(8,128)(2,1)S(1)} fusion(f32[1,2,768,128]{3,2,1,0:T(8,128)} %param.9), kind=kLoop, calls=%fused_computation | loop fusion | flops 196608 | bytes 1179648 | tf_op jit(solution)/shard_map/convert_element_type | solution.py:223
  1.3 3.9 %collective-permute-start = (bf16[2,768,128]{2,1,0:T(8,128)(2,1)S(1)}, bf16[2,768,128]{2,1,0:T(8,128)(2,1)S(1)}, u32[]{:S(2)}, u32[]{:S(2)}) collective-permute-start(bf16[2,768,128]{2,1,0:T(8,128)(2,1)S(1)} %convert_bitcast_fusion.own_ref), channel_id=1, source_target_pairs={{0,3},{1,0},{2,1},{3,2},{4,7},{5,4},{6,5},{7,6},{8,11},{9,8},{10,9... | collective-permute-start | bytes 1179656 | tf_op jit(solution)/shard_map/ppermute | solution.py:25
  5.2 0.7 %copy-done.4 = s32[4]{0:T(128)S(1)} copy-done((s32[4]{0:T(128)S(1)}, s32[4]{0:T(128)}, u32[]{:S(2)}) %copy-start.4) | copy-done | bytes 40
  5.9 0.7 %dynamic_slice.11 = s32[1]{0:T(128)} dynamic-slice(s32[4]{0:T(128)S(1)} %copy-done.4, s32[]{:T(128)S(6)} %select_n.41), dynamic_slice_sizes={1} | dynamic-slice | bytes 12 | tf_op jit(solution)/shard_map/dynamic_slice | solution.py:229
  7.2 1.3 %pad_add_fusion.1.place_ref = s32[2]{0:T(128)S(1)} fusion(s32[1]{0:T(128)} %dynamic_slice.11, s32[1]{0:T(128)} %dynamic_slice.10), kind=kLoop, calls=%fused_computation.29 | loop fusion | flops 2 | bytes 16 | tf_op jit(solution)/shard_map/stack | solution.py:229
  9.3 0.7 %shard_map.91.refs_4_ = bf16[4,2,128,128]{3,2,1,0:T(8,128)(2,1)S(1)} custom-call(s32[2]{0:T(128)S(1)} %pad_add_fusion.1.place_ref, f32[4,2,128,128]{3,2,1,0:T(8,128)S(1)} %copy-done.1), custom_call_target="tpu_custom_call" | custom-call | tf_op jit(solution)/shard_map/pallas_call | solution.py:230
  10.0 0.8 %copy-done.6 = f32[128,128]{1,0:T(8,128)S(1)} copy-done((f32[128,128]{1,0:T(8,128)S(1)}, f32[128,128]{1,0:T(8,128)}, u32[]{:S(2)}) %copy-start.6) | copy-done | bytes 65560
  11.1 2.5 %collective-permute-done.beside_ref = bf16[2,768,128]{2,1,0:T(8,128)(2,1)S(1)} collective-permute-done((bf16[2,768,128]{2,1,0:T(8,128)(2,1)S(1)}, bf16[2,768,128]{2,1,0:T(8,128)(2,1)S(1)}, u32[]{:S(2)}, u32[]{:S(2)}) %collective-permute-start) | collective-permute-done | bytes 393248 | tf_op jit(solution)/shard_map/ppermute | solution.py:25
  13.6 0.7 %shard_map.92 = (bf16[2,128,128]{2,1,0:T(8,128)(2,1)S(1)}, bf16[2,128,128]{2,1,0:T(8,128)(2,1)S(1)}, bf16[2,128,128]{2,1,0:T(8,128)(2,1)S(1)}, bf16[2,128,128]{2,1,0:T(8,128)(2,1)S(1)}) custom-call(s32[3]{0:T(128)S(1)} %pad_add_fusion.ints_ref.refs_0_, s32[4]{0:T(128)S(1)} %copy-done.5, s32[4]{0:T(128)S(1)} %copy-done.4, ...), custom_call_target="tpu_custom_call" | custom-call | tf_op jit(solution)/shard_map/pallas_call | solution.py:251
  14.3 1.7 %collective-permute-start.1 = (bf16[2,128,128]{2,1,0:T(8,128)(2,1)S(1)}, bf16[2,128,128]{2,1,0:T(8,128)(2,1)S(1)}, u32[]{:S(2)}, u32[]{:S(2)}) collective-permute-start(bf16[2,128,128]{2,1,0:T(8,128)(2,1)S(1)} %get-tuple-element.27), channel_id=1, source_target_pairs={{0,8},{4,12},{8,0},{12,4},{16,24},{20,28},{24,16},{28,20},{1,9},{5... | collective-permute-start | bytes 196616 | tf_op jit(solution)/shard_map/ppermute | solution.py:30
  16.0 2.6 %collective-permute-start.2 = (bf16[2,128,128]{2,1,0:T(8,128)(2,1)S(1)}, bf16[2,128,128]{2,1,0:T(8,128)(2,1)S(1)}, u32[]{:S(2)}, u32[]{:S(2)}) collective-permute-start(bf16[2,128,128]{2,1,0:T(8,128)(2,1)S(1)} %get-tuple-element.28), channel_id=1, source_target_pairs={{0,16},{4,20},{8,24},{12,28},{16,0},{20,4},{24,8},{28,12},{1,17},{... | collective-permute-start | bytes 196616 | tf_op jit(solution)/shard_map/ppermute | solution.py:30
  19.4 3.2 %collective-permute-done.2.refs_10_ = bf16[2,128,128]{2,1,0:T(8,128)(2,1)S(1)} collective-permute-done((bf16[2,128,128]{2,1,0:T(8,128)(2,1)S(1)}, bf16[2,128,128]{2,1,0:T(8,128)(2,1)S(1)}, u32[]{:S(2)}, u32[]{:S(2)}) %collective-permute-start.2) | collective-permute-done | bytes 65568 | tf_op jit(solution)/shard_map/ppermute | solution.py:30
  22.6 2.1 %collective-permute-done.3.refs_11_ = bf16[2,128,128]{2,1,0:T(8,128)(2,1)S(1)} collective-permute-done((bf16[2,128,128]{2,1,0:T(8,128)(2,1)S(1)}, bf16[2,128,128]{2,1,0:T(8,128)(2,1)S(1)}, u32[]{:S(2)}, u32[]{:S(2)}) %collective-permute-start.3) | collective-permute-done | bytes 65568 | tf_op jit(solution)/shard_map/ppermute | solution.py:30
  24.7 1.2 %collective-permute-done.5.refs_13_ = bf16[2,128,128]{2,1,0:T(8,128)(2,1)S(1)} collective-permute-done((bf16[2,128,128]{2,1,0:T(8,128)(2,1)S(1)}, bf16[2,128,128]{2,1,0:T(8,128)(2,1)S(1)}, u32[]{:S(2)}, u32[]{:S(2)}) %collective-permute-start.5) | collective-permute-done | bytes 65568 | tf_op jit(solution)/shard_map/ppermute | solution.py:35
  25.9 13.1 %shard_map.93 = (bf16[2,128,128]{2,1,0:T(8,128)(2,1)S(1)}, bf16[2,128,128]{2,1,0:T(8,128)(2,1)S(1)}, bf16[2,128,128]{2,1,0:T(8,128)(2,1)S(1)}, bf16[2,128,128]{2,1,0:T(8,128)(2,1)S(1)}) custom-call(s32[3]{0:T(128)S(1)} %pad_add_fusion.ints_ref.refs_0_, f32[1]{0:T(128)S(6)} %convert_element_type.17.refs_1_, bf16[256,256]{1,0:T(8,128)(2,1)S(1)} %copy-done.3, ...), custom_call_target="tpu_custom_call" | custom-call | tf_op jit(solution)/shard_map/pallas_call | solution.py:264
  39.1 2.2 %collective-permute-start.9 = (bf16[2,128,128]{2,1,0:T(8,128)(2,1)S(1)}, bf16[2,128,128]{2,1,0:T(8,128)(2,1)S(1)}, u32[]{:S(2)}, u32[]{:S(2)}) collective-permute-start(bf16[2,128,128]{2,1,0:T(8,128)(2,1)S(1)} %get-tuple-element.33), channel_id=1, source_target_pairs={{0,24},{4,28},{8,16},{12,20},{16,8},{20,12},{24,0},{28,4},{1,25},{... | collective-permute-start | bytes 196616 | tf_op jit(solution)/shard_map/ppermute | solution.py:30
  41.3 1.3 %collective-permute-start.10 = (bf16[2,128,128]{2,1,0:T(8,128)(2,1)S(1)}, bf16[2,128,128]{2,1,0:T(8,128)(2,1)S(1)}, u32[]{:S(2)}, u32[]{:S(2)}) collective-permute-start(bf16[2,128,128]{2,1,0:T(8,128)(2,1)S(1)} %get-tuple-element.34), channel_id=1, source_target_pairs={{0,16},{4,20},{8,24},{12,28},{16,0},{20,4},{24,8},{28,12},{1,17},{... | collective-permute-start | bytes 196616 | tf_op jit(solution)/shard_map/ppermute | solution.py:30
  42.6 0.8 %collective-permute-done.7.refs_4_ = bf16[2,128,128]{2,1,0:T(8,128)(2,1)S(1)} collective-permute-done((bf16[2,128,128]{2,1,0:T(8,128)(2,1)S(1)}, bf16[2,128,128]{2,1,0:T(8,128)(2,1)S(1)}, u32[]{:S(2)}, u32[]{:S(2)}) %collective-permute-start.7) | collective-permute-done | bytes 65568 | tf_op jit(solution)/shard_map/ppermute | solution.py:30
  43.4 2.4 %collective-permute-start.8 = (bf16[528,128]{1,0:T(8,128)(2,1)S(1)}, bf16[528,128]{1,0:T(8,128)(2,1)S(1)}, u32[]{:S(2)}, u32[]{:S(2)}) collective-permute-start(bf16[528,128]{1,0:T(8,128)(2,1)S(1)} %pad_maximum_fusion), channel_id=1, source_target_pairs={{0,1},{1,2},{2,3},{3,0},{4,5},{5,6},{6,7},{7,4},{8,9},{9,10},{10,1... | collective-permute-start | bytes 405512 | tf_op jit(solution)/shard_map/ppermute | solution.py:25
  46.0 2.7 %collective-permute-done.10.refs_5_ = bf16[2,128,128]{2,1,0:T(8,128)(2,1)S(1)} collective-permute-done((bf16[2,128,128]{2,1,0:T(8,128)(2,1)S(1)}, bf16[2,128,128]{2,1,0:T(8,128)(2,1)S(1)}, u32[]{:S(2)}, u32[]{:S(2)}) %collective-permute-start.10) | collective-permute-done | bytes 65568 | tf_op jit(solution)/shard_map/ppermute | solution.py:30
  48.7 2.4 %collective-permute-start.11 = (bf16[4,128,128]{2,1,0:T(8,128)(2,1)S(1)}, bf16[4,128,128]{2,1,0:T(8,128)(2,1)S(1)}, u32[]{:S(2)}, u32[]{:S(2)}) collective-permute-start(bf16[4,128,128]{2,1,0:T(8,128)(2,1)S(1)} %pad_maximum_fusion.2), channel_id=1, source_target_pairs={{0,1},{1,2},{2,3},{3,0},{4,5},{5,6},{6,7},{7,4},{8,9},{9,10},{10,1... | collective-permute-start | bytes 393224 | tf_op jit(solution)/shard_map/ppermute | solution.py:25
  51.1 0.8 %shard_map.94.refs_5_ = f32[2,768,128]{2,1,0:T(8,128)S(1)} custom-call(s32[3]{0:T(128)S(1)} %pad_add_fusion.ints_ref.refs_0_, s32[4]{0:T(128)S(1)} %copy-done.5, s32[4]{0:T(128)S(1)} %copy-done.4, bf16[2,128,128]{2,1,0:T(8,128)(2,1)S(1)} %get-tuple-element.30.refs_3_, bf16[2,128,128]{2,1,0:T(8,128)(2,1)S(1)} %collective-permute-done.7.refs_4_, ...), custom_call_target="tpu_custom_call" | custom-call | tf_op jit(solution)/shard_map/pallas_call | solution.py:289
  52.0 3.2 %collective-permute-done.11.refs_4_ = bf16[4,128,128]{2,1,0:T(8,128)(2,1)S(1)} collective-permute-done((bf16[4,128,128]{2,1,0:T(8,128)(2,1)S(1)}, bf16[4,128,128]{2,1,0:T(8,128)(2,1)S(1)}, u32[]{:S(2)}, u32[]{:S(2)}) %collective-permute-start.11) | collective-permute-done | bytes 131104 | tf_op jit(solution)/shard_map/ppermute | solution.py:25
  55.2 1.5 %shard_map.95 = f32[2,768,128]{2,1,0:T(8,128)} custom-call(s32[3]{0:T(128)S(1)} %pad_add_fusion.ints_ref.refs_0_, s32[4]{0:T(128)S(1)} %get-tuple-element.38.refs_1_, s32[4]{0:T(128)S(1)} %get-tuple-element.37.refs_2_, bf16[4,128,128]{2,1,0:T(8,128)(2,1)S(1)} %bitcast.21, bf16[4,128,128]{2,1,0:T(8,128)(2,1)S(1)} %collective-permute-done.11.refs_4_, ...), custom_call_target="tpu_custom_call" | custom-call | tf_op jit(solution)/shard_map/pallas_call | solution.py:289
  (35 shorter events, 2.0 us)
Async XLA Ops:
  0.0 10.0 %copy-start = (f32[4,128,128]{2,1,0:T(8,128)S(1)}, f32[4,128,128]{2,1,0:T(8,128)}, u32[]{:S(2)}) copy-start(f32[4,128,128]{2,1,0:T(8,128)} %param.12) | copy-start | bytes 786436
  0.0 9.2 %copy-start.1 = (f32[4,2,128,128]{3,2,1,0:T(8,128)S(1)}, f32[4,2,128,128]{3,2,1,0:T(8,128)}, u32[]{:S(2)}) copy-start(f32[4,2,128,128]{3,2,1,0:T(8,128)} %probe_ref.1) | copy-start | bytes 1572868
  1.3 12.3 %collective-permute-start = (bf16[2,768,128]{2,1,0:T(8,128)(2,1)S(1)}, bf16[2,768,128]{2,1,0:T(8,128)(2,1)S(1)}, u32[]{:S(2)}, u32[]{:S(2)}) collective-permute-start(bf16[2,768,128]{2,1,0:T(8,128)(2,1)S(1)} %convert_bitcast_fusion.own_ref), channel_id=1, source_target_pairs={{0,3},{1,0},{2,1},{3,2},{4,7},{5,4},{6,5},{7,6},{8,11},{9,8},{10,9... | collective-permute-start | bytes 1179656 | tf_op jit(solution)/shard_map/ppermute | solution.py:25
  5.2 0.7 %copy-start.4 = (s32[4]{0:T(128)S(1)}, s32[4]{0:T(128)}, u32[]{:S(2)}) copy-start(s32[4]{0:T(128)} %refs_2_.2) | copy-start | bytes 52
  5.9 0.7 %copy-start.5 = (s32[4]{0:T(128)S(1)}, s32[4]{0:T(128)}, u32[]{:S(2)}) copy-start(s32[4]{0:T(128)} %refs_1_.1) | copy-start | bytes 52
  10.0 0.8 %copy-start.6 = (f32[128,128]{1,0:T(8,128)S(1)}, f32[128,128]{1,0:T(8,128)}, u32[]{:S(2)}) copy-start(f32[128,128]{1,0:T(8,128)} %param.11) | copy-start | bytes 196612
  14.3 5.0 %collective-permute-start.1 = (bf16[2,128,128]{2,1,0:T(8,128)(2,1)S(1)}, bf16[2,128,128]{2,1,0:T(8,128)(2,1)S(1)}, u32[]{:S(2)}, u32[]{:S(2)}) collective-permute-start(bf16[2,128,128]{2,1,0:T(8,128)(2,1)S(1)} %get-tuple-element.27), channel_id=1, source_target_pairs={{0,8},{4,12},{8,0},{12,4},{16,24},{20,28},{24,16},{28,20},{1,9},{5... | collective-permute-start | bytes 196616 | tf_op jit(solution)/shard_map/ppermute | solution.py:30
  16.0 6.6 %collective-permute-start.2 = (bf16[2,128,128]{2,1,0:T(8,128)(2,1)S(1)}, bf16[2,128,128]{2,1,0:T(8,128)(2,1)S(1)}, u32[]{:S(2)}, u32[]{:S(2)}) collective-permute-start(bf16[2,128,128]{2,1,0:T(8,128)(2,1)S(1)} %get-tuple-element.28), channel_id=1, source_target_pairs={{0,16},{4,20},{8,24},{12,28},{16,0},{20,4},{24,8},{28,12},{1,17},{... | collective-permute-start | bytes 196616 | tf_op jit(solution)/shard_map/ppermute | solution.py:30
  18.6 6.1 %collective-permute-start.3 = (bf16[2,128,128]{2,1,0:T(8,128)(2,1)S(1)}, bf16[2,128,128]{2,1,0:T(8,128)(2,1)S(1)}, u32[]{:S(2)}, u32[]{:S(2)}) collective-permute-start(bf16[2,128,128]{2,1,0:T(8,128)(2,1)S(1)} %get-tuple-element.29), channel_id=1, source_target_pairs={{0,24},{4,28},{8,16},{12,20},{16,8},{20,12},{24,0},{28,4},{1,25},{... | collective-permute-start | bytes 196616 | tf_op jit(solution)/shard_map/ppermute | solution.py:30
  19.3 6.6 %copy-start.2 = (bf16[256,256]{1,0:T(8,128)(2,1)S(1)}, bf16[256,256]{1,0:T(8,128)(2,1)}, u32[]{:S(2)}) copy-start(bf16[256,256]{1,0:T(8,128)(2,1)} %constant.86.clone.refs_3_) | copy-start | bytes 393220
  19.3 6.6 %copy-start.3 = (bf16[256,256]{1,0:T(8,128)(2,1)S(1)}, bf16[256,256]{1,0:T(8,128)(2,1)}, u32[]{:S(2)}) copy-start(bf16[256,256]{1,0:T(8,128)(2,1)} %constant.85.clone.refs_2_) | copy-start | bytes 393220
  19.3 6.6 %collective-permute-start.4 = (bf16[4,128,128]{2,1,0:T(8,128)(2,1)S(1)}, bf16[4,128,128]{2,1,0:T(8,128)(2,1)S(1)}, u32[]{:S(2)}, u32[]{:S(2)}) collective-permute-start(bf16[4,128,128]{2,1,0:T(8,128)(2,1)S(1)} %pad_maximum_fusion.1), channel_id=1, source_target_pairs={{0,4},{4,0},{8,12},{12,8},{16,20},{20,16},{24,28},{28,24},{1,5},{5... | collective-permute-start | bytes 393224 | tf_op jit(solution)/shard_map/ppermute | solution.py:35
  22.6 2.1 %collective-permute-start.6 = (bf16[2,128,128]{2,1,0:T(8,128)(2,1)S(1)}, bf16[2,128,128]{2,1,0:T(8,128)(2,1)S(1)}, u32[]{:S(2)}, u32[]{:S(2)}) collective-permute-start(bf16[2,128,128]{2,1,0:T(8,128)(2,1)S(1)} %collective-permute-done.2.refs_10_), channel_id=1, source_target_pairs={{0,4},{4,0},{8,12},{12,8},{16,20},{20,16},{24,28},{28,24},{1,5},{5... | collective-permute-start | bytes 196616 | tf_op jit(solution)/shard_map/ppermute | solution.py:35
  24.7 1.3 %collective-permute-start.5 = (bf16[2,128,128]{2,1,0:T(8,128)(2,1)S(1)}, bf16[2,128,128]{2,1,0:T(8,128)(2,1)S(1)}, u32[]{:S(2)}, u32[]{:S(2)}) collective-permute-start(bf16[2,128,128]{2,1,0:T(8,128)(2,1)S(1)} %collective-permute-done.3.refs_11_), channel_id=1, source_target_pairs={{0,4},{4,0},{8,12},{12,8},{16,20},{20,16},{24,28},{28,24},{1,5},{5... | collective-permute-start | bytes 196616 | tf_op jit(solution)/shard_map/ppermute | solution.py:35
  39.1 4.3 %collective-permute-start.7 = (bf16[2,128,128]{2,1,0:T(8,128)(2,1)S(1)}, bf16[2,128,128]{2,1,0:T(8,128)(2,1)S(1)}, u32[]{:S(2)}, u32[]{:S(2)}) collective-permute-start(bf16[2,128,128]{2,1,0:T(8,128)(2,1)S(1)} %get-tuple-element.31), channel_id=1, source_target_pairs={{0,8},{4,12},{8,0},{12,4},{16,24},{20,28},{24,16},{28,20},{1,9},{5... | collective-permute-start | bytes 196616 | tf_op jit(solution)/shard_map/ppermute | solution.py:30
  39.1 6.8 %collective-permute-start.9 = (bf16[2,128,128]{2,1,0:T(8,128)(2,1)S(1)}, bf16[2,128,128]{2,1,0:T(8,128)(2,1)S(1)}, u32[]{:S(2)}, u32[]{:S(2)}) collective-permute-start(bf16[2,128,128]{2,1,0:T(8,128)(2,1)S(1)} %get-tuple-element.33), channel_id=1, source_target_pairs={{0,24},{4,28},{8,16},{12,20},{16,8},{20,12},{24,0},{28,4},{1,25},{... | collective-permute-start | bytes 196616 | tf_op jit(solution)/shard_map/ppermute | solution.py:30
  41.3 7.4 %collective-permute-start.10 = (bf16[2,128,128]{2,1,0:T(8,128)(2,1)S(1)}, bf16[2,128,128]{2,1,0:T(8,128)(2,1)S(1)}, u32[]{:S(2)}, u32[]{:S(2)}) collective-permute-start(bf16[2,128,128]{2,1,0:T(8,128)(2,1)S(1)} %get-tuple-element.34), channel_id=1, source_target_pairs={{0,16},{4,20},{8,24},{12,28},{16,0},{20,4},{24,8},{28,12},{1,17},{... | collective-permute-start | bytes 196616 | tf_op jit(solution)/shard_map/ppermute | solution.py:30
  43.4 8.6 %collective-permute-start.8 = (bf16[528,128]{1,0:T(8,128)(2,1)S(1)}, bf16[528,128]{1,0:T(8,128)(2,1)S(1)}, u32[]{:S(2)}, u32[]{:S(2)}) collective-permute-start(bf16[528,128]{1,0:T(8,128)(2,1)S(1)} %pad_maximum_fusion), channel_id=1, source_target_pairs={{0,1},{1,2},{2,3},{3,0},{4,5},{5,6},{6,7},{7,4},{8,9},{9,10},{10,1... | collective-permute-start | bytes 405512 | tf_op jit(solution)/shard_map/ppermute | solution.py:25
  48.7 6.5 %collective-permute-start.11 = (bf16[4,128,128]{2,1,0:T(8,128)(2,1)S(1)}, bf16[4,128,128]{2,1,0:T(8,128)(2,1)S(1)}, u32[]{:S(2)}, u32[]{:S(2)}) collective-permute-start(bf16[4,128,128]{2,1,0:T(8,128)(2,1)S(1)} %pad_maximum_fusion.2), channel_id=1, source_target_pairs={{0,1},{1,2},{2,3},{3,0},{4,5},{5,6},{6,7},{7,4},{8,9},{9,10},{10,1... | collective-permute-start | bytes 393224 | tf_op jit(solution)/shard_map/ppermute | solution.py:25

commit v4 on v3

--- a/solution.py
+++ b/solution.py
@@ -114,7 +114,7 @@
         return from_right(from_left(left_ref[...], pairs), right_ref[...])
 
     def inverse(pairs):
-        return from_right(from_left(right_ref[...], pairs), left_ref[...])
+        return from_left(right_ref[...], from_right(pairs, left_ref[...]))
 
     def mul(a, b):
         return (a[0] * b[0] - a[1] * b[1], a[0] * b[1] + a[1] * b[0])
@@ -145,7 +145,7 @@
                 wave_ref[s + 1, m, part] = waves[m][part]
         return carry
 
-    lax.fori_loop(0, slices - 1, forward_step, 0)
+    lax.fori_loop(0, slices - 1, forward_step, 0, unroll=True)
     patch = patch_at(slices - 1)
     exits = transform([mul(wave, patch) for wave in waves_at(slices - 1)])
     power = sum(pair[0] * pair[0] + pair[1] * pair[1] for pair in exits) * (unit * unit)
@@ -168,7 +168,7 @@
         keep_grad(s - 1, back)
         return back
 
-    lax.fori_loop(0, slices - 1, backward_step, back)
+    lax.fori_loop(0, slices - 1, backward_step, back, unroll=True)
     for p in range(chips):
         out_refs[p][...] = grad_ref[CORES * (chip ^ p) + core]
 

time: 56.9 us -> 55.1 us (0.968)
  Pallas kernels: 16.9 us -> 15.1 us
    pallas_call x1, Pallas kernels: 13.1 us -> 11.3 us  [local(): pl.pallas_call(functools.partial(window_kernel, chips, modes, win, swaps)...]
where the time goes in v4:
time: 55.1 us; the launch traced here: 54.8 us
  starting transfers between devices  16.9 us (31%)
  waiting for transfers between devices  16.3 us (30%)
  Pallas kernels  15.1 us (27%)
  other arithmetic  2.99 us (5%)
  local copies, waits for them, and re-layouts  2.76 us (5%)
  between operations  0.82 us (1%)
    pallas_call x1, Pallas kernels, local(): pl.pallas_call(functools.partial(window_kernel, chips, modes, win, swaps)...  11.3 us
    ppermute x6, waiting for transfers between devices, crossed(): lax.ppermute(block, 'cuts', [(i, i ^ CORES * distance) for i in range(siz...  9.36 us
    ppermute x3, starting transfers between devices, passed_round(): lax.ppermute(block, axis, [(i, (i + distance) % size) for i in range(size)])  8.83 us
    ppermute x6, starting transfers between devices, crossed(): lax.ppermute(block, 'cuts', [(i, i ^ CORES * distance) for i in range(siz...  8 us
    ppermute x3, waiting for transfers between devices, passed_round(): lax.ppermute(block, axis, [(i, (i + distance) % size) for i in range(size)])  5.66 us
    pallas_call x2, Pallas kernels, placed(): pl.pallas_call(functools.partial(place_kernel, chips, slots, win, groups,...  2.35 us
    unnamed x14, local copies, waits for them, and re-layouts  1.49 us
    another operation x1, other arithmetic, local(): place = jnp.stack([row_offsets[slot], col_offsets[slot]])  1.33 us
  transfers between devices with their start and end apart: 12, of which 9 were waited for; matrix products, arithmetic and copies ran while one was open for 5% of the time, Pallas kernels for 3%

profile of v4, /device:TPU:0, one launch (start us, length us, event | category | flops | bytes accessed | tf_op | source)
XLA Modules:
  0.0 54.8 jit_solution(4802881632004747045)
XLA Ops:
  0.0 1.3 %convert_bitcast_fusion.own_ref = bf16[2,768,128]{2,1,0:T(8,128)(2,1)S(1)} fusion(f32[1,2,768,128]{3,2,1,0:T(8,128)} %param.9), kind=kLoop, calls=%fused_computation | loop fusion | flops 196608 | bytes 1179648 | tf_op jit(solution)/shard_map/convert_element_type | solution.py:223
  1.3 3.9 %collective-permute-start = (bf16[2,768,128]{2,1,0:T(8,128)(2,1)S(1)}, bf16[2,768,128]{2,1,0:T(8,128)(2,1)S(1)}, u32[]{:S(2)}, u32[]{:S(2)}) collective-permute-start(bf16[2,768,128]{2,1,0:T(8,128)(2,1)S(1)} %convert_bitcast_fusion.own_ref), channel_id=1, source_target_pairs={{0,3},{1,0},{2,1},{3,2},{4,7},{5,4},{6,5},{7,6},{8,11},{9,8},{10,9... | collective-permute-start | bytes 1179656 | tf_op jit(solution)/shard_map/ppermute | solution.py:25
  5.2 0.7 %copy-done.4 = s32[4]{0:T(128)S(1)} copy-done((s32[4]{0:T(128)S(1)}, s32[4]{0:T(128)}, u32[]{:S(2)}) %copy-start.4) | copy-done | bytes 40
  5.9 0.7 %dynamic_slice.11 = s32[1]{0:T(128)} dynamic-slice(s32[4]{0:T(128)S(1)} %copy-done.4, s32[]{:T(128)S(6)} %select_n.41), dynamic_slice_sizes={1} | dynamic-slice | bytes 12 | tf_op jit(solution)/shard_map/dynamic_slice | solution.py:229
  7.2 1.3 %pad_add_fusion.1.place_ref = s32[2]{0:T(128)S(1)} fusion(s32[1]{0:T(128)} %dynamic_slice.11, s32[1]{0:T(128)} %dynamic_slice.10), kind=kLoop, calls=%fused_computation.29 | loop fusion | flops 2 | bytes 16 | tf_op jit(solution)/shard_map/stack | solution.py:229
  9.3 0.7 %shard_map.91.refs_4_ = bf16[4,2,128,128]{3,2,1,0:T(8,128)(2,1)S(1)} custom-call(s32[2]{0:T(128)S(1)} %pad_add_fusion.1.place_ref, f32[4,2,128,128]{3,2,1,0:T(8,128)S(1)} %copy-done.1), custom_call_target="tpu_custom_call" | custom-call | tf_op jit(solution)/shard_map/pallas_call | solution.py:230
  10.0 0.8 %copy-done.6 = f32[128,128]{1,0:T(8,128)S(1)} copy-done((f32[128,128]{1,0:T(8,128)S(1)}, f32[128,128]{1,0:T(8,128)}, u32[]{:S(2)}) %copy-start.6) | copy-done | bytes 65560
  11.1 2.5 %collective-permute-done.beside_ref = bf16[2,768,128]{2,1,0:T(8,128)(2,1)S(1)} collective-permute-done((bf16[2,768,128]{2,1,0:T(8,128)(2,1)S(1)}, bf16[2,768,128]{2,1,0:T(8,128)(2,1)S(1)}, u32[]{:S(2)}, u32[]{:S(2)}) %collective-permute-start) | collective-permute-done | bytes 393248 | tf_op jit(solution)/shard_map/ppermute | solution.py:25
  13.6 0.7 %shard_map.92 = (bf16[2,128,128]{2,1,0:T(8,128)(2,1)S(1)}, bf16[2,128,128]{2,1,0:T(8,128)(2,1)S(1)}, bf16[2,128,128]{2,1,0:T(8,128)(2,1)S(1)}, bf16[2,128,128]{2,1,0:T(8,128)(2,1)S(1)}) custom-call(s32[3]{0:T(128)S(1)} %pad_add_fusion.ints_ref.refs_0_, s32[4]{0:T(128)S(1)} %copy-done.5, s32[4]{0:T(128)S(1)} %copy-done.4, ...), custom_call_target="tpu_custom_call" | custom-call | tf_op jit(solution)/shard_map/pallas_call | solution.py:251
  14.3 1.7 %collective-permute-start.1 = (bf16[2,128,128]{2,1,0:T(8,128)(2,1)S(1)}, bf16[2,128,128]{2,1,0:T(8,128)(2,1)S(1)}, u32[]{:S(2)}, u32[]{:S(2)}) collective-permute-start(bf16[2,128,128]{2,1,0:T(8,128)(2,1)S(1)} %get-tuple-element.27), channel_id=1, source_target_pairs={{0,8},{4,12},{8,0},{12,4},{16,24},{20,28},{24,16},{28,20},{1,9},{5... | collective-permute-start | bytes 196616 | tf_op jit(solution)/shard_map/ppermute | solution.py:30
  16.0 2.6 %collective-permute-start.2 = (bf16[2,128,128]{2,1,0:T(8,128)(2,1)S(1)}, bf16[2,128,128]{2,1,0:T(8,128)(2,1)S(1)}, u32[]{:S(2)}, u32[]{:S(2)}) collective-permute-start(bf16[2,128,128]{2,1,0:T(8,128)(2,1)S(1)} %get-tuple-element.28), channel_id=1, source_target_pairs={{0,16},{4,20},{8,24},{12,28},{16,0},{20,4},{24,8},{28,12},{1,17},{... | collective-permute-start | bytes 196616 | tf_op jit(solution)/shard_map/ppermute | solution.py:30
  19.4 3.2 %collective-permute-done.2.refs_10_ = bf16[2,128,128]{2,1,0:T(8,128)(2,1)S(1)} collective-permute-done((bf16[2,128,128]{2,1,0:T(8,128)(2,1)S(1)}, bf16[2,128,128]{2,1,0:T(8,128)(2,1)S(1)}, u32[]{:S(2)}, u32[]{:S(2)}) %collective-permute-start.2) | collective-permute-done | bytes 65568 | tf_op jit(solution)/shard_map/ppermute | solution.py:30
  22.6 2.1 %collective-permute-done.3.refs_11_ = bf16[2,128,128]{2,1,0:T(8,128)(2,1)S(1)} collective-permute-done((bf16[2,128,128]{2,1,0:T(8,128)(2,1)S(1)}, bf16[2,128,128]{2,1,0:T(8,128)(2,1)S(1)}, u32[]{:S(2)}, u32[]{:S(2)}) %collective-permute-start.3) | collective-permute-done | bytes 65568 | tf_op jit(solution)/shard_map/ppermute | solution.py:30
  24.7 1.2 %collective-permute-done.5.refs_13_ = bf16[2,128,128]{2,1,0:T(8,128)(2,1)S(1)} collective-permute-done((bf16[2,128,128]{2,1,0:T(8,128)(2,1)S(1)}, bf16[2,128,128]{2,1,0:T(8,128)(2,1)S(1)}, u32[]{:S(2)}, u32[]{:S(2)}) %collective-permute-start.5) | collective-permute-done | bytes 65568 | tf_op jit(solution)/shard_map/ppermute | solution.py:35
  25.9 11.3 %shard_map.93 = (bf16[2,128,128]{2,1,0:T(8,128)(2,1)S(1)}, bf16[2,128,128]{2,1,0:T(8,128)(2,1)S(1)}, bf16[2,128,128]{2,1,0:T(8,128)(2,1)S(1)}, bf16[2,128,128]{2,1,0:T(8,128)(2,1)S(1)}) custom-call(s32[3]{0:T(128)S(1)} %pad_add_fusion.ints_ref.refs_0_, f32[1]{0:T(128)S(6)} %convert_element_type.17.refs_1_, bf16[256,256]{1,0:T(8,128)(2,1)S(1)} %copy-done.3, ...), custom_call_target="tpu_custom_call" | custom-call | tf_op jit(solution)/shard_map/pallas_call | solution.py:264
  37.3 2.2 %collective-permute-start.9 = (bf16[2,128,128]{2,1,0:T(8,128)(2,1)S(1)}, bf16[2,128,128]{2,1,0:T(8,128)(2,1)S(1)}, u32[]{:S(2)}, u32[]{:S(2)}) collective-permute-start(bf16[2,128,128]{2,1,0:T(8,128)(2,1)S(1)} %get-tuple-element.33), channel_id=1, source_target_pairs={{0,24},{4,28},{8,16},{12,20},{16,8},{20,12},{24,0},{28,4},{1,25},{... | collective-permute-start | bytes 196616 | tf_op jit(solution)/shard_map/ppermute | solution.py:30
  39.5 1.3 %collective-permute-start.10 = (bf16[2,128,128]{2,1,0:T(8,128)(2,1)S(1)}, bf16[2,128,128]{2,1,0:T(8,128)(2,1)S(1)}, u32[]{:S(2)}, u32[]{:S(2)}) collective-permute-start(bf16[2,128,128]{2,1,0:T(8,128)(2,1)S(1)} %get-tuple-element.34), channel_id=1, source_target_pairs={{0,16},{4,20},{8,24},{12,28},{16,0},{20,4},{24,8},{28,12},{1,17},{... | collective-permute-start | bytes 196616 | tf_op jit(solution)/shard_map/ppermute | solution.py:30
  40.8 0.8 %collective-permute-done.7.refs_4_ = bf16[2,128,128]{2,1,0:T(8,128)(2,1)S(1)} collective-permute-done((bf16[2,128,128]{2,1,0:T(8,128)(2,1)S(1)}, bf16[2,128,128]{2,1,0:T(8,128)(2,1)S(1)}, u32[]{:S(2)}, u32[]{:S(2)}) %collective-permute-start.7) | collective-permute-done | bytes 65568 | tf_op jit(solution)/shard_map/ppermute | solution.py:30
  41.6 2.4 %collective-permute-start.8 = (bf16[528,128]{1,0:T(8,128)(2,1)S(1)}, bf16[528,128]{1,0:T(8,128)(2,1)S(1)}, u32[]{:S(2)}, u32[]{:S(2)}) collective-permute-start(bf16[528,128]{1,0:T(8,128)(2,1)S(1)} %pad_maximum_fusion), channel_id=1, source_target_pairs={{0,1},{1,2},{2,3},{3,0},{4,5},{5,6},{6,7},{7,4},{8,9},{9,10},{10,1... | collective-permute-start | bytes 405512 | tf_op jit(solution)/shard_map/ppermute | solution.py:25
  44.1 2.7 %collective-permute-done.10.refs_5_ = bf16[2,128,128]{2,1,0:T(8,128)(2,1)S(1)} collective-permute-done((bf16[2,128,128]{2,1,0:T(8,128)(2,1)S(1)}, bf16[2,128,128]{2,1,0:T(8,128)(2,1)S(1)}, u32[]{:S(2)}, u32[]{:S(2)}) %collective-permute-start.10) | collective-permute-done | bytes 65568 | tf_op jit(solution)/shard_map/ppermute | solution.py:30
  46.8 2.4 %collective-permute-start.11 = (bf16[4,128,128]{2,1,0:T(8,128)(2,1)S(1)}, bf16[4,128,128]{2,1,0:T(8,128)(2,1)S(1)}, u32[]{:S(2)}, u32[]{:S(2)}) collective-permute-start(bf16[4,128,128]{2,1,0:T(8,128)(2,1)S(1)} %pad_maximum_fusion.2), channel_id=1, source_target_pairs={{0,1},{1,2},{2,3},{3,0},{4,5},{5,6},{6,7},{7,4},{8,9},{9,10},{10,1... | collective-permute-start | bytes 393224 | tf_op jit(solution)/shard_map/ppermute | solution.py:25
  49.3 0.8 %shard_map.94.refs_5_ = f32[2,768,128]{2,1,0:T(8,128)S(1)} custom-call(s32[3]{0:T(128)S(1)} %pad_add_fusion.ints_ref.refs_0_, s32[4]{0:T(128)S(1)} %copy-done.5, s32[4]{0:T(128)S(1)} %copy-done.4, bf16[2,128,128]{2,1,0:T(8,128)(2,1)S(1)} %get-tuple-element.30.refs_3_, bf16[2,128,128]{2,1,0:T(8,128)(2,1)S(1)} %collective-permute-done.7.refs_4_, ...), custom_call_target="tpu_custom_call" | custom-call | tf_op jit(solution)/shard_map/pallas_call | solution.py:289
  50.2 3.2 %collective-permute-done.11.refs_4_ = bf16[4,128,128]{2,1,0:T(8,128)(2,1)S(1)} collective-permute-done((bf16[4,128,128]{2,1,0:T(8,128)(2,1)S(1)}, bf16[4,128,128]{2,1,0:T(8,128)(2,1)S(1)}, u32[]{:S(2)}, u32[]{:S(2)}) %collective-permute-start.11) | collective-permute-done | bytes 131104 | tf_op jit(solution)/shard_map/ppermute | solution.py:25
  53.3 1.5 %shard_map.95 = f32[2,768,128]{2,1,0:T(8,128)} custom-call(s32[3]{0:T(128)S(1)} %pad_add_fusion.ints_ref.refs_0_, s32[4]{0:T(128)S(1)} %get-tuple-element.38.refs_1_, s32[4]{0:T(128)S(1)} %get-tuple-element.37.refs_2_, bf16[4,128,128]{2,1,0:T(8,128)(2,1)S(1)} %bitcast.21, bf16[4,128,128]{2,1,0:T(8,128)(2,1)S(1)} %collective-permute-done.11.refs_4_, ...), custom_call_target="tpu_custom_call" | custom-call | tf_op jit(solution)/shard_map/pallas_call | solution.py:289
  (35 shorter events, 2.0 us)
Async XLA Ops:
  0.0 10.0 %copy-start = (f32[4,128,128]{2,1,0:T(8,128)S(1)}, f32[4,128,128]{2,1,0:T(8,128)}, u32[]{:S(2)}) copy-start(f32[4,128,128]{2,1,0:T(8,128)} %param.12) | copy-start | bytes 786436
  0.0 9.2 %copy-start.1 = (f32[4,2,128,128]{3,2,1,0:T(8,128)S(1)}, f32[4,2,128,128]{3,2,1,0:T(8,128)}, u32[]{:S(2)}) copy-start(f32[4,2,128,128]{3,2,1,0:T(8,128)} %probe_ref.1) | copy-start | bytes 1572868
  1.3 12.3 %collective-permute-start = (bf16[2,768,128]{2,1,0:T(8,128)(2,1)S(1)}, bf16[2,768,128]{2,1,0:T(8,128)(2,1)S(1)}, u32[]{:S(2)}, u32[]{:S(2)}) collective-permute-start(bf16[2,768,128]{2,1,0:T(8,128)(2,1)S(1)} %convert_bitcast_fusion.own_ref), channel_id=1, source_target_pairs={{0,3},{1,0},{2,1},{3,2},{4,7},{5,4},{6,5},{7,6},{8,11},{9,8},{10,9... | collective-permute-start | bytes 1179656 | tf_op jit(solution)/shard_map/ppermute | solution.py:25
  5.2 0.7 %copy-start.4 = (s32[4]{0:T(128)S(1)}, s32[4]{0:T(128)}, u32[]{:S(2)}) copy-start(s32[4]{0:T(128)} %refs_2_.2) | copy-start | bytes 52
  5.9 0.7 %copy-start.5 = (s32[4]{0:T(128)S(1)}, s32[4]{0:T(128)}, u32[]{:S(2)}) copy-start(s32[4]{0:T(128)} %refs_1_.1) | copy-start | bytes 52
  10.0 0.8 %copy-start.6 = (f32[128,128]{1,0:T(8,128)S(1)}, f32[128,128]{1,0:T(8,128)}, u32[]{:S(2)}) copy-start(f32[128,128]{1,0:T(8,128)} %param.11) | copy-start | bytes 196612
  14.3 5.0 %collective-permute-start.1 = (bf16[2,128,128]{2,1,0:T(8,128)(2,1)S(1)}, bf16[2,128,128]{2,1,0:T(8,128)(2,1)S(1)}, u32[]{:S(2)}, u32[]{:S(2)}) collective-permute-start(bf16[2,128,128]{2,1,0:T(8,128)(2,1)S(1)} %get-tuple-element.27), channel_id=1, source_target_pairs={{0,8},{4,12},{8,0},{12,4},{16,24},{20,28},{24,16},{28,20},{1,9},{5... | collective-permute-start | bytes 196616 | tf_op jit(solution)/shard_map/ppermute | solution.py:30
  16.0 6.6 %collective-permute-start.2 = (bf16[2,128,128]{2,1,0:T(8,128)(2,1)S(1)}, bf16[2,128,128]{2,1,0:T(8,128)(2,1)S(1)}, u32[]{:S(2)}, u32[]{:S(2)}) collective-permute-start(bf16[2,128,128]{2,1,0:T(8,128)(2,1)S(1)} %get-tuple-element.28), channel_id=1, source_target_pairs={{0,16},{4,20},{8,24},{12,28},{16,0},{20,4},{24,8},{28,12},{1,17},{... | collective-permute-start | bytes 196616 | tf_op jit(solution)/shard_map/ppermute | solution.py:30
  18.6 6.1 %collective-permute-start.3 = (bf16[2,128,128]{2,1,0:T(8,128)(2,1)S(1)}, bf16[2,128,128]{2,1,0:T(8,128)(2,1)S(1)}, u32[]{:S(2)}, u32[]{:S(2)}) collective-permute-start(bf16[2,128,128]{2,1,0:T(8,128)(2,1)S(1)} %get-tuple-element.29), channel_id=1, source_target_pairs={{0,24},{4,28},{8,16},{12,20},{16,8},{20,12},{24,0},{28,4},{1,25},{... | collective-permute-start | bytes 196616 | tf_op jit(solution)/shard_map/ppermute | solution.py:30
  19.3 6.6 %copy-start.2 = (bf16[256,256]{1,0:T(8,128)(2,1)S(1)}, bf16[256,256]{1,0:T(8,128)(2,1)}, u32[]{:S(2)}) copy-start(bf16[256,256]{1,0:T(8,128)(2,1)} %constant.86.clone.refs_3_) | copy-start | bytes 393220
  19.3 6.6 %copy-start.3 = (bf16[256,256]{1,0:T(8,128)(2,1)S(1)}, bf16[256,256]{1,0:T(8,128)(2,1)}, u32[]{:S(2)}) copy-start(bf16[256,256]{1,0:T(8,128)(2,1)} %constant.85.clone.refs_2_) | copy-start | bytes 393220
  19.3 6.6 %collective-permute-start.4 = (bf16[4,128,128]{2,1,0:T(8,128)(2,1)S(1)}, bf16[4,128,128]{2,1,0:T(8,128)(2,1)S(1)}, u32[]{:S(2)}, u32[]{:S(2)}) collective-permute-start(bf16[4,128,128]{2,1,0:T(8,128)(2,1)S(1)} %pad_maximum_fusion.1), channel_id=1, source_target_pairs={{0,4},{4,0},{8,12},{12,8},{16,20},{20,16},{24,28},{28,24},{1,5},{5... | collective-permute-start | bytes 393224 | tf_op jit(solution)/shard_map/ppermute | solution.py:35
  22.6 2.1 %collective-permute-start.6 = (bf16[2,128,128]{2,1,0:T(8,128)(2,1)S(1)}, bf16[2,128,128]{2,1,0:T(8,128)(2,1)S(1)}, u32[]{:S(2)}, u32[]{:S(2)}) collective-permute-start(bf16[2,128,128]{2,1,0:T(8,128)(2,1)S(1)} %collective-permute-done.2.refs_10_), channel_id=1, source_target_pairs={{0,4},{4,0},{8,12},{12,8},{16,20},{20,16},{24,28},{28,24},{1,5},{5... | collective-permute-start | bytes 196616 | tf_op jit(solution)/shard_map/ppermute | solution.py:35
  24.7 1.3 %collective-permute-start.5 = (bf16[2,128,128]{2,1,0:T(8,128)(2,1)S(1)}, bf16[2,128,128]{2,1,0:T(8,128)(2,1)S(1)}, u32[]{:S(2)}, u32[]{:S(2)}) collective-permute-start(bf16[2,128,128]{2,1,0:T(8,128)(2,1)S(1)} %collective-permute-done.3.refs_11_), channel_id=1, source_target_pairs={{0,4},{4,0},{8,12},{12,8},{16,20},{20,16},{24,28},{28,24},{1,5},{5... | collective-permute-start | bytes 196616 | tf_op jit(solution)/shard_map/ppermute | solution.py:35
  37.2 4.3 %collective-permute-start.7 = (bf16[2,128,128]{2,1,0:T(8,128)(2,1)S(1)}, bf16[2,128,128]{2,1,0:T(8,128)(2,1)S(1)}, u32[]{:S(2)}, u32[]{:S(2)}) collective-permute-start(bf16[2,128,128]{2,1,0:T(8,128)(2,1)S(1)} %get-tuple-element.31), channel_id=1, source_target_pairs={{0,8},{4,12},{8,0},{12,4},{16,24},{20,28},{24,16},{28,20},{1,9},{5... | collective-permute-start | bytes 196616 | tf_op jit(solution)/shard_map/ppermute | solution.py:30
  37.3 6.8 %collective-permute-start.9 = (bf16[2,128,128]{2,1,0:T(8,128)(2,1)S(1)}, bf16[2,128,128]{2,1,0:T(8,128)(2,1)S(1)}, u32[]{:S(2)}, u32[]{:S(2)}) collective-permute-start(bf16[2,128,128]{2,1,0:T(8,128)(2,1)S(1)} %get-tuple-element.33), channel_id=1, source_target_pairs={{0,24},{4,28},{8,16},{12,20},{16,8},{20,12},{24,0},{28,4},{1,25},{... | collective-permute-start | bytes 196616 | tf_op jit(solution)/shard_map/ppermute | solution.py:30
  39.5 7.4 %collective-permute-start.10 = (bf16[2,128,128]{2,1,0:T(8,128)(2,1)S(1)}, bf16[2,128,128]{2,1,0:T(8,128)(2,1)S(1)}, u32[]{:S(2)}, u32[]{:S(2)}) collective-permute-start(bf16[2,128,128]{2,1,0:T(8,128)(2,1)S(1)} %get-tuple-element.34), channel_id=1, source_target_pairs={{0,16},{4,20},{8,24},{12,28},{16,0},{20,4},{24,8},{28,12},{1,17},{... | collective-permute-start | bytes 196616 | tf_op jit(solution)/shard_map/ppermute | solution.py:30
  41.6 8.5 %collective-permute-start.8 = (bf16[528,128]{1,0:T(8,128)(2,1)S(1)}, bf16[528,128]{1,0:T(8,128)(2,1)S(1)}, u32[]{:S(2)}, u32[]{:S(2)}) collective-permute-start(bf16[528,128]{1,0:T(8,128)(2,1)S(1)} %pad_maximum_fusion), channel_id=1, source_target_pairs={{0,1},{1,2},{2,3},{3,0},{4,5},{5,6},{6,7},{7,4},{8,9},{9,10},{10,1... | collective-permute-start | bytes 405512 | tf_op jit(solution)/shard_map/ppermute | solution.py:25
  46.8 6.5 %collective-permute-start.11 = (bf16[4,128,128]{2,1,0:T(8,128)(2,1)S(1)}, bf16[4,128,128]{2,1,0:T(8,128)(2,1)S(1)}, u32[]{:S(2)}, u32[]{:S(2)}) collective-permute-start(bf16[4,128,128]{2,1,0:T(8,128)(2,1)S(1)} %pad_maximum_fusion.2), channel_id=1, source_target_pairs={{0,1},{1,2},{2,3},{3,0},{4,5},{5,6},{6,7},{7,4},{8,9},{9,10},{10,1... | collective-permute-start | bytes 393224 | tf_op jit(solution)/shard_map/ppermute | solution.py:25

commit v5 on v4

--- a/solution.py
+++ b/solution.py
@@ -84,8 +84,8 @@
     out_refs, (patch_ref, wave_ref, grad_ref) = refs[:chips], refs[chips:]
     chip, core = ints_ref[0], ints_ref[1]
     unit = 1.0 / (ENTRY_SCALE * ENTRY_SCALE * win)
-    for p in range(chips):
-        patch_ref[CORES * (chip ^ p) + core] = own_refs[p][...]
+    for p, own_ref in zip(reversed(range(chips)), own_refs):
+        patch_ref[CORES * (chip ^ p) + core] = own_ref[...]
     for other_ref, group in zip(other_refs, groups):
         for place, p in enumerate(group):
             patch_ref[CORES * (chip ^ p) + 1 - core] = other_ref[2 * place : 2 * place + 2]
@@ -258,7 +258,7 @@
     own_blocks = [merged[0]] + [None] * (chips - 1)
     for p in order:
         own_blocks[p] = crossed(merged[p], p)
-    swaps = [near] + [[p] for p in far]
+    swaps = [[p] for p in order] + [[0]]
     other_blocks = [swapped(joined(own_blocks, group)) for group in swaps]
 
     grads = pl.pallas_call(
@@ -272,11 +272,13 @@
             pltpu.VMEM((CORES * chips, 2, win, win), BF16),
         ],
         compiler_params=LARGE,
-    )(ints, weight, left_matrix, right_matrix, probe, hcos, hsin, target, *own_blocks, *other_blocks)
+    )(ints, weight, left_matrix, right_matrix, probe, hcos, hsin, target, *own_blocks[::-1], *other_blocks)
 
     mine = [grads[0]] + [None] * (chips - 1)
     for p in order:
         mine[p] = crossed(grads[p], p)
+    for p in near[1:]:
+        mine[p], mine[far[-1]] = lax.optimization_barrier((mine[p], mine[far[-1]]))
     size = len(near) * 2 * win
     first = jnp.concatenate([mine[p].reshape(2 * win, win) for p in near] + [note], 0)
     first = passed_round(first, "tile", 1)

time: 55.1 us -> 54.2 us (0.984)
  waiting for transfers between devices: 16.3 us -> 15.6 us
    ppermute x3, starting transfers between devices: 8.83 us -> 7.37 us  [passed_round(): lax.ppermute(block, axis, [(i, (i + distance) % size) for i in range(size)])]
    ppermute x6, waiting for transfers between devices: 9.36 us -> 8.16 us  [crossed(): lax.ppermute(block, 'cuts', [(i, i ^ CORES * distance) for i in range(siz...]
    ppermute x6, starting transfers between devices: 8 us -> 8.9 us  [crossed(): lax.ppermute(block, 'cuts', [(i, i ^ CORES * distance) for i in range(siz...]
    ppermute x3, waiting for transfers between devices: 5.66 us -> 6.54 us  [passed_round(): lax.ppermute(block, axis, [(i, (i + distance) % size) for i in range(size)])]
    ppermute x3 -> x4, waiting for transfers between devices: 1.25 us -> 0.9 us  [swapped(): return lax.ppermute(block, 'cuts', [(i, i ^ 1) for i in range(size)])]
  transfers between devices with their start and end apart: 12 -> 13, of which waited for: 9 -> 9; matrix products, arithmetic and copies ran while one was open for 5% -> 5% of each run, Pallas kernels for 3% -> 3%
where the time goes in v5:
time: 54.2 us; the launch traced here: 54 us
  starting transfers between devices  16.8 us (31%)
  waiting for transfers between devices  15.6 us (29%)
  Pallas kernels  15.1 us (28%)
  other arithmetic  2.96 us (5%)
  local copies, waits for them, and re-layouts  2.81 us (5%)
  between operations  0.79 us (1%)
    pallas_call x1, Pallas kernels, local(): pl.pallas_call(functools.partial(window_kernel, chips, modes, win, swaps)...  11.3 us
    ppermute x6, starting transfers between devices, crossed(): lax.ppermute(block, 'cuts', [(i, i ^ CORES * distance) for i in range(siz...  8.9 us
    ppermute x6, waiting for transfers between devices, crossed(): lax.ppermute(block, 'cuts', [(i, i ^ CORES * distance) for i in range(siz...  8.16 us
    ppermute x3, starting transfers between devices, passed_round(): lax.ppermute(block, axis, [(i, (i + distance) % size) for i in range(size)])  7.37 us
    ppermute x3, waiting for transfers between devices, passed_round(): lax.ppermute(block, axis, [(i, (i + distance) % size) for i in range(size)])  6.54 us
    pallas_call x2, Pallas kernels, placed(): pl.pallas_call(functools.partial(place_kernel, chips, slots, win, groups,...  2.35 us
    unnamed x14, local copies, waits for them, and re-layouts  1.55 us
    another operation x1, other arithmetic, local(): place = jnp.stack([row_offsets[slot], col_offsets[slot]])  1.32 us
  transfers between devices with their start and end apart: 13, of which 9 were waited for; matrix products, arithmetic and copies ran while one was open for 5% of the time, Pallas kernels for 3%

profile of v5, /device:TPU:0, one launch (start us, length us, event | category | flops | bytes accessed | tf_op | source)
XLA Modules:
  0.0 54.0 jit_solution(16713202692679322107)
XLA Ops:
  0.0 1.3 %convert_bitcast_fusion.own_ref = bf16[2,768,128]{2,1,0:T(8,128)(2,1)S(1)} fusion(f32[1,2,768,128]{3,2,1,0:T(8,128)} %param.9), kind=kLoop, calls=%fused_computation | loop fusion | flops 196608 | bytes 1179648 | tf_op jit(solution)/shard_map/convert_element_type | solution.py:223
  1.3 3.9 %collective-permute-start = (bf16[2,768,128]{2,1,0:T(8,128)(2,1)S(1)}, bf16[2,768,128]{2,1,0:T(8,128)(2,1)S(1)}, u32[]{:S(2)}, u32[]{:S(2)}) collective-permute-start(bf16[2,768,128]{2,1,0:T(8,128)(2,1)S(1)} %convert_bitcast_fusion.own_ref), channel_id=1, source_target_pairs={{0,3},{1,0},{2,1},{3,2},{4,7},{5,4},{6,5},{7,6},{8,11},{9,8},{10,9... | collective-permute-start | bytes 1179656 | tf_op jit(solution)/shard_map/ppermute | solution.py:25
  5.2 0.7 %copy-done.4 = s32[4]{0:T(128)S(1)} copy-done((s32[4]{0:T(128)S(1)}, s32[4]{0:T(128)}, u32[]{:S(2)}) %copy-start.4) | copy-done | bytes 40
  7.2 1.3 %pad_add_fusion.1.place_ref = s32[2]{0:T(128)S(1)} fusion(s32[1]{0:T(128)} %dynamic_slice.11, s32[1]{0:T(128)} %dynamic_slice.10), kind=kLoop, calls=%fused_computation.28 | loop fusion | flops 2 | bytes 16 | tf_op jit(solution)/shard_map/stack | solution.py:229
  9.3 0.7 %shard_map.91.refs_4_ = bf16[4,2,128,128]{3,2,1,0:T(8,128)(2,1)S(1)} custom-call(s32[2]{0:T(128)S(1)} %pad_add_fusion.1.place_ref, f32[4,2,128,128]{3,2,1,0:T(8,128)S(1)} %copy-done.1), custom_call_target="tpu_custom_call" | custom-call | tf_op jit(solution)/shard_map/pallas_call | solution.py:230
  10.1 0.8 %copy-done.6 = f32[128,128]{1,0:T(8,128)S(1)} copy-done((f32[128,128]{1,0:T(8,128)S(1)}, f32[128,128]{1,0:T(8,128)}, u32[]{:S(2)}) %copy-start.6) | copy-done | bytes 65560
  11.1 2.5 %collective-permute-done.beside_ref = bf16[2,768,128]{2,1,0:T(8,128)(2,1)S(1)} collective-permute-done((bf16[2,768,128]{2,1,0:T(8,128)(2,1)S(1)}, bf16[2,768,128]{2,1,0:T(8,128)(2,1)S(1)}, u32[]{:S(2)}, u32[]{:S(2)}) %collective-permute-start) | collective-permute-done | bytes 393248 | tf_op jit(solution)/shard_map/ppermute | solution.py:25
  13.6 0.7 %shard_map.92 = (bf16[2,128,128]{2,1,0:T(8,128)(2,1)S(1)}, bf16[2,128,128]{2,1,0:T(8,128)(2,1)S(1)}, bf16[2,128,128]{2,1,0:T(8,128)(2,1)S(1)}, bf16[2,128,128]{2,1,0:T(8,128)(2,1)S(1)}) custom-call(s32[3]{0:T(128)S(1)} %pad_add_fusion.ints_ref.refs_0_, s32[4]{0:T(128)S(1)} %copy-done.5, s32[4]{0:T(128)S(1)} %copy-done.4, ...), custom_call_target="tpu_custom_call" | custom-call | tf_op jit(solution)/shard_map/pallas_call | solution.py:251
  14.3 3.7 %collective-permute-start.1 = (bf16[2,128,128]{2,1,0:T(8,128)(2,1)S(1)}, bf16[2,128,128]{2,1,0:T(8,128)(2,1)S(1)}, u32[]{:S(2)}, u32[]{:S(2)}) collective-permute-start(bf16[2,128,128]{2,1,0:T(8,128)(2,1)S(1)} %get-tuple-element.28), channel_id=1, source_target_pairs={{0,24},{4,28},{8,16},{12,20},{16,8},{20,12},{24,0},{28,4},{1,25},{... | collective-permute-start | bytes 196616 | tf_op jit(solution)/shard_map/ppermute | solution.py:30
  18.0 0.7 %collective-permute-start.3 = (bf16[2,128,128]{2,1,0:T(8,128)(2,1)S(1)}, bf16[2,128,128]{2,1,0:T(8,128)(2,1)S(1)}, u32[]{:S(2)}, u32[]{:S(2)}) collective-permute-start(bf16[2,128,128]{2,1,0:T(8,128)(2,1)S(1)} %get-tuple-element.30), channel_id=1, source_target_pairs={{0,8},{4,12},{8,0},{12,4},{16,24},{20,28},{24,16},{28,20},{1,9},{5... | collective-permute-start | bytes 196616 | tf_op jit(solution)/shard_map/ppermute | solution.py:30
  18.8 1.9 %collective-permute-done.1.refs_8_ = bf16[2,128,128]{2,1,0:T(8,128)(2,1)S(1)} collective-permute-done((bf16[2,128,128]{2,1,0:T(8,128)(2,1)S(1)}, bf16[2,128,128]{2,1,0:T(8,128)(2,1)S(1)}, u32[]{:S(2)}, u32[]{:S(2)}) %collective-permute-start.1) | collective-permute-done | bytes 65568 | tf_op jit(solution)/shard_map/ppermute | solution.py:30
  20.7 2.7 %collective-permute-done.2.refs_9_ = bf16[2,128,128]{2,1,0:T(8,128)(2,1)S(1)} collective-permute-done((bf16[2,128,128]{2,1,0:T(8,128)(2,1)S(1)}, bf16[2,128,128]{2,1,0:T(8,128)(2,1)S(1)}, u32[]{:S(2)}, u32[]{:S(2)}) %collective-permute-start.2) | collective-permute-done | bytes 65568 | tf_op jit(solution)/shard_map/ppermute | solution.py:30
  23.9 0.7 %collective-permute-done.5.refs_13_ = bf16[2,128,128]{2,1,0:T(8,128)(2,1)S(1)} collective-permute-done((bf16[2,128,128]{2,1,0:T(8,128)(2,1)S(1)}, bf16[2,128,128]{2,1,0:T(8,128)(2,1)S(1)}, u32[]{:S(2)}, u32[]{:S(2)}) %collective-permute-start.5) | collective-permute-done | bytes 65568 | tf_op jit(solution)/shard_map/ppermute | solution.py:35
  24.8 11.3 %shard_map.93 = (bf16[2,128,128]{2,1,0:T(8,128)(2,1)S(1)}, bf16[2,128,128]{2,1,0:T(8,128)(2,1)S(1)}, bf16[2,128,128]{2,1,0:T(8,128)(2,1)S(1)}, bf16[2,128,128]{2,1,0:T(8,128)(2,1)S(1)}) custom-call(s32[3]{0:T(128)S(1)} %pad_add_fusion.ints_ref.refs_0_, f32[1]{0:T(128)S(6)} %convert_element_type.17.refs_1_, bf16[256,256]{1,0:T(8,128)(2,1)S(1)} %copy-done.3, ...), custom_call_target="tpu_custom_call" | custom-call | tf_op jit(solution)/shard_map/pallas_call | solution.py:264
  36.4 2.5 %collective-permute-start.9 = (bf16[2,128,128]{2,1,0:T(8,128)(2,1)S(1)}, bf16[2,128,128]{2,1,0:T(8,128)(2,1)S(1)}, u32[]{:S(2)}, u32[]{:S(2)}) collective-permute-start(bf16[2,128,128]{2,1,0:T(8,128)(2,1)S(1)} %get-tuple-element.34), channel_id=1, source_target_pairs={{0,16},{4,20},{8,24},{12,28},{16,0},{20,4},{24,8},{28,12},{1,17},{... | collective-permute-start | bytes 196616 | tf_op jit(solution)/shard_map/ppermute | solution.py:30
  38.9 1.6 %collective-permute-start.11 = (bf16[2,128,128]{2,1,0:T(8,128)(2,1)S(1)}, bf16[2,128,128]{2,1,0:T(8,128)(2,1)S(1)}, u32[]{:S(2)}, u32[]{:S(2)}) collective-permute-start(bf16[2,128,128]{2,1,0:T(8,128)(2,1)S(1)} %get-tuple-element.37), channel_id=1, source_target_pairs={{0,24},{4,28},{8,16},{12,20},{16,8},{20,12},{24,0},{28,4},{1,25},{... | collective-permute-start | bytes 196616 | tf_op jit(solution)/shard_map/ppermute | solution.py:30
  40.5 1.0 %collective-permute-done.8.refs_4_ = bf16[2,128,128]{2,1,0:T(8,128)(2,1)S(1)} collective-permute-done((bf16[2,128,128]{2,1,0:T(8,128)(2,1)S(1)}, bf16[2,128,128]{2,1,0:T(8,128)(2,1)S(1)}, u32[]{:S(2)}, u32[]{:S(2)}) %collective-permute-start.8) | collective-permute-done | bytes 65568 | tf_op jit(solution)/shard_map/ppermute | solution.py:30
  41.6 2.5 %collective-permute-done.9.refs_5_ = bf16[2,128,128]{2,1,0:T(8,128)(2,1)S(1)} collective-permute-done((bf16[2,128,128]{2,1,0:T(8,128)(2,1)S(1)}, bf16[2,128,128]{2,1,0:T(8,128)(2,1)S(1)}, u32[]{:S(2)}, u32[]{:S(2)}) %collective-permute-start.9) | collective-permute-done | bytes 65568 | tf_op jit(solution)/shard_map/ppermute | solution.py:30
  44.1 2.4 %collective-permute-start.10 = (bf16[528,128]{1,0:T(8,128)(2,1)S(1)}, bf16[528,128]{1,0:T(8,128)(2,1)S(1)}, u32[]{:S(2)}, u32[]{:S(2)}) collective-permute-start(bf16[528,128]{1,0:T(8,128)(2,1)S(1)} %pad_maximum_fusion), channel_id=1, source_target_pairs={{0,1},{1,2},{2,3},{3,0},{4,5},{5,6},{6,7},{7,4},{8,9},{9,10},{10,1... | collective-permute-start | bytes 405512 | tf_op jit(solution)/shard_map/ppermute | solution.py:25
  46.6 1.0 %collective-permute-start.12 = (bf16[4,128,128]{2,1,0:T(8,128)(2,1)S(1)}, bf16[4,128,128]{2,1,0:T(8,128)(2,1)S(1)}, u32[]{:S(2)}, u32[]{:S(2)}) collective-permute-start(bf16[4,128,128]{2,1,0:T(8,128)(2,1)S(1)} %pad_maximum_fusion.1), channel_id=1, source_target_pairs={{0,1},{1,2},{2,3},{3,0},{4,5},{5,6},{6,7},{7,4},{8,9},{9,10},{10,1... | collective-permute-start | bytes 393224 | tf_op jit(solution)/shard_map/ppermute | solution.py:25
  47.6 0.8 %shard_map.94.refs_5_ = f32[2,768,128]{2,1,0:T(8,128)S(1)} custom-call(s32[3]{0:T(128)S(1)} %pad_add_fusion.ints_ref.refs_0_, s32[4]{0:T(128)S(1)} %copy-done.5, s32[4]{0:T(128)S(1)} %copy-done.4, bf16[2,128,128]{2,1,0:T(8,128)(2,1)S(1)} %get-tuple-element.32.refs_3_, bf16[2,128,128]{2,1,0:T(8,128)(2,1)S(1)} %collective-permute-done.8.refs_4_, ...), custom_call_target="tpu_custom_call" | custom-call | tf_op jit(solution)/shard_map/pallas_call | solution.py:291
  48.4 2.4 %collective-permute-done.10 = bf16[528,128]{1,0:T(8,128)(2,1)S(1)} collective-permute-done((bf16[528,128]{1,0:T(8,128)(2,1)S(1)}, bf16[528,128]{1,0:T(8,128)(2,1)S(1)}, u32[]{:S(2)}, u32[]{:S(2)}) %collective-permute-start.10) | collective-permute-done | bytes 135200 | tf_op jit(solution)/shard_map/ppermute | solution.py:25
  50.8 1.7 %collective-permute-done.12.refs_4_ = bf16[4,128,128]{2,1,0:T(8,128)(2,1)S(1)} collective-permute-done((bf16[4,128,128]{2,1,0:T(8,128)(2,1)S(1)}, bf16[4,128,128]{2,1,0:T(8,128)(2,1)S(1)}, u32[]{:S(2)}, u32[]{:S(2)}) %collective-permute-start.12) | collective-permute-done | bytes 131104 | tf_op jit(solution)/shard_map/ppermute | solution.py:25
  52.5 1.5 %shard_map.95 = f32[2,768,128]{2,1,0:T(8,128)} custom-call(s32[3]{0:T(128)S(1)} %pad_add_fusion.ints_ref.refs_0_, s32[4]{0:T(128)S(1)} %get-tuple-element.42.refs_1_, s32[4]{0:T(128)S(1)} %get-tuple-element.41.refs_2_, bf16[4,128,128]{2,1,0:T(8,128)(2,1)S(1)} %bitcast.21, bf16[4,128,128]{2,1,0:T(8,128)(2,1)S(1)} %collective-permute-done.12.refs_4_, ...), custom_call_target="tpu_custom_call" | custom-call | tf_op jit(solution)/shard_map/pallas_call | solution.py:291
  (36 shorter events, 2.8 us)
Async XLA Ops:
  0.0 10.0 %copy-start = (f32[4,128,128]{2,1,0:T(8,128)S(1)}, f32[4,128,128]{2,1,0:T(8,128)}, u32[]{:S(2)}) copy-start(f32[4,128,128]{2,1,0:T(8,128)} %param.12) | copy-start | bytes 786436
  0.0 9.3 %copy-start.1 = (f32[4,2,128,128]{3,2,1,0:T(8,128)S(1)}, f32[4,2,128,128]{3,2,1,0:T(8,128)}, u32[]{:S(2)}) copy-start(f32[4,2,128,128]{3,2,1,0:T(8,128)} %probe_ref.1) | copy-start | bytes 1572868
  1.3 12.3 %collective-permute-start = (bf16[2,768,128]{2,1,0:T(8,128)(2,1)S(1)}, bf16[2,768,128]{2,1,0:T(8,128)(2,1)S(1)}, u32[]{:S(2)}, u32[]{:S(2)}) collective-permute-start(bf16[2,768,128]{2,1,0:T(8,128)(2,1)S(1)} %convert_bitcast_fusion.own_ref), channel_id=1, source_target_pairs={{0,3},{1,0},{2,1},{3,2},{4,7},{5,4},{6,5},{7,6},{8,11},{9,8},{10,9... | collective-permute-start | bytes 1179656 | tf_op jit(solution)/shard_map/ppermute | solution.py:25
  5.2 0.7 %copy-start.4 = (s32[4]{0:T(128)S(1)}, s32[4]{0:T(128)}, u32[]{:S(2)}) copy-start(s32[4]{0:T(128)} %refs_2_.2) | copy-start | bytes 52
  5.9 0.7 %copy-start.5 = (s32[4]{0:T(128)S(1)}, s32[4]{0:T(128)}, u32[]{:S(2)}) copy-start(s32[4]{0:T(128)} %refs_1_.1) | copy-start | bytes 52
  10.0 0.8 %copy-start.6 = (f32[128,128]{1,0:T(8,128)S(1)}, f32[128,128]{1,0:T(8,128)}, u32[]{:S(2)}) copy-start(f32[128,128]{1,0:T(8,128)} %param.11) | copy-start | bytes 196612
  13.6 11.2 %copy-start.2 = (bf16[256,256]{1,0:T(8,128)(2,1)S(1)}, bf16[256,256]{1,0:T(8,128)(2,1)}, u32[]{:S(2)}) copy-start(bf16[256,256]{1,0:T(8,128)(2,1)} %constant.86.clone.refs_3_) | copy-start | bytes 393220
  13.6 11.2 %copy-start.3 = (bf16[256,256]{1,0:T(8,128)(2,1)S(1)}, bf16[256,256]{1,0:T(8,128)(2,1)}, u32[]{:S(2)}) copy-start(bf16[256,256]{1,0:T(8,128)(2,1)} %constant.85.clone.refs_2_) | copy-start | bytes 393220
  14.3 6.4 %collective-permute-start.1 = (bf16[2,128,128]{2,1,0:T(8,128)(2,1)S(1)}, bf16[2,128,128]{2,1,0:T(8,128)(2,1)S(1)}, u32[]{:S(2)}, u32[]{:S(2)}) collective-permute-start(bf16[2,128,128]{2,1,0:T(8,128)(2,1)S(1)} %get-tuple-element.28), channel_id=1, source_target_pairs={{0,24},{4,28},{8,16},{12,20},{16,8},{20,12},{24,0},{28,4},{1,25},{... | collective-permute-start | bytes 196616 | tf_op jit(solution)/shard_map/ppermute | solution.py:30
  18.0 5.4 %collective-permute-start.2 = (bf16[2,128,128]{2,1,0:T(8,128)(2,1)S(1)}, bf16[2,128,128]{2,1,0:T(8,128)(2,1)S(1)}, u32[]{:S(2)}, u32[]{:S(2)}) collective-permute-start(bf16[2,128,128]{2,1,0:T(8,128)(2,1)S(1)} %get-tuple-element.29), channel_id=1, source_target_pairs={{0,16},{4,20},{8,24},{12,28},{16,0},{20,4},{24,8},{28,12},{1,17},{... | collective-permute-start | bytes 196616 | tf_op jit(solution)/shard_map/ppermute | solution.py:30
  18.0 5.4 %collective-permute-start.3 = (bf16[2,128,128]{2,1,0:T(8,128)(2,1)S(1)}, bf16[2,128,128]{2,1,0:T(8,128)(2,1)S(1)}, u32[]{:S(2)}, u32[]{:S(2)}) collective-permute-start(bf16[2,128,128]{2,1,0:T(8,128)(2,1)S(1)} %get-tuple-element.30), channel_id=1, source_target_pairs={{0,8},{4,12},{8,0},{12,4},{16,24},{20,28},{24,16},{28,20},{1,9},{5... | collective-permute-start | bytes 196616 | tf_op jit(solution)/shard_map/ppermute | solution.py:30
  18.8 5.1 %collective-permute-start.7 = (bf16[2,128,128]{2,1,0:T(8,128)(2,1)S(1)}, bf16[2,128,128]{2,1,0:T(8,128)(2,1)S(1)}, u32[]{:S(2)}, u32[]{:S(2)}) collective-permute-start(bf16[2,128,128]{2,1,0:T(8,128)(2,1)S(1)} %get-tuple-element.31.refs_11_), channel_id=1, source_target_pairs={{0,4},{4,0},{8,12},{12,8},{16,20},{20,16},{24,28},{28,24},{1,5},{5... | collective-permute-start | bytes 196616 | tf_op jit(solution)/shard_map/ppermute | solution.py:35
  20.7 3.2 %collective-permute-start.4 = (bf16[2,128,128]{2,1,0:T(8,128)(2,1)S(1)}, bf16[2,128,128]{2,1,0:T(8,128)(2,1)S(1)}, u32[]{:S(2)}, u32[]{:S(2)}) collective-permute-start(bf16[2,128,128]{2,1,0:T(8,128)(2,1)S(1)} %collective-permute-done.1.refs_8_), channel_id=1, source_target_pairs={{0,4},{4,0},{8,12},{12,8},{16,20},{20,16},{24,28},{28,24},{1,5},{5... | collective-permute-start | bytes 196616 | tf_op jit(solution)/shard_map/ppermute | solution.py:35
  23.4 1.3 %collective-permute-start.5 = (bf16[2,128,128]{2,1,0:T(8,128)(2,1)S(1)}, bf16[2,128,128]{2,1,0:T(8,128)(2,1)S(1)}, u32[]{:S(2)}, u32[]{:S(2)}) collective-permute-start(bf16[2,128,128]{2,1,0:T(8,128)(2,1)S(1)} %collective-permute-done.2.refs_9_), channel_id=1, source_target_pairs={{0,4},{4,0},{8,12},{12,8},{16,20},{20,16},{24,28},{28,24},{1,5},{5... | collective-permute-start | bytes 196616 | tf_op jit(solution)/shard_map/ppermute | solution.py:35
  23.4 1.4 %collective-permute-start.6 = (bf16[2,128,128]{2,1,0:T(8,128)(2,1)S(1)}, bf16[2,128,128]{2,1,0:T(8,128)(2,1)S(1)}, u32[]{:S(2)}, u32[]{:S(2)}) collective-permute-start(bf16[2,128,128]{2,1,0:T(8,128)(2,1)S(1)} %collective-permute-done.3.refs_10_), channel_id=1, source_target_pairs={{0,4},{4,0},{8,12},{12,8},{16,20},{20,16},{24,28},{28,24},{1,5},{5... | collective-permute-start | bytes 196616 | tf_op jit(solution)/shard_map/ppermute | solution.py:35
  36.1 5.5 %collective-permute-start.8 = (bf16[2,128,128]{2,1,0:T(8,128)(2,1)S(1)}, bf16[2,128,128]{2,1,0:T(8,128)(2,1)S(1)}, u32[]{:S(2)}, u32[]{:S(2)}) collective-permute-start(bf16[2,128,128]{2,1,0:T(8,128)(2,1)S(1)} %get-tuple-element.33), channel_id=1, source_target_pairs={{0,8},{4,12},{8,0},{12,4},{16,24},{20,28},{24,16},{28,20},{1,9},{5... | collective-permute-start | bytes 196616 | tf_op jit(solution)/shard_map/ppermute | solution.py:30
  36.4 7.7 %collective-permute-start.9 = (bf16[2,128,128]{2,1,0:T(8,128)(2,1)S(1)}, bf16[2,128,128]{2,1,0:T(8,128)(2,1)S(1)}, u32[]{:S(2)}, u32[]{:S(2)}) collective-permute-start(bf16[2,128,128]{2,1,0:T(8,128)(2,1)S(1)} %get-tuple-element.34), channel_id=1, source_target_pairs={{0,16},{4,20},{8,24},{12,28},{16,0},{20,4},{24,8},{28,12},{1,17},{... | collective-permute-start | bytes 196616 | tf_op jit(solution)/shard_map/ppermute | solution.py:30
  38.9 7.6 %collective-permute-start.11 = (bf16[2,128,128]{2,1,0:T(8,128)(2,1)S(1)}, bf16[2,128,128]{2,1,0:T(8,128)(2,1)S(1)}, u32[]{:S(2)}, u32[]{:S(2)}) collective-permute-start(bf16[2,128,128]{2,1,0:T(8,128)(2,1)S(1)} %get-tuple-element.37), channel_id=1, source_target_pairs={{0,24},{4,28},{8,16},{12,20},{16,8},{20,12},{24,0},{28,4},{1,25},{... | collective-permute-start | bytes 196616 | tf_op jit(solution)/shard_map/ppermute | solution.py:30
  44.1 6.6 %collective-permute-start.10 = (bf16[528,128]{1,0:T(8,128)(2,1)S(1)}, bf16[528,128]{1,0:T(8,128)(2,1)S(1)}, u32[]{:S(2)}, u32[]{:S(2)}) collective-permute-start(bf16[528,128]{1,0:T(8,128)(2,1)S(1)} %pad_maximum_fusion), channel_id=1, source_target_pairs={{0,1},{1,2},{2,3},{3,0},{4,5},{5,6},{6,7},{7,4},{8,9},{9,10},{10,1... | collective-permute-start | bytes 405512 | tf_op jit(solution)/shard_map/ppermute | solution.py:25
  46.6 5.9 %collective-permute-start.12 = (bf16[4,128,128]{2,1,0:T(8,128)(2,1)S(1)}, bf16[4,128,128]{2,1,0:T(8,128)(2,1)S(1)}, u32[]{:S(2)}, u32[]{:S(2)}) collective-permute-start(bf16[4,128,128]{2,1,0:T(8,128)(2,1)S(1)} %pad_maximum_fusion.1), channel_id=1, source_target_pairs={{0,1},{1,2},{2,3},{3,0},{4,5},{5,6},{6,7},{7,4},{8,9},{9,10},{10,1... | collective-permute-start | bytes 393224 | tf_op jit(solution)/shard_map/ppermute | solution.py:25

commit v6 on v5

--- a/solution.py
+++ b/solution.py
@@ -277,8 +277,7 @@
     mine = [grads[0]] + [None] * (chips - 1)
     for p in order:
         mine[p] = crossed(grads[p], p)
-    for p in near[1:]:
-        mine[p], mine[far[-1]] = lax.optimization_barrier((mine[p], mine[far[-1]]))
+    far = far[::-1]
     size = len(near) * 2 * win
     first = jnp.concatenate([mine[p].reshape(2 * win, win) for p in near] + [note], 0)
     first = passed_round(first, "tile", 1)

time: 54.2 us -> 53.2 us (0.982)
  waiting for transfers between devices: 15.6 us -> 13.1 us
  starting transfers between devices: 16.8 us -> 18.3 us
    ppermute x3, starting transfers between devices: 7.37 us -> 8.83 us  [passed_round(): lax.ppermute(block, axis, [(i, (i + distance) % size) for i in range(size)])]
    ppermute x6, waiting for transfers between devices: 8.16 us -> 6.7 us  [crossed(): lax.ppermute(block, 'cuts', [(i, i ^ CORES * distance) for i in range(siz...]
    ppermute x3, waiting for transfers between devices: 6.54 us -> 5.49 us  [passed_round(): lax.ppermute(block, axis, [(i, (i + distance) % size) for i in range(size)])]
  transfers between devices with their start and end apart: 13 -> 13, of which waited for: 9 -> 9; matrix products, arithmetic and copies ran while one was open for 5% -> 6% of each run, Pallas kernels for 3% -> 3%
where the time goes in v6:
time: 53.2 us; the launch traced here: 53 us
  starting transfers between devices  18.3 us (34%)
  Pallas kernels  15.1 us (28%)
  waiting for transfers between devices  13.1 us (25%)
  other arithmetic  2.96 us (6%)
  local copies, waits for them, and re-layouts  2.81 us (5%)
  between operations  0.8 us (2%)
    pallas_call x1, Pallas kernels, local(): pl.pallas_call(functools.partial(window_kernel, chips, modes, win, swaps)...  11.3 us
    ppermute x6, starting transfers between devices, crossed(): lax.ppermute(block, 'cuts', [(i, i ^ CORES * distance) for i in range(siz...  8.9 us
    ppermute x3, starting transfers between devices, passed_round(): lax.ppermute(block, axis, [(i, (i + distance) % size) for i in range(size)])  8.83 us
    ppermute x6, waiting for transfers between devices, crossed(): lax.ppermute(block, 'cuts', [(i, i ^ CORES * distance) for i in range(siz...  6.7 us
    ppermute x3, waiting for transfers between devices, passed_round(): lax.ppermute(block, axis, [(i, (i + distance) % size) for i in range(size)])  5.49 us
    pallas_call x2, Pallas kernels, placed(): pl.pallas_call(functools.partial(place_kernel, chips, slots, win, groups,...  2.35 us
    unnamed x14, local copies, waits for them, and re-layouts  1.55 us
    another operation x1, other arithmetic, local(): place = jnp.stack([row_offsets[slot], col_offsets[slot]])  1.32 us
  transfers between devices with their start and end apart: 13, of which 9 were waited for; matrix products, arithmetic and copies ran while one was open for 6% of the time, Pallas kernels for 3%

profile of v6, /device:TPU:0, one launch (start us, length us, event | category | flops | bytes accessed | tf_op | source)
XLA Modules:
  0.0 53.0 jit_solution(10529729143386277450)
XLA Ops:
  0.0 1.3 %convert_bitcast_fusion.own_ref = bf16[2,768,128]{2,1,0:T(8,128)(2,1)S(1)} fusion(f32[1,2,768,128]{3,2,1,0:T(8,128)} %param.9), kind=kLoop, calls=%fused_computation | loop fusion | flops 196608 | bytes 1179648 | tf_op jit(solution)/shard_map/convert_element_type | solution.py:223
  1.3 3.9 %collective-permute-start = (bf16[2,768,128]{2,1,0:T(8,128)(2,1)S(1)}, bf16[2,768,128]{2,1,0:T(8,128)(2,1)S(1)}, u32[]{:S(2)}, u32[]{:S(2)}) collective-permute-start(bf16[2,768,128]{2,1,0:T(8,128)(2,1)S(1)} %convert_bitcast_fusion.own_ref), channel_id=1, source_target_pairs={{0,3},{1,0},{2,1},{3,2},{4,7},{5,4},{6,5},{7,6},{8,11},{9,8},{10,9... | collective-permute-start | bytes 1179656 | tf_op jit(solution)/shard_map/ppermute | solution.py:25
  5.2 0.7 %copy-done.4 = s32[4]{0:T(128)S(1)} copy-done((s32[4]{0:T(128)S(1)}, s32[4]{0:T(128)}, u32[]{:S(2)}) %copy-start.4) | copy-done | bytes 40
  6.5 0.6 %dynamic_slice.10 = s32[1]{0:T(128)} dynamic-slice(s32[4]{0:T(128)S(1)} %copy-done.5, s32[]{:T(128)S(6)} %select_n.41), dynamic_slice_sizes={1} | dynamic-slice | bytes 12 | tf_op jit(solution)/shard_map/dynamic_slice | solution.py:229
  7.2 1.3 %pad_add_fusion.1.place_ref = s32[2]{0:T(128)S(1)} fusion(s32[1]{0:T(128)} %dynamic_slice.11, s32[1]{0:T(128)} %dynamic_slice.10), kind=kLoop, calls=%fused_computation.28 | loop fusion | flops 2 | bytes 16 | tf_op jit(solution)/shard_map/stack | solution.py:229
  9.3 0.7 %shard_map.91.refs_4_ = bf16[4,2,128,128]{3,2,1,0:T(8,128)(2,1)S(1)} custom-call(s32[2]{0:T(128)S(1)} %pad_add_fusion.1.place_ref, f32[4,2,128,128]{3,2,1,0:T(8,128)S(1)} %copy-done.1), custom_call_target="tpu_custom_call" | custom-call | tf_op jit(solution)/shard_map/pallas_call | solution.py:230
  10.1 0.8 %copy-done.6 = f32[128,128]{1,0:T(8,128)S(1)} copy-done((f32[128,128]{1,0:T(8,128)S(1)}, f32[128,128]{1,0:T(8,128)}, u32[]{:S(2)}) %copy-start.6) | copy-done | bytes 65560
  11.1 2.5 %collective-permute-done.beside_ref = bf16[2,768,128]{2,1,0:T(8,128)(2,1)S(1)} collective-permute-done((bf16[2,768,128]{2,1,0:T(8,128)(2,1)S(1)}, bf16[2,768,128]{2,1,0:T(8,128)(2,1)S(1)}, u32[]{:S(2)}, u32[]{:S(2)}) %collective-permute-start) | collective-permute-done | bytes 393248 | tf_op jit(solution)/shard_map/ppermute | solution.py:25
  13.6 0.7 %shard_map.92 = (bf16[2,128,128]{2,1,0:T(8,128)(2,1)S(1)}, bf16[2,128,128]{2,1,0:T(8,128)(2,1)S(1)}, bf16[2,128,128]{2,1,0:T(8,128)(2,1)S(1)}, bf16[2,128,128]{2,1,0:T(8,128)(2,1)S(1)}) custom-call(s32[3]{0:T(128)S(1)} %pad_add_fusion.ints_ref.refs_0_, s32[4]{0:T(128)S(1)} %copy-done.5, s32[4]{0:T(128)S(1)} %copy-done.4, ...), custom_call_target="tpu_custom_call" | custom-call | tf_op jit(solution)/shard_map/pallas_call | solution.py:251
  14.3 3.7 %collective-permute-start.1 = (bf16[2,128,128]{2,1,0:T(8,128)(2,1)S(1)}, bf16[2,128,128]{2,1,0:T(8,128)(2,1)S(1)}, u32[]{:S(2)}, u32[]{:S(2)}) collective-permute-start(bf16[2,128,128]{2,1,0:T(8,128)(2,1)S(1)} %get-tuple-element.26), channel_id=1, source_target_pairs={{0,24},{4,28},{8,16},{12,20},{16,8},{20,12},{24,0},{28,4},{1,25},{... | collective-permute-start | bytes 196616 | tf_op jit(solution)/shard_map/ppermute | solution.py:30
  18.0 0.7 %collective-permute-start.3 = (bf16[2,128,128]{2,1,0:T(8,128)(2,1)S(1)}, bf16[2,128,128]{2,1,0:T(8,128)(2,1)S(1)}, u32[]{:S(2)}, u32[]{:S(2)}) collective-permute-start(bf16[2,128,128]{2,1,0:T(8,128)(2,1)S(1)} %get-tuple-element.28), channel_id=1, source_target_pairs={{0,8},{4,12},{8,0},{12,4},{16,24},{20,28},{24,16},{28,20},{1,9},{5... | collective-permute-start | bytes 196616 | tf_op jit(solution)/shard_map/ppermute | solution.py:30
  18.8 1.9 %collective-permute-done.1.refs_8_ = bf16[2,128,128]{2,1,0:T(8,128)(2,1)S(1)} collective-permute-done((bf16[2,128,128]{2,1,0:T(8,128)(2,1)S(1)}, bf16[2,128,128]{2,1,0:T(8,128)(2,1)S(1)}, u32[]{:S(2)}, u32[]{:S(2)}) %collective-permute-start.1) | collective-permute-done | bytes 65568 | tf_op jit(solution)/shard_map/ppermute | solution.py:30
  20.7 2.7 %collective-permute-done.2.refs_9_ = bf16[2,128,128]{2,1,0:T(8,128)(2,1)S(1)} collective-permute-done((bf16[2,128,128]{2,1,0:T(8,128)(2,1)S(1)}, bf16[2,128,128]{2,1,0:T(8,128)(2,1)S(1)}, u32[]{:S(2)}, u32[]{:S(2)}) %collective-permute-start.2) | collective-permute-done | bytes 65568 | tf_op jit(solution)/shard_map/ppermute | solution.py:30
  23.9 0.7 %collective-permute-done.5.refs_13_ = bf16[2,128,128]{2,1,0:T(8,128)(2,1)S(1)} collective-permute-done((bf16[2,128,128]{2,1,0:T(8,128)(2,1)S(1)}, bf16[2,128,128]{2,1,0:T(8,128)(2,1)S(1)}, u32[]{:S(2)}, u32[]{:S(2)}) %collective-permute-start.5) | collective-permute-done | bytes 65568 | tf_op jit(solution)/shard_map/ppermute | solution.py:35
  24.8 11.3 %shard_map.93 = (bf16[2,128,128]{2,1,0:T(8,128)(2,1)S(1)}, bf16[2,128,128]{2,1,0:T(8,128)(2,1)S(1)}, bf16[2,128,128]{2,1,0:T(8,128)(2,1)S(1)}, bf16[2,128,128]{2,1,0:T(8,128)(2,1)S(1)}) custom-call(s32[3]{0:T(128)S(1)} %pad_add_fusion.ints_ref.refs_0_, f32[1]{0:T(128)S(6)} %convert_element_type.17.refs_1_, bf16[256,256]{1,0:T(8,128)(2,1)S(1)} %copy-done.3, ...), custom_call_target="tpu_custom_call" | custom-call | tf_op jit(solution)/shard_map/pallas_call | solution.py:264
  36.4 2.5 %collective-permute-start.10 = (bf16[2,128,128]{2,1,0:T(8,128)(2,1)S(1)}, bf16[2,128,128]{2,1,0:T(8,128)(2,1)S(1)}, u32[]{:S(2)}, u32[]{:S(2)}) collective-permute-start(bf16[2,128,128]{2,1,0:T(8,128)(2,1)S(1)} %get-tuple-element.33), channel_id=1, source_target_pairs={{0,16},{4,20},{8,24},{12,28},{16,0},{20,4},{24,8},{28,12},{1,17},{... | collective-permute-start | bytes 196616 | tf_op jit(solution)/shard_map/ppermute | solution.py:30
  38.9 1.6 %collective-permute-start.11 = (bf16[2,128,128]{2,1,0:T(8,128)(2,1)S(1)}, bf16[2,128,128]{2,1,0:T(8,128)(2,1)S(1)}, u32[]{:S(2)}, u32[]{:S(2)}) collective-permute-start(bf16[2,128,128]{2,1,0:T(8,128)(2,1)S(1)} %get-tuple-element.34), channel_id=1, source_target_pairs={{0,24},{4,28},{8,16},{12,20},{16,8},{20,12},{24,0},{28,4},{1,25},{... | collective-permute-start | bytes 196616 | tf_op jit(solution)/shard_map/ppermute | solution.py:30
  40.5 1.0 %collective-permute-done.8.refs_4_ = bf16[2,128,128]{2,1,0:T(8,128)(2,1)S(1)} collective-permute-done((bf16[2,128,128]{2,1,0:T(8,128)(2,1)S(1)}, bf16[2,128,128]{2,1,0:T(8,128)(2,1)S(1)}, u32[]{:S(2)}, u32[]{:S(2)}) %collective-permute-start.8) | collective-permute-done | bytes 65568 | tf_op jit(solution)/shard_map/ppermute | solution.py:30
  41.6 2.4 %collective-permute-start.9 = (bf16[528,128]{1,0:T(8,128)(2,1)S(1)}, bf16[528,128]{1,0:T(8,128)(2,1)S(1)}, u32[]{:S(2)}, u32[]{:S(2)}) collective-permute-start(bf16[528,128]{1,0:T(8,128)(2,1)S(1)} %pad_maximum_fusion), channel_id=1, source_target_pairs={{0,1},{1,2},{2,3},{3,0},{4,5},{5,6},{6,7},{7,4},{8,9},{9,10},{10,1... | collective-permute-start | bytes 405512 | tf_op jit(solution)/shard_map/ppermute | solution.py:25
  44.1 1.0 %collective-permute-done.11.refs_6_ = bf16[2,128,128]{2,1,0:T(8,128)(2,1)S(1)} collective-permute-done((bf16[2,128,128]{2,1,0:T(8,128)(2,1)S(1)}, bf16[2,128,128]{2,1,0:T(8,128)(2,1)S(1)}, u32[]{:S(2)}, u32[]{:S(2)}) %collective-permute-start.11) | collective-permute-done | bytes 65568 | tf_op jit(solution)/shard_map/ppermute | solution.py:30
  45.1 2.4 %collective-permute-start.12 = (bf16[4,128,128]{2,1,0:T(8,128)(2,1)S(1)}, bf16[4,128,128]{2,1,0:T(8,128)(2,1)S(1)}, u32[]{:S(2)}, u32[]{:S(2)}) collective-permute-start(bf16[4,128,128]{2,1,0:T(8,128)(2,1)S(1)} %pad_maximum_fusion.1), channel_id=1, source_target_pairs={{0,1},{1,2},{2,3},{3,0},{4,5},{5,6},{6,7},{7,4},{8,9},{9,10},{10,1... | collective-permute-start | bytes 393224 | tf_op jit(solution)/shard_map/ppermute | solution.py:25
  47.6 0.8 %shard_map.94.refs_5_ = f32[2,768,128]{2,1,0:T(8,128)S(1)} custom-call(s32[3]{0:T(128)S(1)} %pad_add_fusion.ints_ref.refs_0_, s32[4]{0:T(128)S(1)} %copy-done.5, s32[4]{0:T(128)S(1)} %copy-done.4, bf16[2,128,128]{2,1,0:T(8,128)(2,1)S(1)} %get-tuple-element.30.refs_3_, bf16[2,128,128]{2,1,0:T(8,128)(2,1)S(1)} %collective-permute-done.8.refs_4_, ...), custom_call_target="tpu_custom_call" | custom-call | tf_op jit(solution)/shard_map/pallas_call | solution.py:290
  48.4 3.0 %collective-permute-done.12.refs_4_ = bf16[4,128,128]{2,1,0:T(8,128)(2,1)S(1)} collective-permute-done((bf16[4,128,128]{2,1,0:T(8,128)(2,1)S(1)}, bf16[4,128,128]{2,1,0:T(8,128)(2,1)S(1)}, u32[]{:S(2)}, u32[]{:S(2)}) %collective-permute-start.12) | collective-permute-done | bytes 131104 | tf_op jit(solution)/shard_map/ppermute | solution.py:25
  51.5 1.5 %shard_map.95 = f32[2,768,128]{2,1,0:T(8,128)} custom-call(s32[3]{0:T(128)S(1)} %pad_add_fusion.ints_ref.refs_0_, s32[4]{0:T(128)S(1)} %get-tuple-element.38.refs_1_, s32[4]{0:T(128)S(1)} %get-tuple-element.37.refs_2_, bf16[4,128,128]{2,1,0:T(8,128)(2,1)S(1)} %bitcast.21, bf16[4,128,128]{2,1,0:T(8,128)(2,1)S(1)} %collective-permute-done.12.refs_4_, ...), custom_call_target="tpu_custom_call" | custom-call | tf_op jit(solution)/shard_map/pallas_call | solution.py:290
  (36 shorter events, 2.2 us)
Async XLA Ops:
  0.0 10.0 %copy-start = (f32[4,128,128]{2,1,0:T(8,128)S(1)}, f32[4,128,128]{2,1,0:T(8,128)}, u32[]{:S(2)}) copy-start(f32[4,128,128]{2,1,0:T(8,128)} %param.12) | copy-start | bytes 786436
  0.0 9.3 %copy-start.1 = (f32[4,2,128,128]{3,2,1,0:T(8,128)S(1)}, f32[4,2,128,128]{3,2,1,0:T(8,128)}, u32[]{:S(2)}) copy-start(f32[4,2,128,128]{3,2,1,0:T(8,128)} %probe_ref.1) | copy-start | bytes 1572868
  1.3 12.3 %collective-permute-start = (bf16[2,768,128]{2,1,0:T(8,128)(2,1)S(1)}, bf16[2,768,128]{2,1,0:T(8,128)(2,1)S(1)}, u32[]{:S(2)}, u32[]{:S(2)}) collective-permute-start(bf16[2,768,128]{2,1,0:T(8,128)(2,1)S(1)} %convert_bitcast_fusion.own_ref), channel_id=1, source_target_pairs={{0,3},{1,0},{2,1},{3,2},{4,7},{5,4},{6,5},{7,6},{8,11},{9,8},{10,9... | collective-permute-start | bytes 1179656 | tf_op jit(solution)/shard_map/ppermute | solution.py:25
  5.2 0.7 %copy-start.4 = (s32[4]{0:T(128)S(1)}, s32[4]{0:T(128)}, u32[]{:S(2)}) copy-start(s32[4]{0:T(128)} %refs_2_.2) | copy-start | bytes 52
  5.9 0.7 %copy-start.5 = (s32[4]{0:T(128)S(1)}, s32[4]{0:T(128)}, u32[]{:S(2)}) copy-start(s32[4]{0:T(128)} %refs_1_.1) | copy-start | bytes 52
  10.0 0.8 %copy-start.6 = (f32[128,128]{1,0:T(8,128)S(1)}, f32[128,128]{1,0:T(8,128)}, u32[]{:S(2)}) copy-start(f32[128,128]{1,0:T(8,128)} %param.11) | copy-start | bytes 196612
  13.6 11.2 %copy-start.2 = (bf16[256,256]{1,0:T(8,128)(2,1)S(1)}, bf16[256,256]{1,0:T(8,128)(2,1)}, u32[]{:S(2)}) copy-start(bf16[256,256]{1,0:T(8,128)(2,1)} %constant.86.clone.refs_3_) | copy-start | bytes 393220
  13.6 11.2 %copy-start.3 = (bf16[256,256]{1,0:T(8,128)(2,1)S(1)}, bf16[256,256]{1,0:T(8,128)(2,1)}, u32[]{:S(2)}) copy-start(bf16[256,256]{1,0:T(8,128)(2,1)} %constant.85.clone.refs_2_) | copy-start | bytes 393220
  14.3 6.4 %collective-permute-start.1 = (bf16[2,128,128]{2,1,0:T(8,128)(2,1)S(1)}, bf16[2,128,128]{2,1,0:T(8,128)(2,1)S(1)}, u32[]{:S(2)}, u32[]{:S(2)}) collective-permute-start(bf16[2,128,128]{2,1,0:T(8,128)(2,1)S(1)} %get-tuple-element.26), channel_id=1, source_target_pairs={{0,24},{4,28},{8,16},{12,20},{16,8},{20,12},{24,0},{28,4},{1,25},{... | collective-permute-start | bytes 196616 | tf_op jit(solution)/shard_map/ppermute | solution.py:30
  18.0 5.4 %collective-permute-start.2 = (bf16[2,128,128]{2,1,0:T(8,128)(2,1)S(1)}, bf16[2,128,128]{2,1,0:T(8,128)(2,1)S(1)}, u32[]{:S(2)}, u32[]{:S(2)}) collective-permute-start(bf16[2,128,128]{2,1,0:T(8,128)(2,1)S(1)} %get-tuple-element.27), channel_id=1, source_target_pairs={{0,16},{4,20},{8,24},{12,28},{16,0},{20,4},{24,8},{28,12},{1,17},{... | collective-permute-start | bytes 196616 | tf_op jit(solution)/shard_map/ppermute | solution.py:30
  18.0 5.4 %collective-permute-start.3 = (bf16[2,128,128]{2,1,0:T(8,128)(2,1)S(1)}, bf16[2,128,128]{2,1,0:T(8,128)(2,1)S(1)}, u32[]{:S(2)}, u32[]{:S(2)}) collective-permute-start(bf16[2,128,128]{2,1,0:T(8,128)(2,1)S(1)} %get-tuple-element.28), channel_id=1, source_target_pairs={{0,8},{4,12},{8,0},{12,4},{16,24},{20,28},{24,16},{28,20},{1,9},{5... | collective-permute-start | bytes 196616 | tf_op jit(solution)/shard_map/ppermute | solution.py:30
  18.8 5.1 %collective-permute-start.7 = (bf16[2,128,128]{2,1,0:T(8,128)(2,1)S(1)}, bf16[2,128,128]{2,1,0:T(8,128)(2,1)S(1)}, u32[]{:S(2)}, u32[]{:S(2)}) collective-permute-start(bf16[2,128,128]{2,1,0:T(8,128)(2,1)S(1)} %get-tuple-element.29.refs_11_), channel_id=1, source_target_pairs={{0,4},{4,0},{8,12},{12,8},{16,20},{20,16},{24,28},{28,24},{1,5},{5... | collective-permute-start | bytes 196616 | tf_op jit(solution)/shard_map/ppermute | solution.py:35
  20.7 3.2 %collective-permute-start.4 = (bf16[2,128,128]{2,1,0:T(8,128)(2,1)S(1)}, bf16[2,128,128]{2,1,0:T(8,128)(2,1)S(1)}, u32[]{:S(2)}, u32[]{:S(2)}) collective-permute-start(bf16[2,128,128]{2,1,0:T(8,128)(2,1)S(1)} %collective-permute-done.1.refs_8_), channel_id=1, source_target_pairs={{0,4},{4,0},{8,12},{12,8},{16,20},{20,16},{24,28},{28,24},{1,5},{5... | collective-permute-start | bytes 196616 | tf_op jit(solution)/shard_map/ppermute | solution.py:35
  23.4 1.3 %collective-permute-start.5 = (bf16[2,128,128]{2,1,0:T(8,128)(2,1)S(1)}, bf16[2,128,128]{2,1,0:T(8,128)(2,1)S(1)}, u32[]{:S(2)}, u32[]{:S(2)}) collective-permute-start(bf16[2,128,128]{2,1,0:T(8,128)(2,1)S(1)} %collective-permute-done.2.refs_9_), channel_id=1, source_target_pairs={{0,4},{4,0},{8,12},{12,8},{16,20},{20,16},{24,28},{28,24},{1,5},{5... | collective-permute-start | bytes 196616 | tf_op jit(solution)/shard_map/ppermute | solution.py:35
  23.4 1.4 %collective-permute-start.6 = (bf16[2,128,128]{2,1,0:T(8,128)(2,1)S(1)}, bf16[2,128,128]{2,1,0:T(8,128)(2,1)S(1)}, u32[]{:S(2)}, u32[]{:S(2)}) collective-permute-start(bf16[2,128,128]{2,1,0:T(8,128)(2,1)S(1)} %collective-permute-done.3.refs_10_), channel_id=1, source_target_pairs={{0,4},{4,0},{8,12},{12,8},{16,20},{20,16},{24,28},{28,24},{1,5},{5... | collective-permute-start | bytes 196616 | tf_op jit(solution)/shard_map/ppermute | solution.py:35
  36.1 5.5 %collective-permute-start.8 = (bf16[2,128,128]{2,1,0:T(8,128)(2,1)S(1)}, bf16[2,128,128]{2,1,0:T(8,128)(2,1)S(1)}, u32[]{:S(2)}, u32[]{:S(2)}) collective-permute-start(bf16[2,128,128]{2,1,0:T(8,128)(2,1)S(1)} %get-tuple-element.31), channel_id=1, source_target_pairs={{0,8},{4,12},{8,0},{12,4},{16,24},{20,28},{24,16},{28,20},{1,9},{5... | collective-permute-start | bytes 196616 | tf_op jit(solution)/shard_map/ppermute | solution.py:30
  36.4 7.7 %collective-permute-start.10 = (bf16[2,128,128]{2,1,0:T(8,128)(2,1)S(1)}, bf16[2,128,128]{2,1,0:T(8,128)(2,1)S(1)}, u32[]{:S(2)}, u32[]{:S(2)}) collective-permute-start(bf16[2,128,128]{2,1,0:T(8,128)(2,1)S(1)} %get-tuple-element.33), channel_id=1, source_target_pairs={{0,16},{4,20},{8,24},{12,28},{16,0},{20,4},{24,8},{28,12},{1,17},{... | collective-permute-start | bytes 196616 | tf_op jit(solution)/shard_map/ppermute | solution.py:30
  38.9 6.2 %collective-permute-start.11 = (bf16[2,128,128]{2,1,0:T(8,128)(2,1)S(1)}, bf16[2,128,128]{2,1,0:T(8,128)(2,1)S(1)}, u32[]{:S(2)}, u32[]{:S(2)}) collective-permute-start(bf16[2,128,128]{2,1,0:T(8,128)(2,1)S(1)} %get-tuple-element.34), channel_id=1, source_target_pairs={{0,24},{4,28},{8,16},{12,20},{16,8},{20,12},{24,0},{28,4},{1,25},{... | collective-permute-start | bytes 196616 | tf_op jit(solution)/shard_map/ppermute | solution.py:30
  41.6 6.8 %collective-permute-start.9 = (bf16[528,128]{1,0:T(8,128)(2,1)S(1)}, bf16[528,128]{1,0:T(8,128)(2,1)S(1)}, u32[]{:S(2)}, u32[]{:S(2)}) collective-permute-start(bf16[528,128]{1,0:T(8,128)(2,1)S(1)} %pad_maximum_fusion), channel_id=1, source_target_pairs={{0,1},{1,2},{2,3},{3,0},{4,5},{5,6},{6,7},{7,4},{8,9},{9,10},{10,1... | collective-permute-start | bytes 405512 | tf_op jit(solution)/shard_map/ppermute | solution.py:25
  45.1 6.3 %collective-permute-start.12 = (bf16[4,128,128]{2,1,0:T(8,128)(2,1)S(1)}, bf16[4,128,128]{2,1,0:T(8,128)(2,1)S(1)}, u32[]{:S(2)}, u32[]{:S(2)}) collective-permute-start(bf16[4,128,128]{2,1,0:T(8,128)(2,1)S(1)} %pad_maximum_fusion.1), channel_id=1, source_target_pairs={{0,1},{1,2},{2,3},{3,0},{4,5},{5,6},{6,7},{7,4},{8,9},{9,10},{10,1... | collective-permute-start | bytes 393224 | tf_op jit(solution)/shard_map/ppermute | solution.py:25

commit v7 on v6

--- a/solution.py
+++ b/solution.py
@@ -94,21 +94,34 @@
         stacked = jnp.concatenate(
             [jnp.concatenate([pair[k].astype(BF16) for pair in pairs], 1) for k in range(2)], 0
         )
-        prod = jnp.dot(matrix, stacked, preferred_element_type=F32)
+        prod = jnp.concatenate(
+            [
+                jnp.concatenate(
+                    [
+                        jnp.dot(rows, stacked[:, at : at + win], preferred_element_type=F32)
+                        for rows in (matrix[:win], matrix[win:])
+                    ],
+                    0,
+                )
+                for at in range(0, modes * win, win)
+            ],
+            1,
+        )
         return [
             (prod[:win, m * win : (m + 1) * win], prod[win:, m * win : (m + 1) * win])
             for m in range(modes)
         ]
 
     def from_right(pairs, matrix):
-        stacked = jnp.concatenate(
-            [jnp.concatenate([pair[k].astype(BF16) for k in range(2)], 1) for pair in pairs], 0
-        )
-        prod = jnp.dot(stacked, matrix, preferred_element_type=F32)
-        return [
-            (prod[m * win : (m + 1) * win, :win], prod[m * win : (m + 1) * win, win:])
-            for m in range(modes)
+        prods = [
+            jnp.dot(
+                jnp.concatenate([pair[k].astype(BF16) for k in range(2)], 1),
+                matrix,
+                preferred_element_type=F32,
+            )
+            for pair in pairs
         ]
+        return [(prod[:, :win], prod[:, win:]) for prod in prods]
 
     def transform(pairs):
         return from_right(from_left(left_ref[...], pairs), right_ref[...])

time: 53.2 us -> 52.2 us (0.981)
  Pallas kernels: 15.1 us -> 14.1 us
    pallas_call x1, Pallas kernels: 11.3 us -> 10.3 us  [local(): pl.pallas_call(functools.partial(window_kernel, chips, modes, win, swaps)...]
where the time goes in v7:
time: 52.2 us; the launch traced here: 52 us
  starting transfers between devices  18.3 us (35%)
  Pallas kernels  14.1 us (27%)
  waiting for transfers between devices  13.1 us (25%)
  other arithmetic  2.96 us (6%)
  local copies, waits for them, and re-layouts  2.81 us (5%)
  between operations  0.8 us (2%)
    pallas_call x1, Pallas kernels, local(): pl.pallas_call(functools.partial(window_kernel, chips, modes, win, swaps)...  10.3 us
    ppermute x6, starting transfers between devices, crossed(): lax.ppermute(block, 'cuts', [(i, i ^ CORES * distance) for i in range(siz...  8.9 us
    ppermute x3, starting transfers between devices, passed_round(): lax.ppermute(block, axis, [(i, (i + distance) % size) for i in range(size)])  8.83 us
    ppermute x6, waiting for transfers between devices, crossed(): lax.ppermute(block, 'cuts', [(i, i ^ CORES * distance) for i in range(siz...  6.7 us
    ppermute x3, waiting for transfers between devices, passed_round(): lax.ppermute(block, axis, [(i, (i + distance) % size) for i in range(size)])  5.48 us
    pallas_call x2, Pallas kernels, placed(): pl.pallas_call(functools.partial(place_kernel, chips, slots, win, groups,...  2.35 us
    unnamed x14, local copies, waits for them, and re-layouts  1.55 us
    another operation x1, other arithmetic, local(): place = jnp.stack([row_offsets[slot], col_offsets[slot]])  1.32 us
  transfers between devices with their start and end apart: 13, of which 9 were waited for; matrix products, arithmetic and copies ran while one was open for 6% of the time, Pallas kernels for 3%

profile of v7, /device:TPU:0, one launch (start us, length us, event | category | flops | bytes accessed | tf_op | source)
XLA Modules:
  0.0 52.0 jit_solution(7230724540270091782)
XLA Ops:
  0.0 1.3 %convert_bitcast_fusion.own_ref = bf16[2,768,128]{2,1,0:T(8,128)(2,1)S(1)} fusion(f32[1,2,768,128]{3,2,1,0:T(8,128)} %param.9), kind=kLoop, calls=%fused_computation | loop fusion | flops 196608 | bytes 1179648 | tf_op jit(solution)/shard_map/convert_element_type | solution.py:236
  1.3 3.9 %collective-permute-start = (bf16[2,768,128]{2,1,0:T(8,128)(2,1)S(1)}, bf16[2,768,128]{2,1,0:T(8,128)(2,1)S(1)}, u32[]{:S(2)}, u32[]{:S(2)}) collective-permute-start(bf16[2,768,128]{2,1,0:T(8,128)(2,1)S(1)} %convert_bitcast_fusion.own_ref), channel_id=1, source_target_pairs={{0,3},{1,0},{2,1},{3,2},{4,7},{5,4},{6,5},{7,6},{8,11},{9,8},{10,9... | collective-permute-start | bytes 1179656 | tf_op jit(solution)/shard_map/ppermute | solution.py:25
  5.2 0.7 %copy-done.4 = s32[4]{0:T(128)S(1)} copy-done((s32[4]{0:T(128)S(1)}, s32[4]{0:T(128)}, u32[]{:S(2)}) %copy-start.4) | copy-done | bytes 40
  6.5 0.6 %dynamic_slice.10 = s32[1]{0:T(128)} dynamic-slice(s32[4]{0:T(128)S(1)} %copy-done.5, s32[]{:T(128)S(6)} %select_n.41), dynamic_slice_sizes={1} | dynamic-slice | bytes 12 | tf_op jit(solution)/shard_map/dynamic_slice | solution.py:242
  7.2 1.3 %pad_add_fusion.1.place_ref = s32[2]{0:T(128)S(1)} fusion(s32[1]{0:T(128)} %dynamic_slice.11, s32[1]{0:T(128)} %dynamic_slice.10), kind=kLoop, calls=%fused_computation.28 | loop fusion | flops 2 | bytes 16 | tf_op jit(solution)/shard_map/stack | solution.py:242
  9.3 0.7 %shard_map.91.refs_4_ = bf16[4,2,128,128]{3,2,1,0:T(8,128)(2,1)S(1)} custom-call(s32[2]{0:T(128)S(1)} %pad_add_fusion.1.place_ref, f32[4,2,128,128]{3,2,1,0:T(8,128)S(1)} %copy-done.1), custom_call_target="tpu_custom_call" | custom-call | tf_op jit(solution)/shard_map/pallas_call | solution.py:243
  10.1 0.8 %copy-done.6 = f32[128,128]{1,0:T(8,128)S(1)} copy-done((f32[128,128]{1,0:T(8,128)S(1)}, f32[128,128]{1,0:T(8,128)}, u32[]{:S(2)}) %copy-start.6) | copy-done | bytes 65560
  11.1 2.5 %collective-permute-done.beside_ref = bf16[2,768,128]{2,1,0:T(8,128)(2,1)S(1)} collective-permute-done((bf16[2,768,128]{2,1,0:T(8,128)(2,1)S(1)}, bf16[2,768,128]{2,1,0:T(8,128)(2,1)S(1)}, u32[]{:S(2)}, u32[]{:S(2)}) %collective-permute-start) | collective-permute-done | bytes 393248 | tf_op jit(solution)/shard_map/ppermute | solution.py:25
  13.6 0.7 %shard_map.92 = (bf16[2,128,128]{2,1,0:T(8,128)(2,1)S(1)}, bf16[2,128,128]{2,1,0:T(8,128)(2,1)S(1)}, bf16[2,128,128]{2,1,0:T(8,128)(2,1)S(1)}, bf16[2,128,128]{2,1,0:T(8,128)(2,1)S(1)}) custom-call(s32[3]{0:T(128)S(1)} %pad_add_fusion.ints_ref.refs_0_, s32[4]{0:T(128)S(1)} %copy-done.5, s32[4]{0:T(128)S(1)} %copy-done.4, ...), custom_call_target="tpu_custom_call" | custom-call | tf_op jit(solution)/shard_map/pallas_call | solution.py:264
  14.3 3.7 %collective-permute-start.1 = (bf16[2,128,128]{2,1,0:T(8,128)(2,1)S(1)}, bf16[2,128,128]{2,1,0:T(8,128)(2,1)S(1)}, u32[]{:S(2)}, u32[]{:S(2)}) collective-permute-start(bf16[2,128,128]{2,1,0:T(8,128)(2,1)S(1)} %get-tuple-element.26), channel_id=1, source_target_pairs={{0,24},{4,28},{8,16},{12,20},{16,8},{20,12},{24,0},{28,4},{1,25},{... | collective-permute-start | bytes 196616 | tf_op jit(solution)/shard_map/ppermute | solution.py:30
  18.0 0.7 %collective-permute-start.3 = (bf16[2,128,128]{2,1,0:T(8,128)(2,1)S(1)}, bf16[2,128,128]{2,1,0:T(8,128)(2,1)S(1)}, u32[]{:S(2)}, u32[]{:S(2)}) collective-permute-start(bf16[2,128,128]{2,1,0:T(8,128)(2,1)S(1)} %get-tuple-element.28), channel_id=1, source_target_pairs={{0,8},{4,12},{8,0},{12,4},{16,24},{20,28},{24,16},{28,20},{1,9},{5... | collective-permute-start | bytes 196616 | tf_op jit(solution)/shard_map/ppermute | solution.py:30
  18.8 1.9 %collective-permute-done.1.refs_8_ = bf16[2,128,128]{2,1,0:T(8,128)(2,1)S(1)} collective-permute-done((bf16[2,128,128]{2,1,0:T(8,128)(2,1)S(1)}, bf16[2,128,128]{2,1,0:T(8,128)(2,1)S(1)}, u32[]{:S(2)}, u32[]{:S(2)}) %collective-permute-start.1) | collective-permute-done | bytes 65568 | tf_op jit(solution)/shard_map/ppermute | solution.py:30
  20.7 2.7 %collective-permute-done.2.refs_9_ = bf16[2,128,128]{2,1,0:T(8,128)(2,1)S(1)} collective-permute-done((bf16[2,128,128]{2,1,0:T(8,128)(2,1)S(1)}, bf16[2,128,128]{2,1,0:T(8,128)(2,1)S(1)}, u32[]{:S(2)}, u32[]{:S(2)}) %collective-permute-start.2) | collective-permute-done | bytes 65568 | tf_op jit(solution)/shard_map/ppermute | solution.py:30
  23.9 0.7 %collective-permute-done.5.refs_13_ = bf16[2,128,128]{2,1,0:T(8,128)(2,1)S(1)} collective-permute-done((bf16[2,128,128]{2,1,0:T(8,128)(2,1)S(1)}, bf16[2,128,128]{2,1,0:T(8,128)(2,1)S(1)}, u32[]{:S(2)}, u32[]{:S(2)}) %collective-permute-start.5) | collective-permute-done | bytes 65568 | tf_op jit(solution)/shard_map/ppermute | solution.py:35
  24.8 10.3 %shard_map.93 = (bf16[2,128,128]{2,1,0:T(8,128)(2,1)S(1)}, bf16[2,128,128]{2,1,0:T(8,128)(2,1)S(1)}, bf16[2,128,128]{2,1,0:T(8,128)(2,1)S(1)}, bf16[2,128,128]{2,1,0:T(8,128)(2,1)S(1)}) custom-call(s32[3]{0:T(128)S(1)} %pad_add_fusion.ints_ref.refs_0_, f32[1]{0:T(128)S(6)} %convert_element_type.17.refs_1_, bf16[256,256]{1,0:T(8,128)(2,1)S(1)} %copy-done.3, ...), custom_call_target="tpu_custom_call" | custom-call | tf_op jit(solution)/shard_map/pallas_call | solution.py:277
  35.5 2.5 %collective-permute-start.10 = (bf16[2,128,128]{2,1,0:T(8,128)(2,1)S(1)}, bf16[2,128,128]{2,1,0:T(8,128)(2,1)S(1)}, u32[]{:S(2)}, u32[]{:S(2)}) collective-permute-start(bf16[2,128,128]{2,1,0:T(8,128)(2,1)S(1)} %get-tuple-element.33), channel_id=1, source_target_pairs={{0,16},{4,20},{8,24},{12,28},{16,0},{20,4},{24,8},{28,12},{1,17},{... | collective-permute-start | bytes 196616 | tf_op jit(solution)/shard_map/ppermute | solution.py:30
  38.0 1.6 %collective-permute-start.11 = (bf16[2,128,128]{2,1,0:T(8,128)(2,1)S(1)}, bf16[2,128,128]{2,1,0:T(8,128)(2,1)S(1)}, u32[]{:S(2)}, u32[]{:S(2)}) collective-permute-start(bf16[2,128,128]{2,1,0:T(8,128)(2,1)S(1)} %get-tuple-element.34), channel_id=1, source_target_pairs={{0,24},{4,28},{8,16},{12,20},{16,8},{20,12},{24,0},{28,4},{1,25},{... | collective-permute-start | bytes 196616 | tf_op jit(solution)/shard_map/ppermute | solution.py:30
  39.6 1.0 %collective-permute-done.8.refs_4_ = bf16[2,128,128]{2,1,0:T(8,128)(2,1)S(1)} collective-permute-done((bf16[2,128,128]{2,1,0:T(8,128)(2,1)S(1)}, bf16[2,128,128]{2,1,0:T(8,128)(2,1)S(1)}, u32[]{:S(2)}, u32[]{:S(2)}) %collective-permute-start.8) | collective-permute-done | bytes 65568 | tf_op jit(solution)/shard_map/ppermute | solution.py:30
  40.6 2.4 %collective-permute-start.9 = (bf16[528,128]{1,0:T(8,128)(2,1)S(1)}, bf16[528,128]{1,0:T(8,128)(2,1)S(1)}, u32[]{:S(2)}, u32[]{:S(2)}) collective-permute-start(bf16[528,128]{1,0:T(8,128)(2,1)S(1)} %pad_maximum_fusion), channel_id=1, source_target_pairs={{0,1},{1,2},{2,3},{3,0},{4,5},{5,6},{6,7},{7,4},{8,9},{9,10},{10,1... | collective-permute-start | bytes 405512 | tf_op jit(solution)/shard_map/ppermute | solution.py:25
  43.1 1.0 %collective-permute-done.11.refs_6_ = bf16[2,128,128]{2,1,0:T(8,128)(2,1)S(1)} collective-permute-done((bf16[2,128,128]{2,1,0:T(8,128)(2,1)S(1)}, bf16[2,128,128]{2,1,0:T(8,128)(2,1)S(1)}, u32[]{:S(2)}, u32[]{:S(2)}) %collective-permute-start.11) | collective-permute-done | bytes 65568 | tf_op jit(solution)/shard_map/ppermute | solution.py:30
  44.1 2.4 %collective-permute-start.12 = (bf16[4,128,128]{2,1,0:T(8,128)(2,1)S(1)}, bf16[4,128,128]{2,1,0:T(8,128)(2,1)S(1)}, u32[]{:S(2)}, u32[]{:S(2)}) collective-permute-start(bf16[4,128,128]{2,1,0:T(8,128)(2,1)S(1)} %pad_maximum_fusion.1), channel_id=1, source_target_pairs={{0,1},{1,2},{2,3},{3,0},{4,5},{5,6},{6,7},{7,4},{8,9},{9,10},{10,1... | collective-permute-start | bytes 393224 | tf_op jit(solution)/shard_map/ppermute | solution.py:25
  46.6 0.8 %shard_map.94.refs_5_ = f32[2,768,128]{2,1,0:T(8,128)S(1)} custom-call(s32[3]{0:T(128)S(1)} %pad_add_fusion.ints_ref.refs_0_, s32[4]{0:T(128)S(1)} %copy-done.5, s32[4]{0:T(128)S(1)} %copy-done.4, bf16[2,128,128]{2,1,0:T(8,128)(2,1)S(1)} %get-tuple-element.30.refs_3_, bf16[2,128,128]{2,1,0:T(8,128)(2,1)S(1)} %collective-permute-done.8.refs_4_, ...), custom_call_target="tpu_custom_call" | custom-call | tf_op jit(solution)/shard_map/pallas_call | solution.py:303
  47.5 3.0 %collective-permute-done.12.refs_4_ = bf16[4,128,128]{2,1,0:T(8,128)(2,1)S(1)} collective-permute-done((bf16[4,128,128]{2,1,0:T(8,128)(2,1)S(1)}, bf16[4,128,128]{2,1,0:T(8,128)(2,1)S(1)}, u32[]{:S(2)}, u32[]{:S(2)}) %collective-permute-start.12) | collective-permute-done | bytes 131104 | tf_op jit(solution)/shard_map/ppermute | solution.py:25
  50.5 1.5 %shard_map.95 = f32[2,768,128]{2,1,0:T(8,128)} custom-call(s32[3]{0:T(128)S(1)} %pad_add_fusion.ints_ref.refs_0_, s32[4]{0:T(128)S(1)} %get-tuple-element.38.refs_1_, s32[4]{0:T(128)S(1)} %get-tuple-element.37.refs_2_, bf16[4,128,128]{2,1,0:T(8,128)(2,1)S(1)} %bitcast.21, bf16[4,128,128]{2,1,0:T(8,128)(2,1)S(1)} %collective-permute-done.12.refs_4_, ...), custom_call_target="tpu_custom_call" | custom-call | tf_op jit(solution)/shard_map/pallas_call | solution.py:303
  (36 shorter events, 2.2 us)
Async XLA Ops:
  0.0 10.0 %copy-start = (f32[4,128,128]{2,1,0:T(8,128)S(1)}, f32[4,128,128]{2,1,0:T(8,128)}, u32[]{:S(2)}) copy-start(f32[4,128,128]{2,1,0:T(8,128)} %param.12) | copy-start | bytes 786436
  0.0 9.3 %copy-start.1 = (f32[4,2,128,128]{3,2,1,0:T(8,128)S(1)}, f32[4,2,128,128]{3,2,1,0:T(8,128)}, u32[]{:S(2)}) copy-start(f32[4,2,128,128]{3,2,1,0:T(8,128)} %probe_ref.1) | copy-start | bytes 1572868
  1.3 12.3 %collective-permute-start = (bf16[2,768,128]{2,1,0:T(8,128)(2,1)S(1)}, bf16[2,768,128]{2,1,0:T(8,128)(2,1)S(1)}, u32[]{:S(2)}, u32[]{:S(2)}) collective-permute-start(bf16[2,768,128]{2,1,0:T(8,128)(2,1)S(1)} %convert_bitcast_fusion.own_ref), channel_id=1, source_target_pairs={{0,3},{1,0},{2,1},{3,2},{4,7},{5,4},{6,5},{7,6},{8,11},{9,8},{10,9... | collective-permute-start | bytes 1179656 | tf_op jit(solution)/shard_map/ppermute | solution.py:25
  5.2 0.7 %copy-start.4 = (s32[4]{0:T(128)S(1)}, s32[4]{0:T(128)}, u32[]{:S(2)}) copy-start(s32[4]{0:T(128)} %refs_2_.2) | copy-start | bytes 52
  5.9 0.7 %copy-start.5 = (s32[4]{0:T(128)S(1)}, s32[4]{0:T(128)}, u32[]{:S(2)}) copy-start(s32[4]{0:T(128)} %refs_1_.1) | copy-start | bytes 52
  10.0 0.8 %copy-start.6 = (f32[128,128]{1,0:T(8,128)S(1)}, f32[128,128]{1,0:T(8,128)}, u32[]{:S(2)}) copy-start(f32[128,128]{1,0:T(8,128)} %param.11) | copy-start | bytes 196612
  13.6 11.2 %copy-start.2 = (bf16[256,256]{1,0:T(8,128)(2,1)S(1)}, bf16[256,256]{1,0:T(8,128)(2,1)}, u32[]{:S(2)}) copy-start(bf16[256,256]{1,0:T(8,128)(2,1)} %constant.86.clone.refs_3_) | copy-start | bytes 393220
  13.6 11.2 %copy-start.3 = (bf16[256,256]{1,0:T(8,128)(2,1)S(1)}, bf16[256,256]{1,0:T(8,128)(2,1)}, u32[]{:S(2)}) copy-start(bf16[256,256]{1,0:T(8,128)(2,1)} %constant.85.clone.refs_2_) | copy-start | bytes 393220
  14.3 6.4 %collective-permute-start.1 = (bf16[2,128,128]{2,1,0:T(8,128)(2,1)S(1)}, bf16[2,128,128]{2,1,0:T(8,128)(2,1)S(1)}, u32[]{:S(2)}, u32[]{:S(2)}) collective-permute-start(bf16[2,128,128]{2,1,0:T(8,128)(2,1)S(1)} %get-tuple-element.26), channel_id=1, source_target_pairs={{0,24},{4,28},{8,16},{12,20},{16,8},{20,12},{24,0},{28,4},{1,25},{... | collective-permute-start | bytes 196616 | tf_op jit(solution)/shard_map/ppermute | solution.py:30
  18.0 5.4 %collective-permute-start.2 = (bf16[2,128,128]{2,1,0:T(8,128)(2,1)S(1)}, bf16[2,128,128]{2,1,0:T(8,128)(2,1)S(1)}, u32[]{:S(2)}, u32[]{:S(2)}) collective-permute-start(bf16[2,128,128]{2,1,0:T(8,128)(2,1)S(1)} %get-tuple-element.27), channel_id=1, source_target_pairs={{0,16},{4,20},{8,24},{12,28},{16,0},{20,4},{24,8},{28,12},{1,17},{... | collective-permute-start | bytes 196616 | tf_op jit(solution)/shard_map/ppermute | solution.py:30
  18.0 5.4 %collective-permute-start.3 = (bf16[2,128,128]{2,1,0:T(8,128)(2,1)S(1)}, bf16[2,128,128]{2,1,0:T(8,128)(2,1)S(1)}, u32[]{:S(2)}, u32[]{:S(2)}) collective-permute-start(bf16[2,128,128]{2,1,0:T(8,128)(2,1)S(1)} %get-tuple-element.28), channel_id=1, source_target_pairs={{0,8},{4,12},{8,0},{12,4},{16,24},{20,28},{24,16},{28,20},{1,9},{5... | collective-permute-start | bytes 196616 | tf_op jit(solution)/shard_map/ppermute | solution.py:30
  18.8 5.1 %collective-permute-start.7 = (bf16[2,128,128]{2,1,0:T(8,128)(2,1)S(1)}, bf16[2,128,128]{2,1,0:T(8,128)(2,1)S(1)}, u32[]{:S(2)}, u32[]{:S(2)}) collective-permute-start(bf16[2,128,128]{2,1,0:T(8,128)(2,1)S(1)} %get-tuple-element.29.refs_11_), channel_id=1, source_target_pairs={{0,4},{4,0},{8,12},{12,8},{16,20},{20,16},{24,28},{28,24},{1,5},{5... | collective-permute-start | bytes 196616 | tf_op jit(solution)/shard_map/ppermute | solution.py:35
  20.7 3.2 %collective-permute-start.4 = (bf16[2,128,128]{2,1,0:T(8,128)(2,1)S(1)}, bf16[2,128,128]{2,1,0:T(8,128)(2,1)S(1)}, u32[]{:S(2)}, u32[]{:S(2)}) collective-permute-start(bf16[2,128,128]{2,1,0:T(8,128)(2,1)S(1)} %collective-permute-done.1.refs_8_), channel_id=1, source_target_pairs={{0,4},{4,0},{8,12},{12,8},{16,20},{20,16},{24,28},{28,24},{1,5},{5... | collective-permute-start | bytes 196616 | tf_op jit(solution)/shard_map/ppermute | solution.py:35
  23.4 1.3 %collective-permute-start.5 = (bf16[2,128,128]{2,1,0:T(8,128)(2,1)S(1)}, bf16[2,128,128]{2,1,0:T(8,128)(2,1)S(1)}, u32[]{:S(2)}, u32[]{:S(2)}) collective-permute-start(bf16[2,128,128]{2,1,0:T(8,128)(2,1)S(1)} %collective-permute-done.2.refs_9_), channel_id=1, source_target_pairs={{0,4},{4,0},{8,12},{12,8},{16,20},{20,16},{24,28},{28,24},{1,5},{5... | collective-permute-start | bytes 196616 | tf_op jit(solution)/shard_map/ppermute | solution.py:35
  23.4 1.4 %collective-permute-start.6 = (bf16[2,128,128]{2,1,0:T(8,128)(2,1)S(1)}, bf16[2,128,128]{2,1,0:T(8,128)(2,1)S(1)}, u32[]{:S(2)}, u32[]{:S(2)}) collective-permute-start(bf16[2,128,128]{2,1,0:T(8,128)(2,1)S(1)} %collective-permute-done.3.refs_10_), channel_id=1, source_target_pairs={{0,4},{4,0},{8,12},{12,8},{16,20},{20,16},{24,28},{28,24},{1,5},{5... | collective-permute-start | bytes 196616 | tf_op jit(solution)/shard_map/ppermute | solution.py:35
  35.1 5.5 %collective-permute-start.8 = (bf16[2,128,128]{2,1,0:T(8,128)(2,1)S(1)}, bf16[2,128,128]{2,1,0:T(8,128)(2,1)S(1)}, u32[]{:S(2)}, u32[]{:S(2)}) collective-permute-start(bf16[2,128,128]{2,1,0:T(8,128)(2,1)S(1)} %get-tuple-element.31), channel_id=1, source_target_pairs={{0,8},{4,12},{8,0},{12,4},{16,24},{20,28},{24,16},{28,20},{1,9},{5... | collective-permute-start | bytes 196616 | tf_op jit(solution)/shard_map/ppermute | solution.py:30
  35.5 7.7 %collective-permute-start.10 = (bf16[2,128,128]{2,1,0:T(8,128)(2,1)S(1)}, bf16[2,128,128]{2,1,0:T(8,128)(2,1)S(1)}, u32[]{:S(2)}, u32[]{:S(2)}) collective-permute-start(bf16[2,128,128]{2,1,0:T(8,128)(2,1)S(1)} %get-tuple-element.33), channel_id=1, source_target_pairs={{0,16},{4,20},{8,24},{12,28},{16,0},{20,4},{24,8},{28,12},{1,17},{... | collective-permute-start | bytes 196616 | tf_op jit(solution)/shard_map/ppermute | solution.py:30
  38.0 6.2 %collective-permute-start.11 = (bf16[2,128,128]{2,1,0:T(8,128)(2,1)S(1)}, bf16[2,128,128]{2,1,0:T(8,128)(2,1)S(1)}, u32[]{:S(2)}, u32[]{:S(2)}) collective-permute-start(bf16[2,128,128]{2,1,0:T(8,128)(2,1)S(1)} %get-tuple-element.34), channel_id=1, source_target_pairs={{0,24},{4,28},{8,16},{12,20},{16,8},{20,12},{24,0},{28,4},{1,25},{... | collective-permute-start | bytes 196616 | tf_op jit(solution)/shard_map/ppermute | solution.py:30
  40.6 6.8 %collective-permute-start.9 = (bf16[528,128]{1,0:T(8,128)(2,1)S(1)}, bf16[528,128]{1,0:T(8,128)(2,1)S(1)}, u32[]{:S(2)}, u32[]{:S(2)}) collective-permute-start(bf16[528,128]{1,0:T(8,128)(2,1)S(1)} %pad_maximum_fusion), channel_id=1, source_target_pairs={{0,1},{1,2},{2,3},{3,0},{4,5},{5,6},{6,7},{7,4},{8,9},{9,10},{10,1... | collective-permute-start | bytes 405512 | tf_op jit(solution)/shard_map/ppermute | solution.py:25
  44.1 6.3 %collective-permute-start.12 = (bf16[4,128,128]{2,1,0:T(8,128)(2,1)S(1)}, bf16[4,128,128]{2,1,0:T(8,128)(2,1)S(1)}, u32[]{:S(2)}, u32[]{:S(2)}) collective-permute-start(bf16[4,128,128]{2,1,0:T(8,128)(2,1)S(1)} %pad_maximum_fusion.1), channel_id=1, source_target_pairs={{0,1},{1,2},{2,3},{3,0},{4,5},{5,6},{6,7},{7,4},{8,9},{9,10},{10,1... | collective-permute-start | bytes 393224 | tf_op jit(solution)/shard_map/ppermute | solution.py:25

commit v8 on v7

--- a/solution.py
+++ b/solution.py
@@ -91,26 +91,16 @@
             patch_ref[CORES * (chip ^ p) + 1 - core] = other_ref[2 * place : 2 * place + 2]
 
     def from_left(matrix, pairs):
-        stacked = jnp.concatenate(
-            [jnp.concatenate([pair[k].astype(BF16) for pair in pairs], 1) for k in range(2)], 0
-        )
-        prod = jnp.concatenate(
-            [
-                jnp.concatenate(
-                    [
-                        jnp.dot(rows, stacked[:, at : at + win], preferred_element_type=F32)
-                        for rows in (matrix[:win], matrix[win:])
-                    ],
-                    0,
+        prods = []
+        for pair in pairs:
+            stacked = jnp.concatenate([pair[k].astype(BF16) for k in range(2)], 0)
+            prods.append(
+                tuple(
+                    jnp.dot(rows, stacked, preferred_element_type=F32)
+                    for rows in (matrix[:win], matrix[win:])
                 )
-                for at in range(0, modes * win, win)
-            ],
-            1,
-        )
-        return [
-            (prod[:win, m * win : (m + 1) * win], prod[win:, m * win : (m + 1) * win])
-            for m in range(modes)
-        ]
+            )
+        return prods
 
     def from_right(pairs, matrix):
         prods = [
@@ -150,9 +140,9 @@
 
     def forward_step(s, carry):
         patch = patch_at(s)
-        freq = transform([mul(wave, patch) for wave in waves_at(s)])
+        freq = transform(mul(wave, patch) for wave in waves_at(s))
         spread = propagator()
-        waves = inverse([mul(spread, pair) for pair in freq])
+        waves = inverse(mul(spread, pair) for pair in freq)
         for m in range(modes):
             for part in range(2):
                 wave_ref[s + 1, m, part] = waves[m][part]
@@ -160,10 +150,10 @@
 
     lax.fori_loop(0, slices - 1, forward_step, 0, unroll=True)
     patch = patch_at(slices - 1)
-    exits = transform([mul(wave, patch) for wave in waves_at(slices - 1)])
+    exits = transform(mul(wave, patch) for wave in waves_at(slices - 1))
     power = sum(pair[0] * pair[0] + pair[1] * pair[1] for pair in exits) * (unit * unit)
     factor = (power - target_ref[...]) * (weight_ref[0] * (0.25 * unit * unit))
-    back = inverse([(factor * pair[0], factor * pair[1]) for pair in exits])
+    back = inverse((factor * pair[0], factor * pair[1]) for pair in exits)
 
     def keep_grad(s, back):
         grads = [conj_mul(wave, pair) for wave, pair in zip(waves_at(s), back)]
@@ -175,9 +165,9 @@
     def backward_step(i, back):
         s = slices - 1 - i
         patch = patch_at(s)
-        freq = transform([conj_mul(patch, pair) for pair in back])
+        freq = transform(conj_mul(patch, pair) for pair in back)
         spread = propagator()
-        back = inverse([conj_mul(spread, pair) for pair in freq])
+        back = inverse(conj_mul(spread, pair) for pair in freq)
         keep_grad(s - 1, back)
         return back
 

time: 52.2 us -> 52.2 us (level)
  no operation moved by 1% of the time
where the time goes in v8:
time: 52.2 us; the launch traced here: 52 us
  starting transfers between devices  18.3 us (35%)
  Pallas kernels  14.1 us (27%)
  waiting for transfers between devices  13.1 us (25%)
  other arithmetic  2.96 us (6%)
  local copies, waits for them, and re-layouts  2.81 us (5%)
  between operations  0.8 us (2%)
    pallas_call x1, Pallas kernels, local(): pl.pallas_call(functools.partial(window_kernel, chips, modes, win, swaps)...  10.3 us
    ppermute x6, starting transfers between devices, crossed(): lax.ppermute(block, 'cuts', [(i, i ^ CORES * distance) for i in range(siz...  8.9 us
    ppermute x3, starting transfers between devices, passed_round(): lax.ppermute(block, axis, [(i, (i + distance) % size) for i in range(size)])  8.83 us
    ppermute x6, waiting for transfers between devices, crossed(): lax.ppermute(block, 'cuts', [(i, i ^ CORES * distance) for i in range(siz...  6.7 us
    ppermute x3, waiting for transfers between devices, passed_round(): lax.ppermute(block, axis, [(i, (i + distance) % size) for i in range(size)])  5.48 us
    pallas_call x2, Pallas kernels, placed(): pl.pallas_call(functools.partial(place_kernel, chips, slots, win, groups,...  2.35 us
    unnamed x14, local copies, waits for them, and re-layouts  1.55 us
    another operation x1, other arithmetic, local(): place = jnp.stack([row_offsets[slot], col_offsets[slot]])  1.32 us
  transfers between devices with their start and end apart: 13, of which 9 were waited for; matrix products, arithmetic and copies ran while one was open for 6% of the time, Pallas kernels for 3%

profile of v8, /device:TPU:0, one launch (start us, length us, event | category | flops | bytes accessed | tf_op | source)
XLA Modules:
  0.0 52.0 jit_solution(7230724540270091782)
XLA Ops:
  0.0 1.3 %convert_bitcast_fusion.own_ref = bf16[2,768,128]{2,1,0:T(8,128)(2,1)S(1)} fusion(f32[1,2,768,128]{3,2,1,0:T(8,128)} %param.9), kind=kLoop, calls=%fused_computation | loop fusion | flops 196608 | bytes 1179648 | tf_op jit(solution)/shard_map/convert_element_type | solution.py:226
  1.3 3.9 %collective-permute-start = (bf16[2,768,128]{2,1,0:T(8,128)(2,1)S(1)}, bf16[2,768,128]{2,1,0:T(8,128)(2,1)S(1)}, u32[]{:S(2)}, u32[]{:S(2)}) collective-permute-start(bf16[2,768,128]{2,1,0:T(8,128)(2,1)S(1)} %convert_bitcast_fusion.own_ref), channel_id=1, source_target_pairs={{0,3},{1,0},{2,1},{3,2},{4,7},{5,4},{6,5},{7,6},{8,11},{9,8},{10,9... | collective-permute-start | bytes 1179656 | tf_op jit(solution)/shard_map/ppermute | solution.py:25
  5.2 0.7 %copy-done.4 = s32[4]{0:T(128)S(1)} copy-done((s32[4]{0:T(128)S(1)}, s32[4]{0:T(128)}, u32[]{:S(2)}) %copy-start.4) | copy-done | bytes 40
  6.5 0.6 %dynamic_slice.10 = s32[1]{0:T(128)} dynamic-slice(s32[4]{0:T(128)S(1)} %copy-done.5, s32[]{:T(128)S(6)} %select_n.41), dynamic_slice_sizes={1} | dynamic-slice | bytes 12 | tf_op jit(solution)/shard_map/dynamic_slice | solution.py:232
  7.2 1.3 %pad_add_fusion.1.place_ref = s32[2]{0:T(128)S(1)} fusion(s32[1]{0:T(128)} %dynamic_slice.11, s32[1]{0:T(128)} %dynamic_slice.10), kind=kLoop, calls=%fused_computation.28 | loop fusion | flops 2 | bytes 16 | tf_op jit(solution)/shard_map/stack | solution.py:232
  9.3 0.7 %shard_map.91.refs_4_ = bf16[4,2,128,128]{3,2,1,0:T(8,128)(2,1)S(1)} custom-call(s32[2]{0:T(128)S(1)} %pad_add_fusion.1.place_ref, f32[4,2,128,128]{3,2,1,0:T(8,128)S(1)} %copy-done.1), custom_call_target="tpu_custom_call" | custom-call | tf_op jit(solution)/shard_map/pallas_call | solution.py:233
  10.1 0.8 %copy-done.6 = f32[128,128]{1,0:T(8,128)S(1)} copy-done((f32[128,128]{1,0:T(8,128)S(1)}, f32[128,128]{1,0:T(8,128)}, u32[]{:S(2)}) %copy-start.6) | copy-done | bytes 65560
  11.1 2.5 %collective-permute-done.beside_ref = bf16[2,768,128]{2,1,0:T(8,128)(2,1)S(1)} collective-permute-done((bf16[2,768,128]{2,1,0:T(8,128)(2,1)S(1)}, bf16[2,768,128]{2,1,0:T(8,128)(2,1)S(1)}, u32[]{:S(2)}, u32[]{:S(2)}) %collective-permute-start) | collective-permute-done | bytes 393248 | tf_op jit(solution)/shard_map/ppermute | solution.py:25
  13.6 0.7 %shard_map.92 = (bf16[2,128,128]{2,1,0:T(8,128)(2,1)S(1)}, bf16[2,128,128]{2,1,0:T(8,128)(2,1)S(1)}, bf16[2,128,128]{2,1,0:T(8,128)(2,1)S(1)}, bf16[2,128,128]{2,1,0:T(8,128)(2,1)S(1)}) custom-call(s32[3]{0:T(128)S(1)} %pad_add_fusion.ints_ref.refs_0_, s32[4]{0:T(128)S(1)} %copy-done.5, s32[4]{0:T(128)S(1)} %copy-done.4, ...), custom_call_target="tpu_custom_call" | custom-call | tf_op jit(solution)/shard_map/pallas_call | solution.py:254
  14.3 3.7 %collective-permute-start.1 = (bf16[2,128,128]{2,1,0:T(8,128)(2,1)S(1)}, bf16[2,128,128]{2,1,0:T(8,128)(2,1)S(1)}, u32[]{:S(2)}, u32[]{:S(2)}) collective-permute-start(bf16[2,128,128]{2,1,0:T(8,128)(2,1)S(1)} %get-tuple-element.26), channel_id=1, source_target_pairs={{0,24},{4,28},{8,16},{12,20},{16,8},{20,12},{24,0},{28,4},{1,25},{... | collective-permute-start | bytes 196616 | tf_op jit(solution)/shard_map/ppermute | solution.py:30
  18.0 0.7 %collective-permute-start.3 = (bf16[2,128,128]{2,1,0:T(8,128)(2,1)S(1)}, bf16[2,128,128]{2,1,0:T(8,128)(2,1)S(1)}, u32[]{:S(2)}, u32[]{:S(2)}) collective-permute-start(bf16[2,128,128]{2,1,0:T(8,128)(2,1)S(1)} %get-tuple-element.28), channel_id=1, source_target_pairs={{0,8},{4,12},{8,0},{12,4},{16,24},{20,28},{24,16},{28,20},{1,9},{5... | collective-permute-start | bytes 196616 | tf_op jit(solution)/shard_map/ppermute | solution.py:30
  18.8 1.9 %collective-permute-done.1.refs_8_ = bf16[2,128,128]{2,1,0:T(8,128)(2,1)S(1)} collective-permute-done((bf16[2,128,128]{2,1,0:T(8,128)(2,1)S(1)}, bf16[2,128,128]{2,1,0:T(8,128)(2,1)S(1)}, u32[]{:S(2)}, u32[]{:S(2)}) %collective-permute-start.1) | collective-permute-done | bytes 65568 | tf_op jit(solution)/shard_map/ppermute | solution.py:30
  20.7 2.7 %collective-permute-done.2.refs_9_ = bf16[2,128,128]{2,1,0:T(8,128)(2,1)S(1)} collective-permute-done((bf16[2,128,128]{2,1,0:T(8,128)(2,1)S(1)}, bf16[2,128,128]{2,1,0:T(8,128)(2,1)S(1)}, u32[]{:S(2)}, u32[]{:S(2)}) %collective-permute-start.2) | collective-permute-done | bytes 65568 | tf_op jit(solution)/shard_map/ppermute | solution.py:30
  23.9 0.7 %collective-permute-done.5.refs_13_ = bf16[2,128,128]{2,1,0:T(8,128)(2,1)S(1)} collective-permute-done((bf16[2,128,128]{2,1,0:T(8,128)(2,1)S(1)}, bf16[2,128,128]{2,1,0:T(8,128)(2,1)S(1)}, u32[]{:S(2)}, u32[]{:S(2)}) %collective-permute-start.5) | collective-permute-done | bytes 65568 | tf_op jit(solution)/shard_map/ppermute | solution.py:35
  24.8 10.3 %shard_map.93 = (bf16[2,128,128]{2,1,0:T(8,128)(2,1)S(1)}, bf16[2,128,128]{2,1,0:T(8,128)(2,1)S(1)}, bf16[2,128,128]{2,1,0:T(8,128)(2,1)S(1)}, bf16[2,128,128]{2,1,0:T(8,128)(2,1)S(1)}) custom-call(s32[3]{0:T(128)S(1)} %pad_add_fusion.ints_ref.refs_0_, f32[1]{0:T(128)S(6)} %convert_element_type.17.refs_1_, bf16[256,256]{1,0:T(8,128)(2,1)S(1)} %copy-done.3, ...), custom_call_target="tpu_custom_call" | custom-call | tf_op jit(solution)/shard_map/pallas_call | solution.py:267
  35.5 2.5 %collective-permute-start.10 = (bf16[2,128,128]{2,1,0:T(8,128)(2,1)S(1)}, bf16[2,128,128]{2,1,0:T(8,128)(2,1)S(1)}, u32[]{:S(2)}, u32[]{:S(2)}) collective-permute-start(bf16[2,128,128]{2,1,0:T(8,128)(2,1)S(1)} %get-tuple-element.33), channel_id=1, source_target_pairs={{0,16},{4,20},{8,24},{12,28},{16,0},{20,4},{24,8},{28,12},{1,17},{... | collective-permute-start | bytes 196616 | tf_op jit(solution)/shard_map/ppermute | solution.py:30
  38.0 1.6 %collective-permute-start.11 = (bf16[2,128,128]{2,1,0:T(8,128)(2,1)S(1)}, bf16[2,128,128]{2,1,0:T(8,128)(2,1)S(1)}, u32[]{:S(2)}, u32[]{:S(2)}) collective-permute-start(bf16[2,128,128]{2,1,0:T(8,128)(2,1)S(1)} %get-tuple-element.34), channel_id=1, source_target_pairs={{0,24},{4,28},{8,16},{12,20},{16,8},{20,12},{24,0},{28,4},{1,25},{... | collective-permute-start | bytes 196616 | tf_op jit(solution)/shard_map/ppermute | solution.py:30
  39.6 1.0 %collective-permute-done.8.refs_4_ = bf16[2,128,128]{2,1,0:T(8,128)(2,1)S(1)} collective-permute-done((bf16[2,128,128]{2,1,0:T(8,128)(2,1)S(1)}, bf16[2,128,128]{2,1,0:T(8,128)(2,1)S(1)}, u32[]{:S(2)}, u32[]{:S(2)}) %collective-permute-start.8) | collective-permute-done | bytes 65568 | tf_op jit(solution)/shard_map/ppermute | solution.py:30
  40.6 2.4 %collective-permute-start.9 = (bf16[528,128]{1,0:T(8,128)(2,1)S(1)}, bf16[528,128]{1,0:T(8,128)(2,1)S(1)}, u32[]{:S(2)}, u32[]{:S(2)}) collective-permute-start(bf16[528,128]{1,0:T(8,128)(2,1)S(1)} %pad_maximum_fusion), channel_id=1, source_target_pairs={{0,1},{1,2},{2,3},{3,0},{4,5},{5,6},{6,7},{7,4},{8,9},{9,10},{10,1... | collective-permute-start | bytes 405512 | tf_op jit(solution)/shard_map/ppermute | solution.py:25
  43.1 1.0 %collective-permute-done.11.refs_6_ = bf16[2,128,128]{2,1,0:T(8,128)(2,1)S(1)} collective-permute-done((bf16[2,128,128]{2,1,0:T(8,128)(2,1)S(1)}, bf16[2,128,128]{2,1,0:T(8,128)(2,1)S(1)}, u32[]{:S(2)}, u32[]{:S(2)}) %collective-permute-start.11) | collective-permute-done | bytes 65568 | tf_op jit(solution)/shard_map/ppermute | solution.py:30
  44.1 2.4 %collective-permute-start.12 = (bf16[4,128,128]{2,1,0:T(8,128)(2,1)S(1)}, bf16[4,128,128]{2,1,0:T(8,128)(2,1)S(1)}, u32[]{:S(2)}, u32[]{:S(2)}) collective-permute-start(bf16[4,128,128]{2,1,0:T(8,128)(2,1)S(1)} %pad_maximum_fusion.1), channel_id=1, source_target_pairs={{0,1},{1,2},{2,3},{3,0},{4,5},{5,6},{6,7},{7,4},{8,9},{9,10},{10,1... | collective-permute-start | bytes 393224 | tf_op jit(solution)/shard_map/ppermute | solution.py:25
  46.6 0.8 %shard_map.94.refs_5_ = f32[2,768,128]{2,1,0:T(8,128)S(1)} custom-call(s32[3]{0:T(128)S(1)} %pad_add_fusion.ints_ref.refs_0_, s32[4]{0:T(128)S(1)} %copy-done.5, s32[4]{0:T(128)S(1)} %copy-done.4, bf16[2,128,128]{2,1,0:T(8,128)(2,1)S(1)} %get-tuple-element.30.refs_3_, bf16[2,128,128]{2,1,0:T(8,128)(2,1)S(1)} %collective-permute-done.8.refs_4_, ...), custom_call_target="tpu_custom_call" | custom-call | tf_op jit(solution)/shard_map/pallas_call | solution.py:293
  47.5 3.0 %collective-permute-done.12.refs_4_ = bf16[4,128,128]{2,1,0:T(8,128)(2,1)S(1)} collective-permute-done((bf16[4,128,128]{2,1,0:T(8,128)(2,1)S(1)}, bf16[4,128,128]{2,1,0:T(8,128)(2,1)S(1)}, u32[]{:S(2)}, u32[]{:S(2)}) %collective-permute-start.12) | collective-permute-done | bytes 131104 | tf_op jit(solution)/shard_map/ppermute | solution.py:25
  50.5 1.5 %shard_map.95 = f32[2,768,128]{2,1,0:T(8,128)} custom-call(s32[3]{0:T(128)S(1)} %pad_add_fusion.ints_ref.refs_0_, s32[4]{0:T(128)S(1)} %get-tuple-element.38.refs_1_, s32[4]{0:T(128)S(1)} %get-tuple-element.37.refs_2_, bf16[4,128,128]{2,1,0:T(8,128)(2,1)S(1)} %bitcast.21, bf16[4,128,128]{2,1,0:T(8,128)(2,1)S(1)} %collective-permute-done.12.refs_4_, ...), custom_call_target="tpu_custom_call" | custom-call | tf_op jit(solution)/shard_map/pallas_call | solution.py:293
  (36 shorter events, 2.2 us)
Async XLA Ops:
  0.0 10.0 %copy-start = (f32[4,128,128]{2,1,0:T(8,128)S(1)}, f32[4,128,128]{2,1,0:T(8,128)}, u32[]{:S(2)}) copy-start(f32[4,128,128]{2,1,0:T(8,128)} %param.12) | copy-start | bytes 786436
  0.0 9.3 %copy-start.1 = (f32[4,2,128,128]{3,2,1,0:T(8,128)S(1)}, f32[4,2,128,128]{3,2,1,0:T(8,128)}, u32[]{:S(2)}) copy-start(f32[4,2,128,128]{3,2,1,0:T(8,128)} %probe_ref.1) | copy-start | bytes 1572868
  1.3 12.3 %collective-permute-start = (bf16[2,768,128]{2,1,0:T(8,128)(2,1)S(1)}, bf16[2,768,128]{2,1,0:T(8,128)(2,1)S(1)}, u32[]{:S(2)}, u32[]{:S(2)}) collective-permute-start(bf16[2,768,128]{2,1,0:T(8,128)(2,1)S(1)} %convert_bitcast_fusion.own_ref), channel_id=1, source_target_pairs={{0,3},{1,0},{2,1},{3,2},{4,7},{5,4},{6,5},{7,6},{8,11},{9,8},{10,9... | collective-permute-start | bytes 1179656 | tf_op jit(solution)/shard_map/ppermute | solution.py:25
  5.2 0.7 %copy-start.4 = (s32[4]{0:T(128)S(1)}, s32[4]{0:T(128)}, u32[]{:S(2)}) copy-start(s32[4]{0:T(128)} %refs_2_.2) | copy-start | bytes 52
  5.9 0.7 %copy-start.5 = (s32[4]{0:T(128)S(1)}, s32[4]{0:T(128)}, u32[]{:S(2)}) copy-start(s32[4]{0:T(128)} %refs_1_.1) | copy-start | bytes 52
  10.0 0.8 %copy-start.6 = (f32[128,128]{1,0:T(8,128)S(1)}, f32[128,128]{1,0:T(8,128)}, u32[]{:S(2)}) copy-start(f32[128,128]{1,0:T(8,128)} %param.11) | copy-start | bytes 196612
  13.6 11.2 %copy-start.2 = (bf16[256,256]{1,0:T(8,128)(2,1)S(1)}, bf16[256,256]{1,0:T(8,128)(2,1)}, u32[]{:S(2)}) copy-start(bf16[256,256]{1,0:T(8,128)(2,1)} %constant.86.clone.refs_3_) | copy-start | bytes 393220
  13.6 11.2 %copy-start.3 = (bf16[256,256]{1,0:T(8,128)(2,1)S(1)}, bf16[256,256]{1,0:T(8,128)(2,1)}, u32[]{:S(2)}) copy-start(bf16[256,256]{1,0:T(8,128)(2,1)} %constant.85.clone.refs_2_) | copy-start | bytes 393220
  14.3 6.4 %collective-permute-start.1 = (bf16[2,128,128]{2,1,0:T(8,128)(2,1)S(1)}, bf16[2,128,128]{2,1,0:T(8,128)(2,1)S(1)}, u32[]{:S(2)}, u32[]{:S(2)}) collective-permute-start(bf16[2,128,128]{2,1,0:T(8,128)(2,1)S(1)} %get-tuple-element.26), channel_id=1, source_target_pairs={{0,24},{4,28},{8,16},{12,20},{16,8},{20,12},{24,0},{28,4},{1,25},{... | collective-permute-start | bytes 196616 | tf_op jit(solution)/shard_map/ppermute | solution.py:30
  18.0 5.4 %collective-permute-start.2 = (bf16[2,128,128]{2,1,0:T(8,128)(2,1)S(1)}, bf16[2,128,128]{2,1,0:T(8,128)(2,1)S(1)}, u32[]{:S(2)}, u32[]{:S(2)}) collective-permute-start(bf16[2,128,128]{2,1,0:T(8,128)(2,1)S(1)} %get-tuple-element.27), channel_id=1, source_target_pairs={{0,16},{4,20},{8,24},{12,28},{16,0},{20,4},{24,8},{28,12},{1,17},{... | collective-permute-start | bytes 196616 | tf_op jit(solution)/shard_map/ppermute | solution.py:30
  18.0 5.4 %collective-permute-start.3 = (bf16[2,128,128]{2,1,0:T(8,128)(2,1)S(1)}, bf16[2,128,128]{2,1,0:T(8,128)(2,1)S(1)}, u32[]{:S(2)}, u32[]{:S(2)}) collective-permute-start(bf16[2,128,128]{2,1,0:T(8,128)(2,1)S(1)} %get-tuple-element.28), channel_id=1, source_target_pairs={{0,8},{4,12},{8,0},{12,4},{16,24},{20,28},{24,16},{28,20},{1,9},{5... | collective-permute-start | bytes 196616 | tf_op jit(solution)/shard_map/ppermute | solution.py:30
  18.8 5.1 %collective-permute-start.7 = (bf16[2,128,128]{2,1,0:T(8,128)(2,1)S(1)}, bf16[2,128,128]{2,1,0:T(8,128)(2,1)S(1)}, u32[]{:S(2)}, u32[]{:S(2)}) collective-permute-start(bf16[2,128,128]{2,1,0:T(8,128)(2,1)S(1)} %get-tuple-element.29.refs_11_), channel_id=1, source_target_pairs={{0,4},{4,0},{8,12},{12,8},{16,20},{20,16},{24,28},{28,24},{1,5},{5... | collective-permute-start | bytes 196616 | tf_op jit(solution)/shard_map/ppermute | solution.py:35
  20.7 3.2 %collective-permute-start.4 = (bf16[2,128,128]{2,1,0:T(8,128)(2,1)S(1)}, bf16[2,128,128]{2,1,0:T(8,128)(2,1)S(1)}, u32[]{:S(2)}, u32[]{:S(2)}) collective-permute-start(bf16[2,128,128]{2,1,0:T(8,128)(2,1)S(1)} %collective-permute-done.1.refs_8_), channel_id=1, source_target_pairs={{0,4},{4,0},{8,12},{12,8},{16,20},{20,16},{24,28},{28,24},{1,5},{5... | collective-permute-start | bytes 196616 | tf_op jit(solution)/shard_map/ppermute | solution.py:35
  23.4 1.3 %collective-permute-start.5 = (bf16[2,128,128]{2,1,0:T(8,128)(2,1)S(1)}, bf16[2,128,128]{2,1,0:T(8,128)(2,1)S(1)}, u32[]{:S(2)}, u32[]{:S(2)}) collective-permute-start(bf16[2,128,128]{2,1,0:T(8,128)(2,1)S(1)} %collective-permute-done.2.refs_9_), channel_id=1, source_target_pairs={{0,4},{4,0},{8,12},{12,8},{16,20},{20,16},{24,28},{28,24},{1,5},{5... | collective-permute-start | bytes 196616 | tf_op jit(solution)/shard_map/ppermute | solution.py:35
  23.4 1.4 %collective-permute-start.6 = (bf16[2,128,128]{2,1,0:T(8,128)(2,1)S(1)}, bf16[2,128,128]{2,1,0:T(8,128)(2,1)S(1)}, u32[]{:S(2)}, u32[]{:S(2)}) collective-permute-start(bf16[2,128,128]{2,1,0:T(8,128)(2,1)S(1)} %collective-permute-done.3.refs_10_), channel_id=1, source_target_pairs={{0,4},{4,0},{8,12},{12,8},{16,20},{20,16},{24,28},{28,24},{1,5},{5... | collective-permute-start | bytes 196616 | tf_op jit(solution)/shard_map/ppermute | solution.py:35
  35.1 5.5 %collective-permute-start.8 = (bf16[2,128,128]{2,1,0:T(8,128)(2,1)S(1)}, bf16[2,128,128]{2,1,0:T(8,128)(2,1)S(1)}, u32[]{:S(2)}, u32[]{:S(2)}) collective-permute-start(bf16[2,128,128]{2,1,0:T(8,128)(2,1)S(1)} %get-tuple-element.31), channel_id=1, source_target_pairs={{0,8},{4,12},{8,0},{12,4},{16,24},{20,28},{24,16},{28,20},{1,9},{5... | collective-permute-start | bytes 196616 | tf_op jit(solution)/shard_map/ppermute | solution.py:30
  35.5 7.7 %collective-permute-start.10 = (bf16[2,128,128]{2,1,0:T(8,128)(2,1)S(1)}, bf16[2,128,128]{2,1,0:T(8,128)(2,1)S(1)}, u32[]{:S(2)}, u32[]{:S(2)}) collective-permute-start(bf16[2,128,128]{2,1,0:T(8,128)(2,1)S(1)} %get-tuple-element.33), channel_id=1, source_target_pairs={{0,16},{4,20},{8,24},{12,28},{16,0},{20,4},{24,8},{28,12},{1,17},{... | collective-permute-start | bytes 196616 | tf_op jit(solution)/shard_map/ppermute | solution.py:30
  38.0 6.2 %collective-permute-start.11 = (bf16[2,128,128]{2,1,0:T(8,128)(2,1)S(1)}, bf16[2,128,128]{2,1,0:T(8,128)(2,1)S(1)}, u32[]{:S(2)}, u32[]{:S(2)}) collective-permute-start(bf16[2,128,128]{2,1,0:T(8,128)(2,1)S(1)} %get-tuple-element.34), channel_id=1, source_target_pairs={{0,24},{4,28},{8,16},{12,20},{16,8},{20,12},{24,0},{28,4},{1,25},{... | collective-permute-start | bytes 196616 | tf_op jit(solution)/shard_map/ppermute | solution.py:30
  40.6 6.8 %collective-permute-start.9 = (bf16[528,128]{1,0:T(8,128)(2,1)S(1)}, bf16[528,128]{1,0:T(8,128)(2,1)S(1)}, u32[]{:S(2)}, u32[]{:S(2)}) collective-permute-start(bf16[528,128]{1,0:T(8,128)(2,1)S(1)} %pad_maximum_fusion), channel_id=1, source_target_pairs={{0,1},{1,2},{2,3},{3,0},{4,5},{5,6},{6,7},{7,4},{8,9},{9,10},{10,1... | collective-permute-start | bytes 405512 | tf_op jit(solution)/shard_map/ppermute | solution.py:25
  44.1 6.3 %collective-permute-start.12 = (bf16[4,128,128]{2,1,0:T(8,128)(2,1)S(1)}, bf16[4,128,128]{2,1,0:T(8,128)(2,1)S(1)}, u32[]{:S(2)}, u32[]{:S(2)}) collective-permute-start(bf16[4,128,128]{2,1,0:T(8,128)(2,1)S(1)} %pad_maximum_fusion.1), channel_id=1, source_target_pairs={{0,1},{1,2},{2,3},{3,0},{4,5},{5,6},{6,7},{7,4},{8,9},{9,10},{10,1... | collective-permute-start | bytes 393224 | tf_op jit(solution)/shard_map/ppermute | solution.py:25
